TPU v7x, 128 devices: a whole 4x4x4 slice. The times are simulated.
128 devices in a mesh: rep: 16 (over y, z), tp: 8 (over x, core).
Axes of the slice: x: 4, y: 4, z: 4, core: 2. Of those that a mesh axis runs over, the one named last changes fastest.
Arguments:
- grads: bfloat16 [16, 12, 768, 2048], P('rep', None, None, 'tp'), may hold values from -6 to 6
- error: float32 [16, 12, 768, 2048], P('rep', None, None, 'tp'), may hold values from -2 to 2
- query: float32 [12, 32, 2048], P(None, None, 'tp'), may hold values from -6 to 6
- momentum: float32 [9216, 2048], P(('rep', 'tp')), may hold values from -0.8 to 0.8
- master: float32 [9216, 2048], P(('rep', 'tp')), may hold values from -0.8 to 0.8
Outputs:
- new_error: float32 [16, 12, 768, 2048], P('rep', None, None, 'tp')
- new_query: float32 [12, 32, 2048], P(None, None, 'tp')
- new_momentum: float32 [9216, 2048], P(('rep', 'tp'))
- new_master: float32 [9216, 2048], P(('rep', 'tp'))
- weights: bfloat16 [12, 768, 2048], P(None, None, 'tp')
All inputs are finite; a program needn't handle non-finite values.
Results may differ from a plain program's by a relative error of at most 0.0004.
Values may be sent and summed in bfloat16 or wider, within the bound.
A program may use at most 128 MiB of HBM per device.

v0:
```python
import jax
import jax.numpy as jnp
from jax import lax
from jax.sharding import PartitionSpec as P

ROUNDS = 2
NS_STEPS = 5


NORM_EPSILON = 1e-06
MOMENTUM_DECAY = 0.9
LEARNING_RATE = 0.5


def local_gram(factor):
    return jnp.einsum("krd,ksd->krs", factor, factor, precision=lax.Precision.HIGHEST)


def orthonormal(factor, gram_of):
    gram_now = gram_of(factor)
    sum_squares = jnp.trace(gram_now, axis1=1, axis2=2)[:, None, None]
    factor_scale = lax.rsqrt(sum_squares + NORM_EPSILON)
    ortho_basis = factor * factor_scale
    gram_now = gram_now * (factor_scale * factor_scale)
    for iteration in range(NS_STEPS):
        if iteration > 0:
            gram_now = gram_of(ortho_basis)
        ortho_basis = 1.5 * ortho_basis - 0.5 * jnp.einsum(
            "krs,ksd->krd", gram_now, ortho_basis, precision=lax.Precision.HIGHEST
        )
    return ortho_basis


def local(grads, error, query, momentum, master):
    corrected = grads[0].astype(jnp.float32) + error[0]
    current = query
    replicas = lax.axis_size("rep")
    for power_pass in range(ROUNDS):
        partial_factor = jnp.einsum(
            "kdf,krf->krd", corrected, current, precision=lax.Precision.HIGHEST
        )
        summed = lax.psum(partial_factor, ("rep", "tp"))
        ortho_basis = orthonormal(summed, local_gram)
        partial_query = jnp.einsum(
            "kdf,krd->krf", corrected, ortho_basis, precision=lax.Precision.HIGHEST
        )
        current = lax.psum(partial_query, "rep") / replicas
    approx = jnp.einsum("krd,krf->kdf", ortho_basis, current, precision=lax.Precision.HIGHEST)
    new_error = (corrected - approx)[None]
    matrices, model_width, shard_cols = approx.shape
    block_rows = matrices * model_width // replicas
    approx_rows = approx.reshape(matrices * model_width, shard_cols)
    own_block = lax.dynamic_slice_in_dim(
        approx_rows, lax.axis_index("rep") * block_rows, block_rows, 0
    )
    flat_approx = lax.all_to_all(own_block, "tp", split_axis=0, concat_axis=1, tiled=True)
    new_momentum = MOMENTUM_DECAY * momentum + flat_approx
    new_master = master - LEARNING_RATE * new_momentum
    working = new_master.astype(jnp.bfloat16)
    by_columns = lax.all_to_all(working, "tp", split_axis=1, concat_axis=0, tiled=True)
    weight_rows = lax.all_gather(by_columns, "rep", axis=0, tiled=True)
    weights = weight_rows.reshape(matrices, model_width, shard_cols)
    return (new_error, current, new_momentum, new_master, weights)


def solution(mesh):
    placed = (
        P("rep", None, None, "tp"),
        P("rep", None, None, "tp"),
        P(None, None, "tp"),
        P(("rep", "tp"), None),
        P(("rep", "tp"), None),
    )
    return jax.shard_map(
        local,
        mesh=mesh,
        in_specs=placed,
        out_specs=(
            P("rep", None, None, "tp"),
            P(None, None, "tp"),
            P(("rep", "tp"), None),
            P(("rep", "tp"), None),
            P(None, None, "tp"),
        ),
        check_vma=False,
    )
```

profile of v0, /device:TPU:1, one launch (start us, length us, event | category | flops | bytes accessed | tf_op | source)
XLA Modules:
  0.0 643.5 jit_solution(3805032442626660912)
XLA Ops:
  7.2 0.0 all-reduce.5.cloned.1.call-start
  7.2 0.9 copy-done
  8.2 14.9 %fusion.9 = f32[12,32,768]{2,1,0:T(8,128)} fusion(f32[12,32,256]{2,1,0:T(8,128)S(1)} %copy-done, f32[1,12,768,256]{3,2,1,0:T(8,128)} %param.6, bf16[1,12,768,256]{3,2,1,0:T(8,128)(2,1)} %param.5), kind=kOutput, calls=%fused_computation.11 | convolution fusion | flops 910688256 | bytes 15728640 | tf_op jit(solution)/shard_map/kdf,krf->krd/dot_general | solution.py:39
  23.1 0.0 all-reduce.5.cloned.1.call-update
  23.1 0.2 all-reduce.7.cloned.1.call-start
  23.3 150.7 %all-reduce.5.cloned.1.call-done = f32[12,32,768]{2,1,0:T(8,128)} async-done(((f32[12,32,768]{2,1,0:T(8,128)}), f32[12,32,768]{2,1,0:T(8,128)}) %all-reduce.5.cloned.1.call-update) | async-done | bytes 1179664 | tf_op jit(solution)/shard_map/psum | solution.py:42
  174.1 3.0 select_reduce_fusion.1
  177.1 1.3 fusion.21
  178.4 1.2 fusion.36
  179.6 1.2 fusion.20
  180.9 1.2 fusion.37
  182.1 1.2 fusion.19
  183.3 1.2 fusion.38
  184.5 1.2 fusion.18
  185.7 1.2 fusion.39
  186.9 1.2 fusion.17
  188.1 0.4 slice-done.6
  188.6 6.7 %fusion.4 = f32[12,32,256]{2,1,0:T(8,128)} fusion(f32[12,32,768]{2,1,0:T(8,128)S(1)} %fusion.17, f32[1,12,768,256]{3,2,1,0:T(8,128)S(1)} %bitcast.73, bf16[1,12,768,256]{3,2,1,0:T(8,128)(2,1)S(1)} %bitcast.77), kind=kOutput, calls=%fused_computation.5 | convolution fusion | flops 910688256 | bytes 15728640 | tf_op jit(solution)/shard_map/kdf,krd->krf/dot_general | solution.py:44
  195.3 0.0 all-reduce.7.cloned.1.call-update
  195.3 0.0 all-reduce.9.cloned.1.call-start
  195.4 81.4 %all-reduce.7.cloned.1.call-done = f32[12,32,256]{2,1,0:T(8,128)} async-done(((f32[12,32,256]{2,1,0:T(8,128)}), f32[12,32,256]{2,1,0:T(8,128)}) %all-reduce.7.cloned.1.call-update) | async-done | bytes 393232 | tf_op jit(solution)/shard_map/psum | solution.py:47
  276.8 14.6 %fusion.2 = f32[12,32,768]{2,1,0:T(8,128)} fusion(f32[12,32,256]{2,1,0:T(8,128)} %all-reduce.7.cloned.1.call-done, f32[1,12,768,256]{3,2,1,0:T(8,128)} %param.6, bf16[1,12,768,256]{3,2,1,0:T(8,128)(2,1)} %param.5), kind=kOutput, calls=%fused_computation.3 | convolution fusion | flops 910786560 | bytes 15728640 | tf_op jit(solution)/shard_map/kdf,krf->krd/dot_general | solution.py:39
  291.3 0.0 all-reduce.9.cloned.1.call-update
  291.4 0.2 all-reduce.11.cloned.1.call-start
  291.6 148.1 %all-reduce.9.cloned.1.call-done = f32[12,32,768]{2,1,0:T(8,128)} async-done(((f32[12,32,768]{2,1,0:T(8,128)}), f32[12,32,768]{2,1,0:T(8,128)}) %all-reduce.9.cloned.1.call-update) | async-done | bytes 1179664 | tf_op jit(solution)/shard_map/psum | solution.py:42
  439.7 3.0 select_reduce_fusion
  442.7 1.3 fusion.16
  444.0 1.2 fusion.40
  445.3 1.2 fusion.15
  446.5 1.2 fusion.41
  447.7 1.2 fusion.14
  448.9 1.2 fusion.42
  450.1 1.2 fusion.13
  451.3 1.2 fusion.43
  452.5 1.2 fusion.12
  454.0 6.8 %fusion = f32[12,32,256]{2,1,0:T(8,128)} fusion(f32[12,32,768]{2,1,0:T(8,128)S(1)} %fusion.12, f32[1,12,768,256]{3,2,1,0:T(8,128)S(1)} %bitcast.75, bf16[1,12,768,256]{3,2,1,0:T(8,128)(2,1)S(1)} %bitcast.79), kind=kOutput, calls=%fused_computation.1 | convolution fusion | flops 910688256 | bytes 15728640 | tf_op jit(solution)/shard_map/kdf,krd->krf/dot_general | solution.py:44
  460.7 0.0 all-reduce.11.cloned.1.call-update
  460.8 0.0 all-gather.2.cloned.1.call-start
  460.8 81.4 %all-reduce.11.cloned.1.call-done = f32[12,32,256]{2,1,0:T(8,128)} async-done(((f32[12,32,256]{2,1,0:T(8,128)}), f32[12,32,256]{2,1,0:T(8,128)}) %all-reduce.11.cloned.1.call-update) | async-done | bytes 393232 | tf_op jit(solution)/shard_map/psum | solution.py:47
  542.2 1.0 broadcast_multiply_fusion
  543.3 7.7 %fusion.44 = f32[12,768,256]{2,1,0:T(8,128)S(1)} fusion(f32[12,32,768]{2,1,0:T(8,128)S(1)} %fusion.12, f32[12,32,256]{2,1,0:T(8,128)S(1)} %broadcast_multiply_fusion), kind=kOutput, calls=%fused_computation.64 | convolution fusion | flops 905969664 | bytes 11010048 | tf_op jit(solution)/shard_map/krd,krf->kdf/dot_general | solution.py:48
  551.1 16.7 %all_to_all.38 = f32[8,72,256]{2,1,0:T(8,128)S(1)} all-to-all(f32[8,72,256]{2,1,0:T(8,128)S(1)} %bitcast.83), channel_id=1, replica_groups=mesh['rep'=16,'tp'=8] {'tp'}, dimensions={0} | all-to-all | bytes 1179648 | tf_op jit(solution)/shard_map/all_to_all | solution.py:56
  567.9 1.2 fusion.35
  569.1 11.1 %all_to_all.39 = bf16[72,8,256]{2,0,1:T(8,128)(2,1)} all-to-all(bf16[72,8,256]{2,0,1:T(8,128)(2,1)S(1)} %bitcast.87), channel_id=1, replica_groups=mesh['rep'=16,'tp'=8] {'tp'}, dimensions={1} | all-to-all | bytes 589824 | tf_op jit(solution)/shard_map/all_to_all | solution.py:60
  580.2 0.0 all-gather.2.cloned.1.call-update
  580.3 12.7 %fusion.8 = f32[1,12,768,256]{3,2,1,0:T(8,128)} fusion(f32[12,768,256]{2,1,0:T(8,128)} %copy-done.2, f32[1,12,768,256]{3,2,1,0:T(8,128)} %param.6, bf16[1,12,768,256]{3,2,1,0:T(8,128)(2,1)} %param.5), kind=kLoop, calls=%fused_computation.9 | loop fusion | flops 7077888 | bytes 33030144 | tf_op jit(solution)/shard_map/broadcast_in_dim | solution.py:49
  592.9 38.9 %all-gather.2.cloned.1.call-done = bf16[9216,256]{1,0:T(8,128)(2,1)} async-done(((bf16[576,256]{1,0:T(8,128)(2,1)}), bf16[9216,256]{1,0:T(8,128)(2,1)}) %all-gather.2.cloned.1.call-update) | async-done | bytes 4718608 | tf_op jit(solution)/shard_map/all_gather | solution.py:61
  631.8 4.9 copy.24
  (44 shorter events, 0.3 us)
Async XLA Ops:
  7.2 1.0 copy-start
  7.2 166.9 %all-reduce.5.cloned.1.call-start = ((), (), s32[]{:S(2)}) async-start(), calls=%async_computation.2 | async-start | bytes 2359296 | tf_op jit(solution)/shard_map/psum | solution.py:42
  23.1 253.7 %all-reduce.7.cloned.1.call-start = ((), (), s32[]{:S(2)}) async-start(), calls=%async_computation.3 | async-start | bytes 786432 | tf_op jit(solution)/shard_map/psum | solution.py:47
  174.1 3.0 copy-start.3
  178.4 9.7 %slice-start = ((s8[9437184]{0:T(1024)(128)(4,1)}), s8[4194304]{0:T(1024)(128)(4,1)S(1)}, s32[]{:S(2)}) async-start(s8[9437184]{0:T(1024)(128)(4,1)} %bitcast.72), calls=%async_computation.7 | async-start | bytes 8388608
  179.6 8.9 %slice-start.6 = ((s8[4718592]{0:T(1024)(128)(4,1)}), s8[4194304]{0:T(1024)(128)(4,1)S(1)}, s32[]{:S(2)}) async-start(s8[4718592]{0:T(1024)(128)(4,1)} %bitcast.76), calls=%async_computation.13 | async-start | bytes 8388608
  180.9 7.6 %slice-start.1 = ((s8[9437184]{0:T(1024)(128)(4,1)}), s8[4194304]{0:T(1024)(128)(4,1)S(1)}, s32[]{:S(2)}) async-start(s8[9437184]{0:T(1024)(128)(4,1)} %bitcast.72), calls=%async_computation.8 | async-start | bytes 8388608
  183.3 5.3 slice-start.7
  184.5 4.0 slice-start.2
  195.3 244.4 %all-reduce.9.cloned.1.call-start = ((), (), s32[]{:S(2)}) async-start(), calls=%async_computation.4 | async-start | bytes 2359296 | tf_op jit(solution)/shard_map/psum | solution.py:42
  291.4 250.9 %all-reduce.11.cloned.1.call-start = ((), (), s32[]{:S(2)}) async-start(), calls=%async_computation.5 | async-start | bytes 786432 | tf_op jit(solution)/shard_map/psum | solution.py:47
  439.7 3.0 copy-start.4
  444.0 9.7 %slice-start.3 = ((s8[9437184]{0:T(1024)(128)(4,1)}), s8[4194304]{0:T(1024)(128)(4,1)S(1)}, s32[]{:S(2)}) async-start(s8[9437184]{0:T(1024)(128)(4,1)} %bitcast.74), calls=%async_computation.10 | async-start | bytes 8388608
  445.2 8.5 %slice-start.8 = ((s8[4718592]{0:T(1024)(128)(4,1)}), s8[4194304]{0:T(1024)(128)(4,1)S(1)}, s32[]{:S(2)}) async-start(s8[4718592]{0:T(1024)(128)(4,1)} %bitcast.78), calls=%async_computation.15 | async-start | bytes 8388608
  446.5 7.2 %slice-start.4 = ((s8[9437184]{0:T(1024)(128)(4,1)}), s8[4194304]{0:T(1024)(128)(4,1)S(1)}, s32[]{:S(2)}) async-start(s8[9437184]{0:T(1024)(128)(4,1)} %bitcast.74), calls=%async_computation.11 | async-start | bytes 8388608
  448.9 4.8 slice-start.9
  450.1 3.8 slice-start.5
  460.8 171.1 %all-gather.2.cloned.1.call-start = ((), (), s32[]{:S(2)}) async-start(), calls=%async_computation.6 | async-start | bytes 5013504 | tf_op jit(solution)/shard_map/all_gather | solution.py:61
  543.3 7.8 %copy-start.5 = (f32[12,32,256]{2,1,0:T(8,128)}, f32[12,32,256]{2,1,0:T(8,128)S(1)}, u32[]{:S(2)}) copy-start(f32[12,32,256]{2,1,0:T(8,128)S(1)} %broadcast_multiply_fusion) | copy-start | bytes 1179652
  551.0 18.1 %copy-start.2 = (f32[12,768,256]{2,1,0:T(8,128)}, f32[12,768,256]{2,1,0:T(8,128)S(1)}, u32[]{:S(2)}) copy-start(f32[12,768,256]{2,1,0:T(8,128)S(1)} %fusion.44) | copy-start | bytes 28311556
  551.1 16.8 %copy-start.6 = (f32[72,2048]{1,0:T(8,128)S(1)}, f32[72,2048]{1,0:T(8,128)}, u32[]{:S(2)}) copy-start(f32[72,2048]{1,0:T(8,128)} %param.9) | copy-start | bytes 1769476
  551.1 16.8 %copy-start.7 = (f32[72,2048]{1,0:T(8,128)S(1)}, f32[72,2048]{1,0:T(8,128)}, u32[]{:S(2)}) copy-start(f32[72,2048]{1,0:T(8,128)} %param.8) | copy-start | bytes 1769476
  631.8 4.9 copy-start.1
Sparse Core Ops, SparseCore 0:
  23.2 150.8 all-reduce.4
  195.4 81.3 all-reduce.6
  291.5 148.1 all-reduce.8
  460.9 81.3 all-reduce.10
  580.4 51.3 all-gather.1
where the time goes:
time: 649 us; the launch traced here: 643 us
  waiting for transfers between devices  501 us (77%)
  matrix products  78.5 us (12%)
  blocking collectives  27.8 us (4%)
  other arithmetic  14.9 us (2%)
  between operations  14.6 us (2%)
    psum x2, waiting for transfers between devices, local(): summed = lax.psum(partial_factor, ('rep', 'tp'))  299 us
    psum x2, waiting for transfers between devices, local(): current = lax.psum(partial_query, 'rep') / replicas  163 us
    all_gather x1, waiting for transfers between devices, local(): weight_rows = lax.all_gather(by_columns, 'rep', axis=0, tiled=True)  38.9 us
    dot_general x2, matrix products, local(): jnp.einsum('kdf,krf->krd', corrected, current, precision=lax.Precision.HI...  29.5 us
    all_to_all x1, blocking collectives, local(): lax.all_to_all(own_block, 'tp', split_axis=0, concat_axis=1, tiled=True)  16.7 us
    dot_general x10, matrix products, local_gram(): jnp.einsum('krd,ksd->krs', factor, factor, precision=lax.Precision.HIGHEST)  15.7 us
    dot_general x2, matrix products, local(): jnp.einsum('kdf,krd->krf', corrected, ortho_basis, precision=lax.Precisio...  13.5 us
  transfers between devices with their start and end apart: 5, of which 5 were waited for; matrix products, arithmetic and copies ran while one was open for 2% of the time, Pallas kernels for 0%

commit v1 on v0

--- a/solution.py
+++ b/solution.py
@@ -1,6 +1,10 @@
+import functools
+
 import jax
 import jax.numpy as jnp
 from jax import lax
+from jax.experimental import pallas as pl
+from jax.experimental.pallas import tpu as pltpu
 from jax.sharding import PartitionSpec as P
 
 ROUNDS = 2
@@ -10,6 +14,144 @@
 NORM_EPSILON = 1e-06
 MOMENTUM_DECAY = 0.9
 LEARNING_RATE = 0.5
+
+MESH_AXES = ("rep", "tp")
+LANES = 128
+
+
+def _peer(name, index):
+    return tuple(index if axis == name else lax.axis_index(axis) for axis in MESH_AXES)
+
+
+def _allreduce_kernel(levels, x_ref, o_ref, *scratch):
+    n_lev = len(levels)
+    it = iter(scratch)
+    recv = [next(it) for _ in range(n_lev)]
+    sums = [next(it) for _ in range(n_lev - 1)]
+    gath = [next(it) for _ in range(n_lev - 1)] + [None]
+    rs_send = [next(it) for _ in range(n_lev)]
+    rs_recv = [next(it) for _ in range(n_lev)]
+    ag_send = [next(it) for _ in range(n_lev)]
+    ag_recv = [next(it) for _ in range(n_lev)]
+    local_sem = next(it)
+
+    me = [lax.axis_index(name) for name, _ in levels]
+
+    barrier = pltpu.get_barrier_semaphore()
+    total_peers = 0
+    for lev, (name, n) in enumerate(levels):
+        for off in range(1, n):
+            j = lax.rem(me[lev] + off, n)
+            pl.semaphore_signal(barrier, inc=1, device_id=_peer(name, j),
+                                device_id_type=pl.DeviceIdType.MESH)
+        total_peers += n - 1
+    pl.semaphore_wait(barrier, total_peers)
+
+    gath_bufs = [o_ref] + gath[: n_lev - 1]
+
+    src = x_ref
+    for lev, (name, n) in enumerate(levels):
+        m = me[lev]
+        copies = []
+        for off in range(1, n):
+            j = lax.rem(m + off, n)
+            cp = pltpu.make_async_remote_copy(
+                src_ref=src.at[j], dst_ref=recv[lev].at[m],
+                send_sem=rs_send[lev].at[off], recv_sem=rs_recv[lev].at[m],
+                device_id=_peer(name, j), device_id_type=pl.DeviceIdType.MESH)
+            cp.start()
+            copies.append((j, off, cp))
+        own = pltpu.make_async_copy(src.at[m], recv[lev].at[m], local_sem.at[0])
+        own.start()
+        own.wait()
+        for j, off, cp in copies:
+            pltpu.make_async_remote_copy(
+                src_ref=src.at[j], dst_ref=recv[lev].at[j],
+                send_sem=rs_send[lev].at[off], recv_sem=rs_recv[lev].at[j],
+                device_id=_peer(name, j), device_id_type=pl.DeviceIdType.MESH).wait_recv()
+        for j, off, cp in copies:
+            cp.wait_send()
+        r = recv[lev]
+        if lev < n_lev - 1:
+            dst = sums[lev]
+        else:
+            dst = gath_bufs[lev].at[m]
+        if len(r.shape) > 3:
+            def body(i, carry, r=r, dst=dst, n=n):
+                acc = r[0, i]
+                for j in range(1, n):
+                    acc = acc + r[j, i]
+                dst[i] = acc
+                return carry
+            lax.fori_loop(0, r.shape[1], body, 0)
+        else:
+            acc = r[0]
+            for j in range(1, n):
+                acc = acc + r[j]
+            dst[...] = acc
+        if lev < n_lev - 1:
+            src = sums[lev]
+
+    for lev in reversed(range(n_lev)):
+        name, n = levels[lev]
+        m = me[lev]
+        buf = gath_bufs[lev]
+        if lev == n_lev - 1:
+            piece = buf.at[m]
+        else:
+            piece = gath_bufs[lev + 1]
+            own = pltpu.make_async_copy(piece, buf.at[m], local_sem.at[0])
+            own.start()
+            own.wait()
+        copies = []
+        for off in range(1, n):
+            j = lax.rem(m + off, n)
+            cp = pltpu.make_async_remote_copy(
+                src_ref=piece, dst_ref=buf.at[m],
+                send_sem=ag_send[lev].at[off], recv_sem=ag_recv[lev].at[m],
+                device_id=_peer(name, j), device_id_type=pl.DeviceIdType.MESH)
+            cp.start()
+            copies.append((j, off, cp))
+        for j, off, cp in copies:
+            pltpu.make_async_remote_copy(
+                src_ref=piece, dst_ref=buf.at[j],
+                send_sem=ag_send[lev].at[off], recv_sem=ag_recv[lev].at[j],
+                device_id=_peer(name, j), device_id_type=pl.DeviceIdType.MESH).wait_recv()
+        for j, off, cp in copies:
+            cp.wait_send()
+
+
+def allreduce(x, levels, collective_id):
+    shape = x.shape
+    total = x.size
+    counts = [n for _, n in levels]
+    per = total
+    for n in counts:
+        per //= n
+    rows = per // LANES
+    full = tuple(counts) + (rows, LANES)
+    xr = x.reshape(full)
+    scratch = []
+    for lev in range(len(levels)):
+        scratch.append(pltpu.VMEM(full[lev:], jnp.float32))
+    for lev in range(len(levels) - 1):
+        scratch.append(pltpu.VMEM(full[lev + 1:], jnp.float32))
+    for lev in range(len(levels) - 1):
+        scratch.append(pltpu.VMEM(full[lev + 1:], jnp.float32))
+    for _ in range(4):
+        for _, n in levels:
+            scratch.append(pltpu.SemaphoreType.DMA((n,)))
+    scratch.append(pltpu.SemaphoreType.DMA((1,)))
+    out = pl.pallas_call(
+        functools.partial(_allreduce_kernel, tuple(levels)),
+        out_shape=jax.ShapeDtypeStruct(full, jnp.float32),
+        in_specs=[pl.BlockSpec(memory_space=pltpu.VMEM)],
+        out_specs=pl.BlockSpec(memory_space=pltpu.VMEM),
+        scratch_shapes=scratch,
+        compiler_params=pltpu.CompilerParams(collective_id=collective_id, has_side_effects=True),
+        cost_estimate=pl.CostEstimate(flops=total * 2, bytes_accessed=total * 4 * 4, transcendentals=0),
+    )(xr)
+    return out.reshape(shape)
 
 
 def local_gram(factor):
@@ -35,16 +177,18 @@
     corrected = grads[0].astype(jnp.float32) + error[0]
     current = query
     replicas = lax.axis_size("rep")
+    both = (("tp", lax.axis_size("tp")), ("rep", replicas))
+    rep_only = (("rep", replicas),)
     for power_pass in range(ROUNDS):
         partial_factor = jnp.einsum(
             "kdf,krf->krd", corrected, current, precision=lax.Precision.HIGHEST
         )
-        summed = lax.psum(partial_factor, ("rep", "tp"))
+        summed = allreduce(partial_factor, both, 0)
         ortho_basis = orthonormal(summed, local_gram)
         partial_query = jnp.einsum(
             "kdf,krd->krf", corrected, ortho_basis, precision=lax.Precision.HIGHEST
         )
-        current = lax.psum(partial_query, "rep") / replicas
+        current = allreduce(partial_query, rep_only, 1) / replicas
     approx = jnp.einsum("krd,krf->kdf", ortho_basis, current, precision=lax.Precision.HIGHEST)
     new_error = (corrected - approx)[None]
     matrices, model_width, shard_cols = approx.shape

time: 649 us -> 321 us (0.49)
  waiting for transfers between devices: 501 us -> 39 us
  Pallas kernels: 0 us -> 135 us
  local copies, waits for them, and re-layouts: 6.46 us -> 15.5 us
  matrix products: 78.5 us -> 70.5 us
    psum x4 -> x0, waiting for transfers between devices: 462 us -> none  [the longest x2 299 us: local(): summed = lax.psum(partial_factor, ('rep', 'tp'))]
    pallas_call x0 -> x4, Pallas kernels: none -> 135 us  [allreduce(): pl.pallas_call(functools.partial(_allreduce_kernel, tuple(levels)), out_s...]
    reshape x0 -> x6, local copies, waits for them, and re-layouts: none -> 8.2 us  [the longest x4 4.38 us: allreduce(): xr = x.reshape(full)]
  transfers between devices with their start and end apart: 5 -> 1, of which waited for: 5 -> 1; matrix products, arithmetic and copies ran while one was open for 2% -> 4% of each run, Pallas kernels for 0% -> 0%
where the time goes in v1:
time: 321 us; the launch traced here: 316 us
  Pallas kernels  135 us (42%)
  matrix products  70.5 us (22%)
  waiting for transfers between devices  39 us (12%)
  blocking collectives  25.5 us (8%)
  other arithmetic  15.9 us (5%)
  local copies, waits for them, and re-layouts  15.5 us (5%)
  between operations  14.7 us (5%)
    pallas_call x4, Pallas kernels, allreduce(): pl.pallas_call(functools.partial(_allreduce_kernel, tuple(levels)), out_s...  135 us
    all_gather x1, waiting for transfers between devices, local(): weight_rows = lax.all_gather(by_columns, 'rep', axis=0, tiled=True)  39 us
    dot_general x2, matrix products, local(): jnp.einsum('kdf,krf->krd', corrected, current, precision=lax.Precision.HI...  23.8 us
    all_to_all x1, blocking collectives, local(): lax.all_to_all(own_block, 'tp', split_axis=0, concat_axis=1, tiled=True)  14.3 us
    broadcast_in_dim x1, other arithmetic, local(): new_error = (corrected - approx)[None]  12.7 us
    dot_general x10, matrix products, orthonormal(): jnp.einsum('krs,ksd->krd', gram_now, ortho_basis, precision=lax.Precision...  12.5 us
    dot_general x10, matrix products, local_gram(): jnp.einsum('krd,ksd->krs', factor, factor, precision=lax.Precision.HIGHEST)  12.2 us
    dot_general x2, matrix products, local(): jnp.einsum('kdf,krd->krf', corrected, ortho_basis, precision=lax.Precisio...  12 us
  transfers between devices with their start and end apart: 1, of which 1 were waited for; matrix products, arithmetic and copies ran while one was open for 4% of the time, Pallas kernels for 0%

profile of v1, /device:TPU:1, one launch (start us, length us, event | category | flops | bytes accessed | tf_op | source)
XLA Modules:
  0.0 315.9 jit_solution(4328408349612891012)
XLA Ops:
  7.2 0.0 all-gather.2.cloned.1.call-start
  7.2 0.9 copy-done
  8.2 12.1 %fusion.9 = f32[12,32,768]{2,1,0:T(8,128)S(1)} fusion(f32[12,32,256]{2,1,0:T(8,128)S(1)} %copy-done, f32[1,12,768,256]{3,2,1,0:T(8,128)} %param.6, bf16[1,12,768,256]{3,2,1,0:T(8,128)(2,1)} %param.5), kind=kOutput, calls=%fused_computation.11 | convolution fusion | flops 910688256 | bytes 15728640 | tf_op jit(solution)/shard_map/kdf,krf->krd/dot_general | solution.py:183
  20.3 1.4 reshape.68.x_ref
  21.7 51.3 %shard_map.92 = f32[8,16,18,128]{3,2,1,0:T(8,128)} custom-call(f32[8,16,18,128]{3,2,1,0:T(8,128)} %reshape.68.x_ref), custom_call_target="tpu_custom_call" | custom-call | flops 589824 | bytes 4718592 | tf_op jit(solution)/shard_map/pallas_call | solution.py:145
  73.0 1.8 reshape.69
  74.8 1.3 select_reduce_fusion.1
  76.2 1.3 fusion.21
  77.5 1.2 fusion.33
  78.7 1.2 fusion.20
  79.9 1.2 fusion.34
  81.1 1.2 fusion.19
  82.3 1.2 fusion.35
  83.5 1.2 fusion.18
  84.7 1.2 fusion.36
  85.9 1.4 fusion.17
  87.4 6.0 %fusion.4 = f32[12,32,256]{2,1,0:T(8,128)S(1)} fusion(f32[12,32,768]{2,1,0:T(8,128)S(1)} %fusion.17, f32[1,12,768,256]{3,2,1,0:T(8,128)S(1)} %bitcast.74, bf16[1,12,768,256]{3,2,1,0:T(8,128)(2,1)S(1)} %bitcast.78), kind=kOutput, calls=%fused_computation.5 | convolution fusion | flops 910688256 | bytes 15728640 | tf_op jit(solution)/shard_map/kdf,krd->krf/dot_general | solution.py:188
  93.4 0.8 reshape.70.x_ref
  94.2 19.0 %shard_map.93 = f32[16,48,128]{2,1,0:T(8,128)} custom-call(f32[16,48,128]{2,1,0:T(8,128)} %reshape.70.x_ref), custom_call_target="tpu_custom_call" | custom-call | flops 196608 | bytes 1572864 | tf_op jit(solution)/shard_map/pallas_call | solution.py:145
  113.2 1.0 broadcast_multiply_fusion.1
  114.2 0.1 div.11
  114.4 11.7 %fusion.2 = f32[12,32,768]{2,1,0:T(8,128)S(1)} fusion(f32[12,32,256]{2,1,0:T(8,128)S(1)} %div.11, f32[1,12,768,256]{3,2,1,0:T(8,128)} %param.6, bf16[1,12,768,256]{3,2,1,0:T(8,128)(2,1)} %param.5), kind=kOutput, calls=%fused_computation.3 | convolution fusion | flops 910688256 | bytes 15728640 | tf_op jit(solution)/shard_map/kdf,krf->krd/dot_general | solution.py:183
  126.0 1.4 reshape.71.x_ref
  127.4 46.2 %shard_map.94 = f32[8,16,18,128]{3,2,1,0:T(8,128)} custom-call(f32[8,16,18,128]{3,2,1,0:T(8,128)} %reshape.71.x_ref), custom_call_target="tpu_custom_call" | custom-call | flops 589824 | bytes 4718592 | tf_op jit(solution)/shard_map/pallas_call | solution.py:145
  173.7 2.0 reshape.72
  175.7 1.3 select_reduce_fusion
  177.0 1.3 fusion.16
  178.3 1.2 fusion.37
  179.5 1.2 fusion.15
  180.8 1.2 fusion.38
  182.0 1.2 fusion.14
  183.2 1.2 fusion.39
  184.4 1.2 fusion.13
  185.6 1.2 fusion.40
  186.8 1.4 fusion.12
  188.2 6.0 %fusion = f32[12,32,256]{2,1,0:T(8,128)S(1)} fusion(f32[12,32,768]{2,1,0:T(8,128)S(1)} %fusion.12, f32[1,12,768,256]{3,2,1,0:T(8,128)S(1)} %bitcast.76, bf16[1,12,768,256]{3,2,1,0:T(8,128)(2,1)S(1)} %bitcast.80), kind=kOutput, calls=%fused_computation.1 | convolution fusion | flops 910688256 | bytes 15728640 | tf_op jit(solution)/shard_map/kdf,krd->krf/dot_general | solution.py:188
  194.2 0.8 reshape.73.x_ref
  195.0 18.2 %shard_map.95 = f32[16,48,128]{2,1,0:T(8,128)} custom-call(f32[16,48,128]{2,1,0:T(8,128)} %reshape.73.x_ref), custom_call_target="tpu_custom_call" | custom-call | flops 196608 | bytes 1572864 | tf_op jit(solution)/shard_map/pallas_call | solution.py:145
  213.3 1.0 broadcast_multiply_fusion
  214.3 0.1 div.13
  214.4 10.0 %fusion.41 = f32[12,768,256]{2,1,0:T(8,128)} fusion(f32[12,32,768]{2,1,0:T(8,128)S(1)} %fusion.12, f32[12,32,256]{2,1,0:T(8,128)S(1)} %div.13), kind=kOutput, calls=%fused_computation.62 | convolution fusion | flops 905969664 | bytes 11010048 | tf_op jit(solution)/shard_map/krd,krf->kdf/dot_general | solution.py:192
  224.4 1.1 constant_dynamic-slice_fusion
  225.5 14.3 %all_to_all.38 = f32[8,72,256]{2,1,0:T(8,128)S(1)} all-to-all(f32[8,72,256]{2,1,0:T(8,128)S(1)} %bitcast.84), channel_id=1, replica_groups=mesh['rep'=16,'tp'=8] {'tp'}, dimensions={0} | all-to-all | bytes 1179648 | tf_op jit(solution)/shard_map/all_to_all | solution.py:200
  239.9 1.2 fusion.32
  241.1 11.1 %all_to_all.39 = bf16[72,8,256]{2,0,1:T(8,128)(2,1)} all-to-all(bf16[72,8,256]{2,0,1:T(8,128)(2,1)S(1)} %bitcast.88), channel_id=1, replica_groups=mesh['rep'=16,'tp'=8] {'tp'}, dimensions={1} | all-to-all | bytes 589824 | tf_op jit(solution)/shard_map/all_to_all | solution.py:204
  252.3 12.7 %fusion.8 = f32[1,12,768,256]{3,2,1,0:T(8,128)} fusion(f32[12,768,256]{2,1,0:T(8,128)} %fusion.41, f32[1,12,768,256]{3,2,1,0:T(8,128)} %param.6, bf16[1,12,768,256]{3,2,1,0:T(8,128)(2,1)} %param.5), kind=kLoop, calls=%fused_computation.9 | loop fusion | flops 7077888 | bytes 33030144 | tf_op jit(solution)/shard_map/broadcast_in_dim | solution.py:193
  264.9 39.0 %all-gather.2.cloned.1.call-done = bf16[9216,256]{1,0:T(8,128)(2,1)} async-done(((bf16[576,256]{1,0:T(8,128)(2,1)}), bf16[9216,256]{1,0:T(8,128)(2,1)}) %all-gather.2.cloned.1.call-update) | async-done | bytes 4718608 | tf_op jit(solution)/shard_map/all_gather | solution.py:205
  304.0 4.9 %copy.20 = bf16[12,768,256]{2,1,0:T(8,128)(2,1)} copy(bf16[12,768,256]{2,1,0:T(8,128)(2,1)} %bitcast.82) | data formatting | bytes 9437184
  (39 shorter events, 0.2 us)
Async XLA Ops:
  7.2 1.0 copy-start
  7.2 296.8 %all-gather.2.cloned.1.call-start = ((), (), s32[]{:S(2)}) async-start(), calls=%async_computation.2 | async-start | bytes 5013504 | tf_op jit(solution)/shard_map/all_gather | solution.py:205
  77.5 9.9 %slice-start = ((s8[9437184]{0:T(1024)(128)(4,1)}), s8[4194304]{0:T(1024)(128)(4,1)S(1)}, s32[]{:S(2)}) async-start(s8[9437184]{0:T(1024)(128)(4,1)} %bitcast.73), calls=%async_computation.3 | async-start | bytes 8388608
  78.7 8.7 %slice-start.6 = ((s8[4718592]{0:T(1024)(128)(4,1)}), s8[4194304]{0:T(1024)(128)(4,1)S(1)}, s32[]{:S(2)}) async-start(s8[4718592]{0:T(1024)(128)(4,1)} %bitcast.77), calls=%async_computation.9 | async-start | bytes 8388608
  79.9 7.5 %slice-start.1 = ((s8[9437184]{0:T(1024)(128)(4,1)}), s8[4194304]{0:T(1024)(128)(4,1)S(1)}, s32[]{:S(2)}) async-start(s8[9437184]{0:T(1024)(128)(4,1)} %bitcast.73), calls=%async_computation.4 | async-start | bytes 8388608
  82.3 5.1 %slice-start.7 = ((s8[4718592]{0:T(1024)(128)(4,1)}), s8[524288]{0:T(1024)(128)(4,1)S(1)}, s32[]{:S(2)}) async-start(s8[4718592]{0:T(1024)(128)(4,1)} %bitcast.77), calls=%async_computation.10 | async-start | bytes 1048576
  83.5 3.9 %slice-start.2 = ((s8[9437184]{0:T(1024)(128)(4,1)}), s8[1048576]{0:T(1024)(128)(4,1)S(1)}, s32[]{:S(2)}) async-start(s8[9437184]{0:T(1024)(128)(4,1)} %bitcast.73), calls=%async_computation.5 | async-start | bytes 2097152
  178.3 9.8 %slice-start.3 = ((s8[9437184]{0:T(1024)(128)(4,1)}), s8[4194304]{0:T(1024)(128)(4,1)S(1)}, s32[]{:S(2)}) async-start(s8[9437184]{0:T(1024)(128)(4,1)} %bitcast.75), calls=%async_computation.6 | async-start | bytes 8388608
  179.5 8.6 %slice-start.8 = ((s8[4718592]{0:T(1024)(128)(4,1)}), s8[4194304]{0:T(1024)(128)(4,1)S(1)}, s32[]{:S(2)}) async-start(s8[4718592]{0:T(1024)(128)(4,1)} %bitcast.79), calls=%async_computation.11 | async-start | bytes 8388608
  180.8 7.4 %slice-start.4 = ((s8[9437184]{0:T(1024)(128)(4,1)}), s8[4194304]{0:T(1024)(128)(4,1)S(1)}, s32[]{:S(2)}) async-start(s8[9437184]{0:T(1024)(128)(4,1)} %bitcast.75), calls=%async_computation.7 | async-start | bytes 8388608
  183.2 5.0 %slice-start.9 = ((s8[4718592]{0:T(1024)(128)(4,1)}), s8[524288]{0:T(1024)(128)(4,1)S(1)}, s32[]{:S(2)}) async-start(s8[4718592]{0:T(1024)(128)(4,1)} %bitcast.79), calls=%async_computation.12 | async-start | bytes 1048576
  184.4 3.8 %slice-start.5 = ((s8[9437184]{0:T(1024)(128)(4,1)}), s8[1048576]{0:T(1024)(128)(4,1)S(1)}, s32[]{:S(2)}) async-start(s8[9437184]{0:T(1024)(128)(4,1)} %bitcast.75), calls=%async_computation.8 | async-start | bytes 2097152
  214.4 10.0 %copy-start.2 = (f32[12,32,256]{2,1,0:T(8,128)}, f32[12,32,256]{2,1,0:T(8,128)S(1)}, u32[]{:S(2)}) copy-start(f32[12,32,256]{2,1,0:T(8,128)S(1)} %div.13) | copy-start | bytes 1179652
  225.5 14.4 %copy-start.3 = (f32[72,2048]{1,0:T(8,128)S(1)}, f32[72,2048]{1,0:T(8,128)}, u32[]{:S(2)}) copy-start(f32[72,2048]{1,0:T(8,128)} %param.9) | copy-start | bytes 1769476
  225.5 14.4 %copy-start.4 = (f32[72,2048]{1,0:T(8,128)S(1)}, f32[72,2048]{1,0:T(8,128)}, u32[]{:S(2)}) copy-start(f32[72,2048]{1,0:T(8,128)} %param.8) | copy-start | bytes 1769476
  304.0 4.9 %copy-start.1 = (f32[12,32,256]{2,1,0:T(8,128)S(1)}, f32[12,32,256]{2,1,0:T(8,128)}, u32[]{:S(2)}) copy-start(f32[12,32,256]{2,1,0:T(8,128)} %param.7) | copy-start | bytes 1179652
Sparse Core Ops, SparseCore 0:
  252.4 51.5 all-gather.1

commit v2 on v1

--- a/solution.py
+++ b/solution.py
@@ -19,8 +19,15 @@
 LANES = 128
 
 
-def _peer(name, index):
-    return tuple(index if axis == name else lax.axis_index(axis) for axis in MESH_AXES)
+def _coord(level):
+    name, n, stride = level
+    return lax.rem(lax.div(lax.axis_index(name), stride), n)
+
+
+def _peer(level, j):
+    name, n, stride = level
+    base = lax.axis_index(name) + (j - _coord(level)) * stride
+    return tuple(base if axis == name else lax.axis_index(axis) for axis in MESH_AXES)
 
 
 def _allreduce_kernel(levels, x_ref, o_ref, *scratch):
@@ -35,14 +42,14 @@
     ag_recv = [next(it) for _ in range(n_lev)]
     local_sem = next(it)
 
-    me = [lax.axis_index(name) for name, _ in levels]
+    me = [_coord(level) for level in levels]
 
     barrier = pltpu.get_barrier_semaphore()
     total_peers = 0
-    for lev, (name, n) in enumerate(levels):
+    for lev, (name, n, _) in enumerate(levels):
         for off in range(1, n):
             j = lax.rem(me[lev] + off, n)
-            pl.semaphore_signal(barrier, inc=1, device_id=_peer(name, j),
+            pl.semaphore_signal(barrier, inc=1, device_id=_peer(levels[lev], j),
                                 device_id_type=pl.DeviceIdType.MESH)
         total_peers += n - 1
     pl.semaphore_wait(barrier, total_peers)
@@ -50,7 +57,7 @@
     gath_bufs = [o_ref] + gath[: n_lev - 1]
 
     src = x_ref
-    for lev, (name, n) in enumerate(levels):
+    for lev, (name, n, _) in enumerate(levels):
         m = me[lev]
         copies = []
         for off in range(1, n):
@@ -58,7 +65,7 @@
             cp = pltpu.make_async_remote_copy(
                 src_ref=src.at[j], dst_ref=recv[lev].at[m],
                 send_sem=rs_send[lev].at[off], recv_sem=rs_recv[lev].at[m],
-                device_id=_peer(name, j), device_id_type=pl.DeviceIdType.MESH)
+                device_id=_peer(levels[lev], j), device_id_type=pl.DeviceIdType.MESH)
             cp.start()
             copies.append((j, off, cp))
         own = pltpu.make_async_copy(src.at[m], recv[lev].at[m], local_sem.at[0])
@@ -68,7 +75,7 @@
             pltpu.make_async_remote_copy(
                 src_ref=src.at[j], dst_ref=recv[lev].at[j],
                 send_sem=rs_send[lev].at[off], recv_sem=rs_recv[lev].at[j],
-                device_id=_peer(name, j), device_id_type=pl.DeviceIdType.MESH).wait_recv()
+                device_id=_peer(levels[lev], j), device_id_type=pl.DeviceIdType.MESH).wait_recv()
         for j, off, cp in copies:
             cp.wait_send()
         r = recv[lev]
@@ -77,13 +84,24 @@
         else:
             dst = gath_bufs[lev].at[m]
         if len(r.shape) > 3:
-            def body(i, carry, r=r, dst=dst, n=n):
-                acc = r[0, i]
+            lead = r.shape[1:-2]
+            count = 1
+            for d in lead:
+                count *= d
+
+            def body(i, carry, r=r, dst=dst, n=n, lead=lead):
+                idx = []
+                rest = i
+                for d in reversed(lead):
+                    idx.append(lax.rem(rest, d))
+                    rest = lax.div(rest, d)
+                idx = tuple(reversed(idx))
+                acc = r[(0,) + idx]
                 for j in range(1, n):
-                    acc = acc + r[j, i]
-                dst[i] = acc
+                    acc = acc + r[(j,) + idx]
+                dst[idx] = acc
                 return carry
-            lax.fori_loop(0, r.shape[1], body, 0)
+            lax.fori_loop(0, count, body, 0)
         else:
             acc = r[0]
             for j in range(1, n):
@@ -93,7 +111,7 @@
             src = sums[lev]
 
     for lev in reversed(range(n_lev)):
-        name, n = levels[lev]
+        name, n, _ = levels[lev]
         m = me[lev]
         buf = gath_bufs[lev]
         if lev == n_lev - 1:
@@ -109,14 +127,14 @@
             cp = pltpu.make_async_remote_copy(
                 src_ref=piece, dst_ref=buf.at[m],
                 send_sem=ag_send[lev].at[off], recv_sem=ag_recv[lev].at[m],
-                device_id=_peer(name, j), device_id_type=pl.DeviceIdType.MESH)
+                device_id=_peer(levels[lev], j), device_id_type=pl.DeviceIdType.MESH)
             cp.start()
             copies.append((j, off, cp))
         for j, off, cp in copies:
             pltpu.make_async_remote_copy(
                 src_ref=piece, dst_ref=buf.at[j],
                 send_sem=ag_send[lev].at[off], recv_sem=ag_recv[lev].at[j],
-                device_id=_peer(name, j), device_id_type=pl.DeviceIdType.MESH).wait_recv()
+                device_id=_peer(levels[lev], j), device_id_type=pl.DeviceIdType.MESH).wait_recv()
         for j, off, cp in copies:
             cp.wait_send()
 
@@ -124,7 +142,7 @@
 def allreduce(x, levels, collective_id):
     shape = x.shape
     total = x.size
-    counts = [n for _, n in levels]
+    counts = [n for _, n, _ in levels]
     per = total
     for n in counts:
         per //= n
@@ -139,7 +157,7 @@
     for lev in range(len(levels) - 1):
         scratch.append(pltpu.VMEM(full[lev + 1:], jnp.float32))
     for _ in range(4):
-        for _, n in levels:
+        for _, n, _ in levels:
             scratch.append(pltpu.SemaphoreType.DMA((n,)))
     scratch.append(pltpu.SemaphoreType.DMA((1,)))
     out = pl.pallas_call(
@@ -152,6 +170,14 @@
         cost_estimate=pl.CostEstimate(flops=total * 2, bytes_accessed=total * 4 * 4, transcendentals=0),
     )(xr)
     return out.reshape(shape)
+
+
+def split_levels(name, size, inner):
+    if size % inner or size == inner:
+        return ((name, size, 1),)
+    if inner == 2:
+        return ((name, inner, 1), (name, size // inner, inner))
+    return ((name, size // inner, inner), (name, inner, 1))
 
 
 def local_gram(factor):
@@ -177,8 +203,8 @@
     corrected = grads[0].astype(jnp.float32) + error[0]
     current = query
     replicas = lax.axis_size("rep")
-    both = (("tp", lax.axis_size("tp")), ("rep", replicas))
-    rep_only = (("rep", replicas),)
+    rep_only = split_levels("rep", replicas, 4)
+    both = split_levels("tp", lax.axis_size("tp"), 2) + rep_only
     for power_pass in range(ROUNDS):
         partial_factor = jnp.einsum(
             "kdf,krf->krd", corrected, current, precision=lax.Precision.HIGHEST

time: 321 us -> 319 us (level)
  Pallas kernels: 135 us -> 131 us
    pallas_call x4, Pallas kernels: 135 us -> 131 us  [allreduce(): pl.pallas_call(functools.partial(_allreduce_kernel, tuple(levels)), out_s...]
where the time goes in v2:
time: 319 us; the launch traced here: 314 us
  Pallas kernels  131 us (41%)
  matrix products  70.5 us (22%)
  waiting for transfers between devices  38.4 us (12%)
  blocking collectives  28.1 us (9%)
  other arithmetic  15.8 us (5%)
  local copies, waits for them, and re-layouts  15.5 us (5%)
  between operations  14.7 us (5%)
    pallas_call x4, Pallas kernels, allreduce(): pl.pallas_call(functools.partial(_allreduce_kernel, tuple(levels)), out_s...  131 us
    all_gather x1, waiting for transfers between devices, local(): weight_rows = lax.all_gather(by_columns, 'rep', axis=0, tiled=True)  38.4 us
    dot_general x2, matrix products, local(): jnp.einsum('kdf,krf->krd', corrected, current, precision=lax.Precision.HI...  23.8 us
    all_to_all x1, blocking collectives, local(): lax.all_to_all(own_block, 'tp', split_axis=0, concat_axis=1, tiled=True)  17 us
    broadcast_in_dim x1, other arithmetic, local(): new_error = (corrected - approx)[None]  12.6 us
    dot_general x10, matrix products, orthonormal(): jnp.einsum('krs,ksd->krd', gram_now, ortho_basis, precision=lax.Precision...  12.5 us
    dot_general x10, matrix products, local_gram(): jnp.einsum('krd,ksd->krs', factor, factor, precision=lax.Precision.HIGHEST)  12.2 us
    dot_general x2, matrix products, local(): jnp.einsum('kdf,krd->krf', corrected, ortho_basis, precision=lax.Precisio...  12 us
  transfers between devices with their start and end apart: 1, of which 1 were waited for; matrix products, arithmetic and copies ran while one was open for 4% of the time, Pallas kernels for 0%

profile of v2, /device:TPU:1, one launch (start us, length us, event | category | flops | bytes accessed | tf_op | source)
XLA Modules:
  0.0 314.4 jit_solution(12947462777988126352)
XLA Ops:
  7.2 0.0 all-gather.2.cloned.1.call-start
  7.2 0.9 copy-done
  8.2 12.1 %fusion.9 = f32[12,32,768]{2,1,0:T(8,128)S(1)} fusion(f32[12,32,256]{2,1,0:T(8,128)S(1)} %copy-done, f32[1,12,768,256]{3,2,1,0:T(8,128)} %param.6, bf16[1,12,768,256]{3,2,1,0:T(8,128)(2,1)} %param.5), kind=kOutput, calls=%fused_computation.11 | convolution fusion | flops 910688256 | bytes 15728640 | tf_op jit(solution)/shard_map/kdf,krf->krd/dot_general | solution.py:209
  20.3 1.4 reshape.68.x_ref
  21.7 45.8 %shard_map.92 = f32[2,4,4,4,18,128]{5,4,3,2,1,0:T(8,128)} custom-call(f32[2,4,4,4,18,128]{5,4,3,2,1,0:T(8,128)} %reshape.68.x_ref), custom_call_target="tpu_custom_call" | custom-call | flops 589824 | bytes 4718592 | tf_op jit(solution)/shard_map/pallas_call | solution.py:163
  67.6 1.8 reshape.69
  69.4 1.3 select_reduce_fusion.1
  70.7 1.3 fusion.21
  72.0 1.2 fusion.33
  73.2 1.2 fusion.20
  74.5 1.2 fusion.34
  75.7 1.2 fusion.19
  76.9 1.2 fusion.35
  78.1 1.2 fusion.18
  79.3 1.2 fusion.36
  80.5 1.4 fusion.17
  82.0 6.0 %fusion.4 = f32[12,32,256]{2,1,0:T(8,128)S(1)} fusion(f32[12,32,768]{2,1,0:T(8,128)S(1)} %fusion.17, f32[1,12,768,256]{3,2,1,0:T(8,128)S(1)} %bitcast.78, bf16[1,12,768,256]{3,2,1,0:T(8,128)(2,1)S(1)} %bitcast.82), kind=kOutput, calls=%fused_computation.5 | convolution fusion | flops 910688256 | bytes 15728640 | tf_op jit(solution)/shard_map/kdf,krd->krf/dot_general | solution.py:214
  87.9 0.8 reshape.70.x_ref
  88.7 21.1 %shard_map.93 = f32[4,4,48,128]{3,2,1,0:T(8,128)} custom-call(f32[4,4,48,128]{3,2,1,0:T(8,128)} %reshape.70.x_ref), custom_call_target="tpu_custom_call" | custom-call | flops 196608 | bytes 1572864 | tf_op jit(solution)/shard_map/pallas_call | solution.py:163
  109.8 1.0 broadcast_multiply_fusion.1
  110.9 0.1 div.11
  111.0 11.7 %fusion.2 = f32[12,32,768]{2,1,0:T(8,128)S(1)} fusion(f32[12,32,256]{2,1,0:T(8,128)S(1)} %div.11, f32[1,12,768,256]{3,2,1,0:T(8,128)} %param.6, bf16[1,12,768,256]{3,2,1,0:T(8,128)(2,1)} %param.5), kind=kOutput, calls=%fused_computation.3 | convolution fusion | flops 910688256 | bytes 15728640 | tf_op jit(solution)/shard_map/kdf,krf->krd/dot_general | solution.py:209
  122.7 1.4 reshape.71.x_ref
  124.1 43.9 %shard_map.94 = f32[2,4,4,4,18,128]{5,4,3,2,1,0:T(8,128)} custom-call(f32[2,4,4,4,18,128]{5,4,3,2,1,0:T(8,128)} %reshape.71.x_ref), custom_call_target="tpu_custom_call" | custom-call | flops 589824 | bytes 4718592 | tf_op jit(solution)/shard_map/pallas_call | solution.py:163
  168.0 2.0 reshape.72
  170.0 1.3 select_reduce_fusion
  171.3 1.3 fusion.16
  172.6 1.2 fusion.37
  173.8 1.2 fusion.15
  175.1 1.2 fusion.38
  176.3 1.2 fusion.14
  177.5 1.2 fusion.39
  178.7 1.2 fusion.13
  179.9 1.2 fusion.40
  181.1 1.4 fusion.12
  182.5 6.0 %fusion = f32[12,32,256]{2,1,0:T(8,128)S(1)} fusion(f32[12,32,768]{2,1,0:T(8,128)S(1)} %fusion.12, f32[1,12,768,256]{3,2,1,0:T(8,128)S(1)} %bitcast.80, bf16[1,12,768,256]{3,2,1,0:T(8,128)(2,1)S(1)} %bitcast.84), kind=kOutput, calls=%fused_computation.1 | convolution fusion | flops 910688256 | bytes 15728640 | tf_op jit(solution)/shard_map/kdf,krd->krf/dot_general | solution.py:214
  188.5 0.8 reshape.73.x_ref
  189.3 20.4 %shard_map.95 = f32[4,4,48,128]{3,2,1,0:T(8,128)} custom-call(f32[4,4,48,128]{3,2,1,0:T(8,128)} %reshape.73.x_ref), custom_call_target="tpu_custom_call" | custom-call | flops 196608 | bytes 1572864 | tf_op jit(solution)/shard_map/pallas_call | solution.py:163
  209.8 1.0 broadcast_multiply_fusion
  210.8 0.1 div.13
  210.9 10.0 %fusion.41 = f32[12,768,256]{2,1,0:T(8,128)} fusion(f32[12,32,768]{2,1,0:T(8,128)S(1)} %fusion.12, f32[12,32,256]{2,1,0:T(8,128)S(1)} %div.13), kind=kOutput, calls=%fused_computation.62 | convolution fusion | flops 905969664 | bytes 11010048 | tf_op jit(solution)/shard_map/krd,krf->kdf/dot_general | solution.py:218
  220.9 1.1 constant_dynamic-slice_fusion
  222.0 17.0 %all_to_all.38 = f32[8,72,256]{2,1,0:T(8,128)S(1)} all-to-all(f32[8,72,256]{2,1,0:T(8,128)S(1)} %bitcast.88), channel_id=1, replica_groups=mesh['rep'=16,'tp'=8] {'tp'}, dimensions={0} | all-to-all | bytes 1179648 | tf_op jit(solution)/shard_map/all_to_all | solution.py:226
  239.1 1.2 fusion.32
  240.3 11.1 %all_to_all.39 = bf16[72,8,256]{2,0,1:T(8,128)(2,1)} all-to-all(bf16[72,8,256]{2,0,1:T(8,128)(2,1)S(1)} %bitcast.92), channel_id=1, replica_groups=mesh['rep'=16,'tp'=8] {'tp'}, dimensions={1} | all-to-all | bytes 589824 | tf_op jit(solution)/shard_map/all_to_all | solution.py:230
  251.5 12.6 %fusion.8 = f32[1,12,768,256]{3,2,1,0:T(8,128)} fusion(f32[12,768,256]{2,1,0:T(8,128)} %fusion.41, f32[1,12,768,256]{3,2,1,0:T(8,128)} %param.6, bf16[1,12,768,256]{3,2,1,0:T(8,128)(2,1)} %param.5), kind=kLoop, calls=%fused_computation.9 | loop fusion | flops 7077888 | bytes 33030144 | tf_op jit(solution)/shard_map/broadcast_in_dim | solution.py:219
  264.0 38.4 %all-gather.2.cloned.1.call-done = bf16[9216,256]{1,0:T(8,128)(2,1)} async-done(((bf16[576,256]{1,0:T(8,128)(2,1)}), bf16[9216,256]{1,0:T(8,128)(2,1)}) %all-gather.2.cloned.1.call-update) | async-done | bytes 4718608 | tf_op jit(solution)/shard_map/all_gather | solution.py:231
  302.4 4.9 %copy.20 = bf16[12,768,256]{2,1,0:T(8,128)(2,1)} copy(bf16[12,768,256]{2,1,0:T(8,128)(2,1)} %bitcast.86) | data formatting | bytes 9437184
  (39 shorter events, 0.2 us)
Async XLA Ops:
  7.2 1.0 copy-start
  7.2 295.3 %all-gather.2.cloned.1.call-start = ((), (), s32[]{:S(2)}) async-start(), calls=%async_computation.2 | async-start | bytes 5013504 | tf_op jit(solution)/shard_map/all_gather | solution.py:231
  72.0 9.9 %slice-start = ((s8[9437184]{0:T(1024)(128)(4,1)}), s8[4194304]{0:T(1024)(128)(4,1)S(1)}, s32[]{:S(2)}) async-start(s8[9437184]{0:T(1024)(128)(4,1)} %bitcast.77), calls=%async_computation.3 | async-start | bytes 8388608
  73.2 8.7 %slice-start.6 = ((s8[4718592]{0:T(1024)(128)(4,1)}), s8[4194304]{0:T(1024)(128)(4,1)S(1)}, s32[]{:S(2)}) async-start(s8[4718592]{0:T(1024)(128)(4,1)} %bitcast.81), calls=%async_computation.9 | async-start | bytes 8388608
  74.4 7.5 %slice-start.1 = ((s8[9437184]{0:T(1024)(128)(4,1)}), s8[4194304]{0:T(1024)(128)(4,1)S(1)}, s32[]{:S(2)}) async-start(s8[9437184]{0:T(1024)(128)(4,1)} %bitcast.77), calls=%async_computation.4 | async-start | bytes 8388608
  76.8 5.1 %slice-start.7 = ((s8[4718592]{0:T(1024)(128)(4,1)}), s8[524288]{0:T(1024)(128)(4,1)S(1)}, s32[]{:S(2)}) async-start(s8[4718592]{0:T(1024)(128)(4,1)} %bitcast.81), calls=%async_computation.10 | async-start | bytes 1048576
  78.1 3.9 %slice-start.2 = ((s8[9437184]{0:T(1024)(128)(4,1)}), s8[1048576]{0:T(1024)(128)(4,1)S(1)}, s32[]{:S(2)}) async-start(s8[9437184]{0:T(1024)(128)(4,1)} %bitcast.77), calls=%async_computation.5 | async-start | bytes 2097152
  172.6 9.8 %slice-start.3 = ((s8[9437184]{0:T(1024)(128)(4,1)}), s8[4194304]{0:T(1024)(128)(4,1)S(1)}, s32[]{:S(2)}) async-start(s8[9437184]{0:T(1024)(128)(4,1)} %bitcast.79), calls=%async_computation.6 | async-start | bytes 8388608
  173.8 8.6 %slice-start.8 = ((s8[4718592]{0:T(1024)(128)(4,1)}), s8[4194304]{0:T(1024)(128)(4,1)S(1)}, s32[]{:S(2)}) async-start(s8[4718592]{0:T(1024)(128)(4,1)} %bitcast.83), calls=%async_computation.11 | async-start | bytes 8388608
  175.1 7.4 %slice-start.4 = ((s8[9437184]{0:T(1024)(128)(4,1)}), s8[4194304]{0:T(1024)(128)(4,1)S(1)}, s32[]{:S(2)}) async-start(s8[9437184]{0:T(1024)(128)(4,1)} %bitcast.79), calls=%async_computation.7 | async-start | bytes 8388608
  177.5 5.0 %slice-start.9 = ((s8[4718592]{0:T(1024)(128)(4,1)}), s8[524288]{0:T(1024)(128)(4,1)S(1)}, s32[]{:S(2)}) async-start(s8[4718592]{0:T(1024)(128)(4,1)} %bitcast.83), calls=%async_computation.12 | async-start | bytes 1048576
  178.7 3.8 %slice-start.5 = ((s8[9437184]{0:T(1024)(128)(4,1)}), s8[1048576]{0:T(1024)(128)(4,1)S(1)}, s32[]{:S(2)}) async-start(s8[9437184]{0:T(1024)(128)(4,1)} %bitcast.79), calls=%async_computation.8 | async-start | bytes 2097152
  210.9 10.0 %copy-start.2 = (f32[12,32,256]{2,1,0:T(8,128)}, f32[12,32,256]{2,1,0:T(8,128)S(1)}, u32[]{:S(2)}) copy-start(f32[12,32,256]{2,1,0:T(8,128)S(1)} %div.13) | copy-start | bytes 1179652
  222.0 17.1 %copy-start.3 = (f32[72,2048]{1,0:T(8,128)S(1)}, f32[72,2048]{1,0:T(8,128)}, u32[]{:S(2)}) copy-start(f32[72,2048]{1,0:T(8,128)} %param.9) | copy-start | bytes 1769476
  222.0 17.1 %copy-start.4 = (f32[72,2048]{1,0:T(8,128)S(1)}, f32[72,2048]{1,0:T(8,128)}, u32[]{:S(2)}) copy-start(f32[72,2048]{1,0:T(8,128)} %param.8) | copy-start | bytes 1769476
  302.4 4.9 %copy-start.1 = (f32[12,32,256]{2,1,0:T(8,128)S(1)}, f32[12,32,256]{2,1,0:T(8,128)}, u32[]{:S(2)}) copy-start(f32[12,32,256]{2,1,0:T(8,128)} %param.7) | copy-start | bytes 1179652
Sparse Core Ops, SparseCore 0:
  251.6 50.8 all-gather.1

commit v3 on v2

--- a/solution.py
+++ b/solution.py
@@ -203,8 +203,8 @@
     corrected = grads[0].astype(jnp.float32) + error[0]
     current = query
     replicas = lax.axis_size("rep")
-    rep_only = split_levels("rep", replicas, 4)
-    both = split_levels("tp", lax.axis_size("tp"), 2) + rep_only
+    rep_only = (("rep", replicas, 1),)
+    both = split_levels("tp", lax.axis_size("tp"), 2) + split_levels("rep", replicas, 4)
     for power_pass in range(ROUNDS):
         partial_factor = jnp.einsum(
             "kdf,krf->krd", corrected, current, precision=lax.Precision.HIGHEST
@@ -219,9 +219,17 @@
     new_error = (corrected - approx)[None]
     matrices, model_width, shard_cols = approx.shape
     block_rows = matrices * model_width // replicas
-    approx_rows = approx.reshape(matrices * model_width, shard_cols)
+    assert block_rows <= model_width and matrices >= 2
+    first_row = lax.axis_index("rep") * block_rows
+    first_mat = jnp.minimum(first_row // model_width, matrices - 2)
+    pair = jnp.einsum(
+        "krd,krf->kdf",
+        lax.dynamic_slice_in_dim(ortho_basis, first_mat, 2, 0),
+        lax.dynamic_slice_in_dim(current, first_mat, 2, 0),
+        precision=lax.Precision.HIGHEST,
+    ).reshape(2 * model_width, shard_cols)
     own_block = lax.dynamic_slice_in_dim(
-        approx_rows, lax.axis_index("rep") * block_rows, block_rows, 0
+        pair, first_row - first_mat * model_width, block_rows, 0
     )
     flat_approx = lax.all_to_all(own_block, "tp", split_axis=0, concat_axis=1, tiled=True)
     new_momentum = MOMENTUM_DECAY * momentum + flat_approx

time: 319 us -> 302 us (0.947)
  other arithmetic: 15.8 us -> 3.26 us
  Pallas kernels: 131 us -> 125 us
  matrix products: 70.5 us -> 75.3 us
    broadcast_in_dim x1 -> x0, other arithmetic: 12.6 us -> none  [local(): new_error = (corrected - approx)[None]]
    pallas_call x4, Pallas kernels: 131 us -> 125 us  [allreduce(): pl.pallas_call(functools.partial(_allreduce_kernel, tuple(levels)), out_s...]
    dot_general x1, matrix products: 9.97 us -> 13.3 us  [local(): jnp.einsum('krd,krf->kdf', ortho_basis, current, precision=lax.Precision....]
where the time goes in v3:
time: 302 us; the launch traced here: 298 us
  Pallas kernels  125 us (41%)
  matrix products  75.3 us (25%)
  waiting for transfers between devices  37.9 us (13%)
  blocking collectives  26.7 us (9%)
  between operations  14.7 us (5%)
  local copies, waits for them, and re-layouts  14.4 us (5%)
  other arithmetic  3.26 us (1%)
    pallas_call x4, Pallas kernels, allreduce(): pl.pallas_call(functools.partial(_allreduce_kernel, tuple(levels)), out_s...  125 us
    all_gather x1, waiting for transfers between devices, local(): weight_rows = lax.all_gather(by_columns, 'rep', axis=0, tiled=True)  37.9 us
    dot_general x2, matrix products, local(): jnp.einsum('kdf,krf->krd', corrected, current, precision=lax.Precision.HI...  23.8 us
    all_to_all x1, blocking collectives, local(): lax.all_to_all(own_block, 'tp', split_axis=0, concat_axis=1, tiled=True)  15.5 us
    dot_general x1, matrix products, local(): jnp.einsum('krd,krf->kdf', ortho_basis, current, precision=lax.Precision....  13.3 us
    dot_general x10, matrix products, orthonormal(): jnp.einsum('krs,ksd->krd', gram_now, ortho_basis, precision=lax.Precision...  12.5 us
    dot_general x10, matrix products, local_gram(): jnp.einsum('krd,ksd->krs', factor, factor, precision=lax.Precision.HIGHEST)  12.2 us
    dot_general x2, matrix products, local(): jnp.einsum('kdf,krd->krf', corrected, ortho_basis, precision=lax.Precisio...  12 us
  transfers between devices with their start and end apart: 1, of which 1 were waited for; matrix products, arithmetic and copies ran while one was open for 4% of the time, Pallas kernels for 0%

profile of v3, /device:TPU:1, one launch (start us, length us, event | category | flops | bytes accessed | tf_op | source)
XLA Modules:
  0.0 297.7 jit_solution(10216622890791049005)
XLA Ops:
  7.2 0.0 all-gather.2.cloned.1.call-start
  7.3 0.9 copy-done
  8.2 12.1 %fusion.9 = f32[12,32,768]{2,1,0:T(8,128)S(1)} fusion(f32[12,32,256]{2,1,0:T(8,128)S(1)} %copy-done, f32[1,12,768,256]{3,2,1,0:T(8,128)} %param.6, bf16[1,12,768,256]{3,2,1,0:T(8,128)(2,1)} %param.5), kind=kOutput, calls=%fused_computation.11 | convolution fusion | flops 910688256 | bytes 15728640 | tf_op jit(solution)/shard_map/kdf,krf->krd/dot_general | solution.py:209
  20.3 1.4 reshape.68.x_ref
  21.7 45.8 %shard_map.92 = f32[2,4,4,4,18,128]{5,4,3,2,1,0:T(8,128)} custom-call(f32[2,4,4,4,18,128]{5,4,3,2,1,0:T(8,128)} %reshape.68.x_ref), custom_call_target="tpu_custom_call" | custom-call | flops 589824 | bytes 4718592 | tf_op jit(solution)/shard_map/pallas_call | solution.py:163
  67.6 1.8 reshape.69
  69.4 1.3 select_reduce_fusion.1
  70.7 1.3 fusion.21
  72.0 1.2 fusion.37
  73.2 1.2 fusion.20
  74.5 1.2 fusion.38
  75.7 1.2 fusion.19
  76.9 1.2 fusion.39
  78.1 1.2 fusion.18
  79.3 1.2 fusion.40
  80.5 1.4 fusion.17
  82.0 6.0 %fusion.4 = f32[12,32,256]{2,1,0:T(8,128)S(1)} fusion(f32[12,32,768]{2,1,0:T(8,128)S(1)} %fusion.17, f32[1,12,768,256]{3,2,1,0:T(8,128)S(1)} %bitcast.74, bf16[1,12,768,256]{3,2,1,0:T(8,128)(2,1)S(1)} %bitcast.78), kind=kOutput, calls=%fused_computation.5 | convolution fusion | flops 910688256 | bytes 15728640 | tf_op jit(solution)/shard_map/kdf,krd->krf/dot_general | solution.py:214
  87.9 0.8 reshape.70.x_ref
  88.7 18.5 %shard_map.93 = f32[16,48,128]{2,1,0:T(8,128)} custom-call(f32[16,48,128]{2,1,0:T(8,128)} %reshape.70.x_ref), custom_call_target="tpu_custom_call" | custom-call | flops 196608 | bytes 1572864 | tf_op jit(solution)/shard_map/pallas_call | solution.py:163
  107.2 1.0 broadcast_multiply_fusion.1
  108.3 0.1 div.15
  108.4 11.7 %fusion.2 = f32[12,32,768]{2,1,0:T(8,128)S(1)} fusion(f32[12,32,256]{2,1,0:T(8,128)S(1)} %div.15, f32[1,12,768,256]{3,2,1,0:T(8,128)} %param.6, bf16[1,12,768,256]{3,2,1,0:T(8,128)(2,1)} %param.5), kind=kOutput, calls=%fused_computation.3 | convolution fusion | flops 910688256 | bytes 15728640 | tf_op jit(solution)/shard_map/kdf,krf->krd/dot_general | solution.py:209
  120.1 1.4 reshape.71.x_ref
  121.5 42.8 %shard_map.94 = f32[2,4,4,4,18,128]{5,4,3,2,1,0:T(8,128)} custom-call(f32[2,4,4,4,18,128]{5,4,3,2,1,0:T(8,128)} %reshape.71.x_ref), custom_call_target="tpu_custom_call" | custom-call | flops 589824 | bytes 4718592 | tf_op jit(solution)/shard_map/pallas_call | solution.py:163
  164.3 2.0 reshape.72
  166.3 1.3 select_reduce_fusion
  167.6 1.3 fusion.16
  168.9 1.2 fusion.41
  170.1 1.2 fusion.15
  171.4 1.2 fusion.42
  172.6 1.2 fusion.14
  173.8 1.2 fusion.43
  175.0 1.2 fusion.13
  176.2 1.2 fusion.44
  177.4 1.4 fusion.12
  178.8 6.0 %fusion = f32[12,32,256]{2,1,0:T(8,128)S(1)} fusion(f32[12,32,768]{2,1,0:T(8,128)S(1)} %fusion.12, f32[1,12,768,256]{3,2,1,0:T(8,128)S(1)} %bitcast.76, bf16[1,12,768,256]{3,2,1,0:T(8,128)(2,1)S(1)} %bitcast.80), kind=kOutput, calls=%fused_computation.1 | convolution fusion | flops 910688256 | bytes 15728640 | tf_op jit(solution)/shard_map/kdf,krd->krf/dot_general | solution.py:214
  184.8 0.8 reshape.73.x_ref
  185.6 18.3 %shard_map.95 = f32[16,48,128]{2,1,0:T(8,128)} custom-call(f32[16,48,128]{2,1,0:T(8,128)} %reshape.73.x_ref), custom_call_target="tpu_custom_call" | custom-call | flops 196608 | bytes 1572864 | tf_op jit(solution)/shard_map/pallas_call | solution.py:163
  203.9 1.0 broadcast_multiply_fusion
  204.9 0.1 div.17
  205.1 1.4 fusion.26
  206.6 15.5 %all_to_all.38 = f32[8,72,256]{2,1,0:T(8,128)S(1)} all-to-all(f32[8,72,256]{2,1,0:T(8,128)S(1)} %bitcast.84), channel_id=1, replica_groups=mesh['rep'=16,'tp'=8] {'tp'}, dimensions={0} | all-to-all | bytes 1179648 | tf_op jit(solution)/shard_map/all_to_all | solution.py:234
  222.2 1.2 fusion.36
  223.4 11.1 %all_to_all.39 = bf16[72,8,256]{2,0,1:T(8,128)(2,1)} all-to-all(bf16[72,8,256]{2,0,1:T(8,128)(2,1)S(1)} %bitcast.88), channel_id=1, replica_groups=mesh['rep'=16,'tp'=8] {'tp'}, dimensions={1} | all-to-all | bytes 589824 | tf_op jit(solution)/shard_map/all_to_all | solution.py:238
  234.5 0.0 all-gather.2.cloned.1.call-update
  234.6 13.3 %fusion.8 = f32[1,12,768,256]{3,2,1,0:T(8,128)} fusion(f32[12,32,768]{2,1,0:T(8,128)S(1)} %fusion.12, f32[12,32,256]{2,1,0:T(8,128)S(1)} %div.17, f32[1,12,768,256]{3,2,1,0:T(8,128)} %param.6, bf16[1,12,768,256]{3,2,1,0:T(8,128)(2,1)} %param.5), kind=kOutput, calls=%fused_computation.9 | convolution fusion | flops 913047552 | bytes 25165824 | tf_op jit(solution)/shard_map/krd,krf->kdf/dot_general | solution.py:218
  247.9 37.9 %all-gather.2.cloned.1.call-done = bf16[9216,256]{1,0:T(8,128)(2,1)} async-done(((bf16[576,256]{1,0:T(8,128)(2,1)}), bf16[9216,256]{1,0:T(8,128)(2,1)}) %all-gather.2.cloned.1.call-update) | async-done | bytes 4718608 | tf_op jit(solution)/shard_map/all_gather | solution.py:239
  285.8 4.9 %copy.20 = bf16[12,768,256]{2,1,0:T(8,128)(2,1)} copy(bf16[12,768,256]{2,1,0:T(8,128)(2,1)} %bitcast.81) | data formatting | bytes 9437184
  (39 shorter events, 0.3 us)
Async XLA Ops:
  7.2 1.0 copy-start
  7.2 278.6 %all-gather.2.cloned.1.call-start = ((), (), s32[]{:S(2)}) async-start(), calls=%async_computation.2 | async-start | bytes 5013504 | tf_op jit(solution)/shard_map/all_gather | solution.py:239
  72.0 9.9 %slice-start = ((s8[9437184]{0:T(1024)(128)(4,1)}), s8[4194304]{0:T(1024)(128)(4,1)S(1)}, s32[]{:S(2)}) async-start(s8[9437184]{0:T(1024)(128)(4,1)} %bitcast.73), calls=%async_computation.3 | async-start | bytes 8388608
  73.2 8.7 %slice-start.6 = ((s8[4718592]{0:T(1024)(128)(4,1)}), s8[4194304]{0:T(1024)(128)(4,1)S(1)}, s32[]{:S(2)}) async-start(s8[4718592]{0:T(1024)(128)(4,1)} %bitcast.77), calls=%async_computation.9 | async-start | bytes 8388608
  74.4 7.5 %slice-start.1 = ((s8[9437184]{0:T(1024)(128)(4,1)}), s8[4194304]{0:T(1024)(128)(4,1)S(1)}, s32[]{:S(2)}) async-start(s8[9437184]{0:T(1024)(128)(4,1)} %bitcast.73), calls=%async_computation.4 | async-start | bytes 8388608
  76.8 5.1 %slice-start.7 = ((s8[4718592]{0:T(1024)(128)(4,1)}), s8[524288]{0:T(1024)(128)(4,1)S(1)}, s32[]{:S(2)}) async-start(s8[4718592]{0:T(1024)(128)(4,1)} %bitcast.77), calls=%async_computation.10 | async-start | bytes 1048576
  78.1 3.9 %slice-start.2 = ((s8[9437184]{0:T(1024)(128)(4,1)}), s8[1048576]{0:T(1024)(128)(4,1)S(1)}, s32[]{:S(2)}) async-start(s8[9437184]{0:T(1024)(128)(4,1)} %bitcast.73), calls=%async_computation.5 | async-start | bytes 2097152
  168.9 9.8 %slice-start.3 = ((s8[9437184]{0:T(1024)(128)(4,1)}), s8[4194304]{0:T(1024)(128)(4,1)S(1)}, s32[]{:S(2)}) async-start(s8[9437184]{0:T(1024)(128)(4,1)} %bitcast.75), calls=%async_computation.6 | async-start | bytes 8388608
  170.1 8.6 %slice-start.8 = ((s8[4718592]{0:T(1024)(128)(4,1)}), s8[4194304]{0:T(1024)(128)(4,1)S(1)}, s32[]{:S(2)}) async-start(s8[4718592]{0:T(1024)(128)(4,1)} %bitcast.79), calls=%async_computation.11 | async-start | bytes 8388608
  171.4 7.4 %slice-start.4 = ((s8[9437184]{0:T(1024)(128)(4,1)}), s8[4194304]{0:T(1024)(128)(4,1)S(1)}, s32[]{:S(2)}) async-start(s8[9437184]{0:T(1024)(128)(4,1)} %bitcast.75), calls=%async_computation.7 | async-start | bytes 8388608
  173.8 5.0 %slice-start.9 = ((s8[4718592]{0:T(1024)(128)(4,1)}), s8[524288]{0:T(1024)(128)(4,1)S(1)}, s32[]{:S(2)}) async-start(s8[4718592]{0:T(1024)(128)(4,1)} %bitcast.79), calls=%async_computation.12 | async-start | bytes 1048576
  175.0 3.8 %slice-start.5 = ((s8[9437184]{0:T(1024)(128)(4,1)}), s8[1048576]{0:T(1024)(128)(4,1)S(1)}, s32[]{:S(2)}) async-start(s8[9437184]{0:T(1024)(128)(4,1)} %bitcast.75), calls=%async_computation.8 | async-start | bytes 2097152
  205.0 29.5 %copy-start.2 = (f32[12,32,256]{2,1,0:T(8,128)}, f32[12,32,256]{2,1,0:T(8,128)S(1)}, u32[]{:S(2)}) copy-start(f32[12,32,256]{2,1,0:T(8,128)S(1)} %div.17) | copy-start | bytes 1179652
  206.6 15.6 %copy-start.3 = (f32[72,2048]{1,0:T(8,128)S(1)}, f32[72,2048]{1,0:T(8,128)}, u32[]{:S(2)}) copy-start(f32[72,2048]{1,0:T(8,128)} %param.9) | copy-start | bytes 1769476
  206.6 15.6 %copy-start.4 = (f32[72,2048]{1,0:T(8,128)S(1)}, f32[72,2048]{1,0:T(8,128)}, u32[]{:S(2)}) copy-start(f32[72,2048]{1,0:T(8,128)} %param.8) | copy-start | bytes 1769476
  285.8 4.9 %copy-start.1 = (f32[12,32,256]{2,1,0:T(8,128)S(1)}, f32[12,32,256]{2,1,0:T(8,128)}, u32[]{:S(2)}) copy-start(f32[12,32,256]{2,1,0:T(8,128)} %param.7) | copy-start | bytes 1179652
Sparse Core Ops, SparseCore 0:
  234.7 51.0 all-gather.1

commit v4 on v3

--- a/solution.py
+++ b/solution.py
@@ -172,6 +172,99 @@
     return out.reshape(shape)
 
 
+def _update_kernel(x_ref, mom_ref, master_ref, mom_out, master_out, cols_out,
+                   rows_buf, work_buf, send1, recv1, send2, recv2, local_sem):
+    n, rows, cols = x_ref.shape
+    me = lax.axis_index("tp")
+    barrier = pltpu.get_barrier_semaphore()
+    for off in range(1, n):
+        j = lax.rem(me + off, n)
+        pl.semaphore_signal(barrier, inc=1, device_id=_peer(("tp", n, 1), j),
+                            device_id_type=pl.DeviceIdType.MESH)
+    pl.semaphore_wait(barrier, n - 1)
+
+    def to_rows(j, src):
+        return pltpu.make_async_remote_copy(
+            src_ref=src, dst_ref=rows_buf.at[:, pl.ds(pl.multiple_of(me * cols, cols), cols)],
+            send_sem=send1.at[j], recv_sem=recv1.at[me],
+            device_id=_peer(("tp", n, 1), j), device_id_type=pl.DeviceIdType.MESH)
+
+    copies = []
+    for off in range(1, n):
+        j = lax.rem(me + off, n)
+        cp = to_rows(j, x_ref.at[j])
+        cp.start()
+        copies.append((j, cp))
+    own = pltpu.make_async_copy(
+        x_ref.at[me], rows_buf.at[:, pl.ds(pl.multiple_of(me * cols, cols), cols)], local_sem.at[0])
+    own.start()
+    own.wait()
+    for j, cp in copies:
+        pltpu.make_async_remote_copy(
+            src_ref=x_ref.at[j], dst_ref=rows_buf.at[:, pl.ds(pl.multiple_of(j * cols, cols), cols)],
+            send_sem=send1.at[j], recv_sem=recv1.at[j],
+            device_id=_peer(("tp", n, 1), j), device_id_type=pl.DeviceIdType.MESH).wait_recv()
+    for j, cp in copies:
+        cp.wait_send()
+
+    new_mom = MOMENTUM_DECAY * mom_ref[...] + rows_buf[...]
+    new_master = master_ref[...] - LEARNING_RATE * new_mom
+    mom_out[...] = new_mom
+    master_out[...] = new_master
+    work_buf[...] = new_master.astype(work_buf.dtype)
+
+    copies = []
+    for off in range(1, n):
+        j = lax.rem(me + off, n)
+        cp = pltpu.make_async_remote_copy(
+            src_ref=work_buf.at[:, pl.ds(pl.multiple_of(j * cols, cols), cols)], dst_ref=cols_out.at[me],
+            send_sem=send2.at[j], recv_sem=recv2.at[me],
+            device_id=_peer(("tp", n, 1), j), device_id_type=pl.DeviceIdType.MESH)
+        cp.start()
+        copies.append((j, cp))
+    own = pltpu.make_async_copy(
+        work_buf.at[:, pl.ds(pl.multiple_of(me * cols, cols), cols)], cols_out.at[me], local_sem.at[0])
+    own.start()
+    own.wait()
+    for j, cp in copies:
+        pltpu.make_async_remote_copy(
+            src_ref=work_buf.at[:, pl.ds(pl.multiple_of(j * cols, cols), cols)], dst_ref=cols_out.at[j],
+            send_sem=send2.at[j], recv_sem=recv2.at[j],
+            device_id=_peer(("tp", n, 1), j), device_id_type=pl.DeviceIdType.MESH).wait_recv()
+    for j, cp in copies:
+        cp.wait_send()
+
+
+def flat_update(own_block, momentum, master, n, collective_id):
+    block_rows, cols = own_block.shape
+    rows = block_rows // n
+    x = own_block.reshape(n, rows, cols)
+    f32 = jnp.float32
+    vmem = pl.BlockSpec(memory_space=pltpu.VMEM)
+    return pl.pallas_call(
+        _update_kernel,
+        out_shape=(
+            jax.ShapeDtypeStruct(momentum.shape, f32),
+            jax.ShapeDtypeStruct(master.shape, f32),
+            jax.ShapeDtypeStruct((n, rows, cols), jnp.bfloat16),
+        ),
+        in_specs=[vmem, vmem, vmem],
+        out_specs=(vmem, vmem, vmem),
+        scratch_shapes=[
+            pltpu.VMEM((rows, n * cols), f32),
+            pltpu.VMEM((rows, n * cols), jnp.bfloat16),
+            pltpu.SemaphoreType.DMA((n,)),
+            pltpu.SemaphoreType.DMA((n,)),
+            pltpu.SemaphoreType.DMA((n,)),
+            pltpu.SemaphoreType.DMA((n,)),
+            pltpu.SemaphoreType.DMA((1,)),
+        ],
+        compiler_params=pltpu.CompilerParams(collective_id=collective_id, has_side_effects=True),
+        cost_estimate=pl.CostEstimate(flops=4 * momentum.size, bytes_accessed=5 * 4 * momentum.size,
+                                      transcendentals=0),
+    )(x, momentum, master)
+
+
 def split_levels(name, size, inner):
     if size % inner or size == inner:
         return ((name, size, 1),)
@@ -219,23 +312,21 @@
     new_error = (corrected - approx)[None]
     matrices, model_width, shard_cols = approx.shape
     block_rows = matrices * model_width // replicas
-    assert block_rows <= model_width and matrices >= 2
+    span = min(matrices, -(-block_rows // model_width) + 1)
     first_row = lax.axis_index("rep") * block_rows
-    first_mat = jnp.minimum(first_row // model_width, matrices - 2)
+    first_mat = jnp.minimum(first_row // model_width, matrices - span)
     pair = jnp.einsum(
         "krd,krf->kdf",
-        lax.dynamic_slice_in_dim(ortho_basis, first_mat, 2, 0),
-        lax.dynamic_slice_in_dim(current, first_mat, 2, 0),
+        lax.dynamic_slice_in_dim(ortho_basis, first_mat, span, 0),
+        lax.dynamic_slice_in_dim(current, first_mat, span, 0),
         precision=lax.Precision.HIGHEST,
-    ).reshape(2 * model_width, shard_cols)
+    ).reshape(span * model_width, shard_cols)
     own_block = lax.dynamic_slice_in_dim(
         pair, first_row - first_mat * model_width, block_rows, 0
     )
-    flat_approx = lax.all_to_all(own_block, "tp", split_axis=0, concat_axis=1, tiled=True)
-    new_momentum = MOMENTUM_DECAY * momentum + flat_approx
-    new_master = master - LEARNING_RATE * new_momentum
-    working = new_master.astype(jnp.bfloat16)
-    by_columns = lax.all_to_all(working, "tp", split_axis=1, concat_axis=0, tiled=True)
+    new_momentum, new_master, by_columns = flat_update(
+        own_block, momentum, master, lax.axis_size("tp"), 2)
+    by_columns = by_columns.reshape(block_rows, shard_cols)
     weight_rows = lax.all_gather(by_columns, "rep", axis=0, tiled=True)
     weights = weight_rows.reshape(matrices, model_width, shard_cols)
     return (new_error, current, new_momentum, new_master, weights)

time: 302 us -> 298 us (0.987)
  blocking collectives: 26.7 us -> 0 us
  Pallas kernels: 125 us -> 146 us
    all_to_all x2 -> x0, blocking collectives: 26.7 us -> none  [the longest x1 15.5 us: local(): lax.all_to_all(own_block, 'tp', split_axis=0, concat_axis=1, tiled=True)]
    pallas_call x0 -> x1, Pallas kernels: none -> 20.8 us  [flat_update(): pl.pallas_call(_update_kernel, out_shape=(jax.ShapeDtypeStruct(momentum.s...]
    unnamed x31 -> x33, local copies, waits for them, and re-layouts: 5.87 us -> 7.5 us
  transfers between devices with their start and end apart: 1 -> 1, of which waited for: 1 -> 1; matrix products, arithmetic and copies ran while one was open for 4% -> 5% of each run, Pallas kernels for 0% -> 0%
where the time goes in v4:
time: 298 us; the launch traced here: 293 us
  Pallas kernels  146 us (49%)
  matrix products  75.3 us (25%)
  waiting for transfers between devices  38.2 us (13%)
  local copies, waits for them, and re-layouts  16.8 us (6%)
  between operations  14.7 us (5%)
    pallas_call x4, Pallas kernels, allreduce(): pl.pallas_call(functools.partial(_allreduce_kernel, tuple(levels)), out_s...  125 us
    all_gather x1, waiting for transfers between devices, local(): weight_rows = lax.all_gather(by_columns, 'rep', axis=0, tiled=True)  38.2 us
    dot_general x2, matrix products, local(): jnp.einsum('kdf,krf->krd', corrected, current, precision=lax.Precision.HI...  23.8 us
    pallas_call x1, Pallas kernels, flat_update(): pl.pallas_call(_update_kernel, out_shape=(jax.ShapeDtypeStruct(momentum.s...  20.8 us
    dot_general x1, matrix products, local(): jnp.einsum('krd,krf->kdf', ortho_basis, current, precision=lax.Precision....  13.3 us
    dot_general x10, matrix products, orthonormal(): jnp.einsum('krs,ksd->krd', gram_now, ortho_basis, precision=lax.Precision...  12.5 us
    dot_general x10, matrix products, local_gram(): jnp.einsum('krd,ksd->krs', factor, factor, precision=lax.Precision.HIGHEST)  12.2 us
    dot_general x2, matrix products, local(): jnp.einsum('kdf,krd->krf', corrected, ortho_basis, precision=lax.Precisio...  12 us
  transfers between devices with their start and end apart: 1, of which 1 were waited for; matrix products, arithmetic and copies ran while one was open for 5% of the time, Pallas kernels for 0%

profile of v4, /device:TPU:1, one launch (start us, length us, event | category | flops | bytes accessed | tf_op | source)
XLA Modules:
  0.0 293.2 jit_solution(1210682902496824263)
XLA Ops:
  7.2 0.0 all-gather.2.cloned.1.call-start
  7.3 0.9 copy-done
  8.2 12.1 %fusion.9 = f32[12,32,768]{2,1,0:T(8,128)S(1)} fusion(f32[12,32,256]{2,1,0:T(8,128)S(1)} %copy-done, f32[1,12,768,256]{3,2,1,0:T(8,128)} %param.6, bf16[1,12,768,256]{3,2,1,0:T(8,128)(2,1)} %param.5), kind=kOutput, calls=%fused_computation.11 | convolution fusion | flops 910688256 | bytes 15728640 | tf_op jit(solution)/shard_map/kdf,krf->krd/dot_general | solution.py:302
  20.3 1.4 reshape.68.x_ref
  21.7 45.8 %shard_map.92 = f32[2,4,4,4,18,128]{5,4,3,2,1,0:T(8,128)} custom-call(f32[2,4,4,4,18,128]{5,4,3,2,1,0:T(8,128)} %reshape.68.x_ref), custom_call_target="tpu_custom_call" | custom-call | flops 589824 | bytes 4718592 | tf_op jit(solution)/shard_map/pallas_call | solution.py:163
  67.6 1.8 reshape.69
  69.4 1.3 select_reduce_fusion.1
  70.7 1.3 fusion.21
  72.0 1.2 fusion.36
  73.2 1.2 fusion.20
  74.5 1.2 fusion.37
  75.7 1.2 fusion.19
  76.9 1.2 fusion.38
  78.1 1.2 fusion.18
  79.3 1.2 fusion.39
  80.5 1.4 fusion.17
  82.0 6.0 %fusion.4 = f32[12,32,256]{2,1,0:T(8,128)S(1)} fusion(f32[12,32,768]{2,1,0:T(8,128)S(1)} %fusion.17, f32[1,12,768,256]{3,2,1,0:T(8,128)S(1)} %bitcast.65, bf16[1,12,768,256]{3,2,1,0:T(8,128)(2,1)S(1)} %bitcast.69), kind=kOutput, calls=%fused_computation.5 | convolution fusion | flops 910688256 | bytes 15728640 | tf_op jit(solution)/shard_map/kdf,krd->krf/dot_general | solution.py:307
  87.9 0.8 reshape.70.x_ref
  88.7 18.5 %shard_map.93 = f32[16,48,128]{2,1,0:T(8,128)} custom-call(f32[16,48,128]{2,1,0:T(8,128)} %reshape.70.x_ref), custom_call_target="tpu_custom_call" | custom-call | flops 196608 | bytes 1572864 | tf_op jit(solution)/shard_map/pallas_call | solution.py:163
  107.2 1.0 broadcast_multiply_fusion.1
  108.3 0.1 div.15
  108.4 11.7 %fusion.2 = f32[12,32,768]{2,1,0:T(8,128)S(1)} fusion(f32[12,32,256]{2,1,0:T(8,128)S(1)} %div.15, f32[1,12,768,256]{3,2,1,0:T(8,128)} %param.6, bf16[1,12,768,256]{3,2,1,0:T(8,128)(2,1)} %param.5), kind=kOutput, calls=%fused_computation.3 | convolution fusion | flops 910688256 | bytes 15728640 | tf_op jit(solution)/shard_map/kdf,krf->krd/dot_general | solution.py:302
  120.1 1.4 reshape.71.x_ref
  121.5 42.8 %shard_map.94 = f32[2,4,4,4,18,128]{5,4,3,2,1,0:T(8,128)} custom-call(f32[2,4,4,4,18,128]{5,4,3,2,1,0:T(8,128)} %reshape.71.x_ref), custom_call_target="tpu_custom_call" | custom-call | flops 589824 | bytes 4718592 | tf_op jit(solution)/shard_map/pallas_call | solution.py:163
  164.3 2.0 reshape.72
  166.3 1.3 select_reduce_fusion
  167.6 1.3 fusion.16
  168.9 1.2 fusion.40
  170.1 1.2 fusion.15
  171.4 1.2 fusion.41
  172.6 1.2 fusion.14
  173.8 1.2 fusion.42
  175.0 1.2 fusion.13
  176.2 1.2 fusion.43
  177.4 1.4 fusion.12
  178.8 6.0 %fusion = f32[12,32,256]{2,1,0:T(8,128)S(1)} fusion(f32[12,32,768]{2,1,0:T(8,128)S(1)} %fusion.12, f32[1,12,768,256]{3,2,1,0:T(8,128)S(1)} %bitcast.67, bf16[1,12,768,256]{3,2,1,0:T(8,128)(2,1)S(1)} %bitcast.71), kind=kOutput, calls=%fused_computation.1 | convolution fusion | flops 910688256 | bytes 15728640 | tf_op jit(solution)/shard_map/kdf,krd->krf/dot_general | solution.py:307
  184.8 0.8 reshape.73.x_ref
  185.6 18.3 %shard_map.95 = f32[16,48,128]{2,1,0:T(8,128)} custom-call(f32[16,48,128]{2,1,0:T(8,128)} %reshape.73.x_ref), custom_call_target="tpu_custom_call" | custom-call | flops 196608 | bytes 1572864 | tf_op jit(solution)/shard_map/pallas_call | solution.py:163
  203.9 1.0 broadcast_multiply_fusion
  204.9 0.1 div.17
  205.1 1.4 fusion.26
  206.5 0.9 constant_dynamic-slice_fusion
  207.4 20.8 %shard_map.96 = (f32[72,2048]{1,0:T(8,128)}, f32[72,2048]{1,0:T(8,128)}, bf16[8,72,256]{2,1,0:T(8,128)(2,1)}) custom-call(f32[8,72,256]{2,1,0:T(8,128)} %bitcast.74, f32[72,2048]{1,0:T(8,128)} %mom_ref.1, f32[72,2048]{1,0:T(8,128)} %master_ref.1), custom_call_target="tpu_custom_call" | custom-call | flops 589824 | bytes 2949120 | tf_op jit(solution)/shard_map/pallas_call | solution.py:244
  228.2 13.3 %fusion.8 = f32[1,12,768,256]{3,2,1,0:T(8,128)} fusion(f32[12,32,768]{2,1,0:T(8,128)S(1)} %fusion.12, f32[12,32,256]{2,1,0:T(8,128)S(1)} %div.17, f32[1,12,768,256]{3,2,1,0:T(8,128)} %param.6, bf16[1,12,768,256]{3,2,1,0:T(8,128)(2,1)} %param.5), kind=kOutput, calls=%fused_computation.9 | convolution fusion | flops 913047552 | bytes 25165824 | tf_op jit(solution)/shard_map/krd,krf->kdf/dot_general | solution.py:311
  241.5 38.2 %all-gather.2.cloned.1.call-done = bf16[9216,256]{1,0:T(8,128)(2,1)} async-done(((bf16[576,256]{1,0:T(8,128)(2,1)}), bf16[9216,256]{1,0:T(8,128)(2,1)}) %all-gather.2.cloned.1.call-update) | async-done | bytes 4718608 | tf_op jit(solution)/shard_map/all_gather | solution.py:330
  279.7 0.8 copy.13
  280.5 0.8 copy.14
  281.3 4.9 %copy.15 = bf16[12,768,256]{2,1,0:T(8,128)(2,1)} copy(bf16[12,768,256]{2,1,0:T(8,128)(2,1)} %bitcast.72) | data formatting | bytes 9437184
  (37 shorter events, 0.1 us)
Async XLA Ops:
  7.2 1.0 copy-start
  7.2 272.5 %all-gather.2.cloned.1.call-start = ((), (), s32[]{:S(2)}) async-start(), calls=%async_computation | async-start | bytes 5013504 | tf_op jit(solution)/shard_map/all_gather | solution.py:330
  72.0 9.9 %slice-start = ((s8[9437184]{0:T(1024)(128)(4,1)}), s8[4194304]{0:T(1024)(128)(4,1)S(1)}, s32[]{:S(2)}) async-start(s8[9437184]{0:T(1024)(128)(4,1)} %bitcast.64), calls=%async_computation.1 | async-start | bytes 8388608
  73.2 8.7 %slice-start.6 = ((s8[4718592]{0:T(1024)(128)(4,1)}), s8[4194304]{0:T(1024)(128)(4,1)S(1)}, s32[]{:S(2)}) async-start(s8[4718592]{0:T(1024)(128)(4,1)} %bitcast.68), calls=%async_computation.7 | async-start | bytes 8388608
  74.4 7.5 %slice-start.1 = ((s8[9437184]{0:T(1024)(128)(4,1)}), s8[4194304]{0:T(1024)(128)(4,1)S(1)}, s32[]{:S(2)}) async-start(s8[9437184]{0:T(1024)(128)(4,1)} %bitcast.64), calls=%async_computation.2 | async-start | bytes 8388608
  76.8 5.1 %slice-start.7 = ((s8[4718592]{0:T(1024)(128)(4,1)}), s8[524288]{0:T(1024)(128)(4,1)S(1)}, s32[]{:S(2)}) async-start(s8[4718592]{0:T(1024)(128)(4,1)} %bitcast.68), calls=%async_computation.8 | async-start | bytes 1048576
  78.1 3.9 %slice-start.2 = ((s8[9437184]{0:T(1024)(128)(4,1)}), s8[1048576]{0:T(1024)(128)(4,1)S(1)}, s32[]{:S(2)}) async-start(s8[9437184]{0:T(1024)(128)(4,1)} %bitcast.64), calls=%async_computation.3 | async-start | bytes 2097152
  168.9 9.8 %slice-start.3 = ((s8[9437184]{0:T(1024)(128)(4,1)}), s8[4194304]{0:T(1024)(128)(4,1)S(1)}, s32[]{:S(2)}) async-start(s8[9437184]{0:T(1024)(128)(4,1)} %bitcast.66), calls=%async_computation.4 | async-start | bytes 8388608
  170.1 8.6 %slice-start.8 = ((s8[4718592]{0:T(1024)(128)(4,1)}), s8[4194304]{0:T(1024)(128)(4,1)S(1)}, s32[]{:S(2)}) async-start(s8[4718592]{0:T(1024)(128)(4,1)} %bitcast.70), calls=%async_computation.9 | async-start | bytes 8388608
  171.4 7.4 %slice-start.4 = ((s8[9437184]{0:T(1024)(128)(4,1)}), s8[4194304]{0:T(1024)(128)(4,1)S(1)}, s32[]{:S(2)}) async-start(s8[9437184]{0:T(1024)(128)(4,1)} %bitcast.66), calls=%async_computation.5 | async-start | bytes 8388608
  173.8 5.0 %slice-start.9 = ((s8[4718592]{0:T(1024)(128)(4,1)}), s8[524288]{0:T(1024)(128)(4,1)S(1)}, s32[]{:S(2)}) async-start(s8[4718592]{0:T(1024)(128)(4,1)} %bitcast.70), calls=%async_computation.10 | async-start | bytes 1048576
  175.0 3.8 %slice-start.5 = ((s8[9437184]{0:T(1024)(128)(4,1)}), s8[1048576]{0:T(1024)(128)(4,1)S(1)}, s32[]{:S(2)}) async-start(s8[9437184]{0:T(1024)(128)(4,1)} %bitcast.66), calls=%async_computation.6 | async-start | bytes 2097152
  205.0 23.1 %copy-start.2 = (f32[12,32,256]{2,1,0:T(8,128)}, f32[12,32,256]{2,1,0:T(8,128)S(1)}, u32[]{:S(2)}) copy-start(f32[12,32,256]{2,1,0:T(8,128)S(1)} %div.17) | copy-start | bytes 1179652
  228.2 51.5 %copy-start.4 = (f32[72,2048]{1,0:T(8,128)S(1)}, f32[72,2048]{1,0:T(8,128)}, u32[]{:S(2)}) copy-start(f32[72,2048]{1,0:T(8,128)} %get-tuple-element.26) | copy-start | bytes 1769476
  241.5 39.0 %copy-start.3 = (f32[72,2048]{1,0:T(8,128)S(1)}, f32[72,2048]{1,0:T(8,128)}, u32[]{:S(2)}) copy-start(f32[72,2048]{1,0:T(8,128)} %get-tuple-element.27) | copy-start | bytes 1769476
  281.3 4.9 %copy-start.1 = (f32[12,32,256]{2,1,0:T(8,128)S(1)}, f32[12,32,256]{2,1,0:T(8,128)}, u32[]{:S(2)}) copy-start(f32[12,32,256]{2,1,0:T(8,128)} %param.7) | copy-start | bytes 1179652
Sparse Core Ops, SparseCore 0:
  228.3 51.3 all-gather.1

commit v5 on v4

--- a/solution.py
+++ b/solution.py
@@ -265,6 +265,46 @@
     )(x, momentum, master)
 
 
+def _orthonormal_kernel(l_ref, o_ref):
+    rank = l_ref.shape[1]
+    hi = lax.Precision.HIGHEST
+    eye = lax.broadcasted_iota(jnp.int32, (rank, rank), 0) == lax.broadcasted_iota(
+        jnp.int32, (rank, rank), 1)
+
+    def gram(x):
+        return lax.dot_general(x, x, (((1,), (1,)), ((), ())), precision=hi,
+                               preferred_element_type=jnp.float32)
+
+    def body(k, carry):
+        x = l_ref[k]
+        g = gram(x)
+        sum_squares = jnp.sum(jnp.where(eye, g, 0.0), keepdims=True)
+        scale = lax.rsqrt(sum_squares + NORM_EPSILON)
+        x = x * scale
+        g = g * (scale * scale)
+        for iteration in range(NS_STEPS):
+            if iteration > 0:
+                g = gram(x)
+            x = 1.5 * x - 0.5 * jnp.dot(g, x, precision=hi, preferred_element_type=jnp.float32)
+        o_ref[k] = x
+        return carry
+
+    lax.fori_loop(0, l_ref.shape[0], body, 0)
+
+
+def orthonormal_kernel(factor):
+    mats, rank, width = factor.shape
+    vmem = pl.BlockSpec(memory_space=pltpu.VMEM)
+    return pl.pallas_call(
+        _orthonormal_kernel,
+        out_shape=jax.ShapeDtypeStruct(factor.shape, jnp.float32),
+        in_specs=[vmem],
+        out_specs=vmem,
+        cost_estimate=pl.CostEstimate(flops=mats * NS_STEPS * 4 * rank * rank * width * 6,
+                                      bytes_accessed=2 * 4 * factor.size, transcendentals=mats),
+    )(factor)
+
+
 def split_levels(name, size, inner):
     if size % inner or size == inner:
         return ((name, size, 1),)
@@ -303,7 +343,7 @@
             "kdf,krf->krd", corrected, current, precision=lax.Precision.HIGHEST
         )
         summed = allreduce(partial_factor, both, 0)
-        ortho_basis = orthonormal(summed, local_gram)
+        ortho_basis = orthonormal_kernel(summed)
         partial_query = jnp.einsum(
             "kdf,krd->krf", corrected, ortho_basis, precision=lax.Precision.HIGHEST
         )

time: 298 us -> 343 us (1.15); the launches traced: 293 us -> 342 us
  Pallas kernels: 146 us -> 208 us
  matrix products: 75.3 us -> 61.5 us
    pallas_call x0 -> x2, Pallas kernels: none -> 62.4 us  [orthonormal_kernel(): pl.pallas_call(_orthonormal_kernel, out_shape=jax.ShapeDtypeStruct(factor...]
    dot_general x20 -> x0, matrix products: 24.7 us -> none  [the longest x10 12.5 us: orthonormal(): jnp.einsum('krs,ksd->krd', gram_now, ortho_basis, precision=lax.Precision...]
    dot_general x2, matrix products: 12 us -> 22.9 us  [local(): jnp.einsum('kdf,krd->krf', corrected, ortho_basis, precision=lax.Precisio...]
    unnamed x33 -> x13, local copies, waits for them, and re-layouts: 7.5 us -> 7.39 us
  transfers between devices with their start and end apart: 1 -> 1, of which waited for: 1 -> 1; matrix products, arithmetic and copies ran while one was open for 5% -> 4% of each run, Pallas kernels for 0% -> 0%
where the time goes in v5:
time: 343 us; the launch traced here: 342 us
  Pallas kernels  208 us (61%)
  matrix products  61.5 us (18%)
  waiting for transfers between devices  38.1 us (11%)
  local copies, waits for them, and re-layouts  17.9 us (5%)
  between operations  14.2 us (4%)
    pallas_call x4, Pallas kernels, allreduce(): pl.pallas_call(functools.partial(_allreduce_kernel, tuple(levels)), out_s...  125 us
    pallas_call x2, Pallas kernels, orthonormal_kernel(): pl.pallas_call(_orthonormal_kernel, out_shape=jax.ShapeDtypeStruct(factor...  62.4 us
    all_gather x1, waiting for transfers between devices, local(): weight_rows = lax.all_gather(by_columns, 'rep', axis=0, tiled=True)  38.1 us
    dot_general x2, matrix products, local(): jnp.einsum('kdf,krf->krd', corrected, current, precision=lax.Precision.HI...  23.8 us
    dot_general x2, matrix products, local(): jnp.einsum('kdf,krd->krf', corrected, ortho_basis, precision=lax.Precisio...  22.9 us
    pallas_call x1, Pallas kernels, flat_update(): pl.pallas_call(_update_kernel, out_shape=(jax.ShapeDtypeStruct(momentum.s...  20.8 us
    dot_general x1, matrix products, local(): jnp.einsum('krd,krf->kdf', ortho_basis, current, precision=lax.Precision....  13.4 us
    unnamed x13, local copies, waits for them, and re-layouts  7.39 us
  transfers between devices with their start and end apart: 1, of which 1 were waited for; matrix products, arithmetic and copies ran while one was open for 4% of the time, Pallas kernels for 0%

profile of v5, /device:TPU:1, one launch (start us, length us, event | category | flops | bytes accessed | tf_op | source)
XLA Modules:
  0.0 342.3 jit_solution(13361449162550970356)
XLA Ops:
  7.2 0.0 copy-start
  7.2 0.0 all-gather.2.cloned.1.call-start
  7.3 0.9 copy-done
  8.2 12.1 %fusion.9 = f32[12,32,768]{2,1,0:T(8,128)S(1)} fusion(f32[12,32,256]{2,1,0:T(8,128)S(1)} %copy-done, f32[1,12,768,256]{3,2,1,0:T(8,128)} %param.6, bf16[1,12,768,256]{3,2,1,0:T(8,128)(2,1)} %param.5), kind=kOutput, calls=%fused_computation.11 | convolution fusion | flops 910688256 | bytes 15728640 | tf_op jit(solution)/shard_map/kdf,krf->krd/dot_general | solution.py:342
  20.3 1.4 reshape.48.x_ref
  21.7 45.8 %shard_map.92 = f32[2,4,4,4,18,128]{5,4,3,2,1,0:T(8,128)} custom-call(f32[2,4,4,4,18,128]{5,4,3,2,1,0:T(8,128)} %reshape.48.x_ref), custom_call_target="tpu_custom_call" | custom-call | flops 589824 | bytes 4718592 | tf_op jit(solution)/shard_map/pallas_call | solution.py:163
  67.5 2.5 reshape.49.l_ref
  70.1 31.2 %shard_map.93 = f32[12,32,768]{2,1,0:T(8,128)} custom-call(f32[12,32,768]{2,1,0:T(8,128)} %reshape.49.l_ref), custom_call_target="tpu_custom_call" | custom-call | flops 1132462080 | bytes 2359296 | tf_op jit(solution)/shard_map/pallas_call | solution.py:298
  101.3 11.4 %fusion.4 = f32[12,32,256]{2,1,0:T(8,128)S(1)} fusion(f32[12,32,768]{2,1,0:T(8,128)} %shard_map.93, f32[1,12,768,256]{3,2,1,0:T(8,128)} %param.6, bf16[1,12,768,256]{3,2,1,0:T(8,128)(2,1)} %param.5), kind=kOutput, calls=%fused_computation.5 | convolution fusion | flops 910688256 | bytes 15728640 | tf_op jit(solution)/shard_map/kdf,krd->krf/dot_general | solution.py:347
  112.7 0.8 reshape.50.x_ref
  113.5 18.5 %shard_map.94 = f32[16,48,128]{2,1,0:T(8,128)} custom-call(f32[16,48,128]{2,1,0:T(8,128)} %reshape.50.x_ref), custom_call_target="tpu_custom_call" | custom-call | flops 196608 | bytes 1572864 | tf_op jit(solution)/shard_map/pallas_call | solution.py:163
  132.0 1.0 broadcast_multiply_fusion.1
  133.0 0.1 div.15
  133.1 11.7 %fusion.2 = f32[12,32,768]{2,1,0:T(8,128)S(1)} fusion(f32[12,32,256]{2,1,0:T(8,128)S(1)} %div.15, f32[1,12,768,256]{3,2,1,0:T(8,128)} %param.6, bf16[1,12,768,256]{3,2,1,0:T(8,128)(2,1)} %param.5), kind=kOutput, calls=%fused_computation.3 | convolution fusion | flops 910688256 | bytes 15728640 | tf_op jit(solution)/shard_map/kdf,krf->krd/dot_general | solution.py:342
  144.8 1.4 reshape.51.x_ref
  146.2 42.7 %shard_map.95 = f32[2,4,4,4,18,128]{5,4,3,2,1,0:T(8,128)} custom-call(f32[2,4,4,4,18,128]{5,4,3,2,1,0:T(8,128)} %reshape.51.x_ref), custom_call_target="tpu_custom_call" | custom-call | flops 589824 | bytes 4718592 | tf_op jit(solution)/shard_map/pallas_call | solution.py:163
  189.0 2.5 reshape.52.l_ref
  191.5 31.2 %shard_map.96 = f32[12,32,768]{2,1,0:T(8,128)} custom-call(f32[12,32,768]{2,1,0:T(8,128)} %reshape.52.l_ref), custom_call_target="tpu_custom_call" | custom-call | flops 1132462080 | bytes 2359296 | tf_op jit(solution)/shard_map/pallas_call | solution.py:298
  222.7 0.0 copy-start.1
  222.7 11.5 %fusion = f32[12,32,256]{2,1,0:T(8,128)S(1)} fusion(f32[12,32,768]{2,1,0:T(8,128)} %shard_map.96, f32[1,12,768,256]{3,2,1,0:T(8,128)} %param.6, bf16[1,12,768,256]{3,2,1,0:T(8,128)(2,1)} %param.5), kind=kOutput, calls=%fused_computation.1 | convolution fusion | flops 910688256 | bytes 15728640 | tf_op jit(solution)/shard_map/kdf,krd->krf/dot_general | solution.py:347
  234.2 0.8 reshape.53.x_ref
  234.9 18.3 %shard_map.97 = f32[16,48,128]{2,1,0:T(8,128)} custom-call(f32[16,48,128]{2,1,0:T(8,128)} %reshape.53.x_ref), custom_call_target="tpu_custom_call" | custom-call | flops 196608 | bytes 1572864 | tf_op jit(solution)/shard_map/pallas_call | solution.py:163
  253.2 1.0 broadcast_multiply_fusion
  254.2 0.1 div.17
  254.4 0.0 copy-start.2
  254.4 0.0 copy-done.1
  254.4 1.4 fusion.12
  255.8 0.9 constant_dynamic-slice_fusion
  256.7 20.8 %shard_map.98 = (f32[72,2048]{1,0:T(8,128)}, f32[72,2048]{1,0:T(8,128)}, bf16[8,72,256]{2,1,0:T(8,128)(2,1)}) custom-call(f32[8,72,256]{2,1,0:T(8,128)} %bitcast.30, f32[72,2048]{1,0:T(8,128)} %mom_ref.1, f32[72,2048]{1,0:T(8,128)} %master_ref.1), custom_call_target="tpu_custom_call" | custom-call | flops 589824 | bytes 2949120 | tf_op jit(solution)/shard_map/pallas_call | solution.py:244
  277.5 0.0 all-gather.2.cloned.1.call-update
  277.5 0.0 copy-start.4
  277.5 0.0 copy-start.3
  277.5 13.4 %fusion.8 = f32[1,12,768,256]{3,2,1,0:T(8,128)} fusion(f32[12,32,768]{2,1,0:T(8,128)S(1)} %copy-done.1, f32[12,32,256]{2,1,0:T(8,128)S(1)} %div.17, f32[1,12,768,256]{3,2,1,0:T(8,128)} %param.6, bf16[1,12,768,256]{3,2,1,0:T(8,128)(2,1)} %param.5), kind=kOutput, calls=%fused_computation.9 | convolution fusion | flops 913047552 | bytes 25165824 | tf_op jit(solution)/shard_map/krd,krf->kdf/dot_general | solution.py:351
  290.9 0.0 copy-done.2
  290.9 38.1 %all-gather.2.cloned.1.call-done = bf16[9216,256]{1,0:T(8,128)(2,1)} async-done(((bf16[576,256]{1,0:T(8,128)(2,1)}), bf16[9216,256]{1,0:T(8,128)(2,1)}) %all-gather.2.cloned.1.call-update) | async-done | bytes 4718608 | tf_op jit(solution)/shard_map/all_gather | solution.py:370
  329.0 0.0 copy-done.4
  329.0 0.8 copy.13
  329.8 0.0 copy-done.3
  329.8 0.8 copy.14
  330.6 4.8 %copy.15 = bf16[12,768,256]{2,1,0:T(8,128)(2,1)} copy(bf16[12,768,256]{2,1,0:T(8,128)(2,1)} %bitcast.28) | data formatting | bytes 9437184
Async XLA Ops:
  7.2 1.0 copy-start
  7.2 321.8 %all-gather.2.cloned.1.call-start = ((), (), s32[]{:S(2)}) async-start(), calls=%async_computation | async-start | bytes 5013504 | tf_op jit(solution)/shard_map/all_gather | solution.py:370
  222.7 31.7 %copy-start.1 = (f32[12,32,768]{2,1,0:T(8,128)S(1)}, f32[12,32,768]{2,1,0:T(8,128)}, u32[]{:S(2)}) copy-start(f32[12,32,768]{2,1,0:T(8,128)} %shard_map.96) | copy-start | bytes 3538948
  254.4 36.5 %copy-start.2 = (f32[12,32,256]{2,1,0:T(8,128)}, f32[12,32,256]{2,1,0:T(8,128)S(1)}, u32[]{:S(2)}) copy-start(f32[12,32,256]{2,1,0:T(8,128)S(1)} %div.17) | copy-start | bytes 1179652
  277.5 51.5 %copy-start.4 = (f32[72,2048]{1,0:T(8,128)S(1)}, f32[72,2048]{1,0:T(8,128)}, u32[]{:S(2)}) copy-start(f32[72,2048]{1,0:T(8,128)} %get-tuple-element.18) | copy-start | bytes 1769476
  277.5 52.3 %copy-start.3 = (f32[72,2048]{1,0:T(8,128)S(1)}, f32[72,2048]{1,0:T(8,128)}, u32[]{:S(2)}) copy-start(f32[72,2048]{1,0:T(8,128)} %get-tuple-element.19) | copy-start | bytes 1769476
Sparse Core Ops, SparseCore 0:
  277.6 51.3 all-gather.1

commit v6 on v4

--- a/solution.py
+++ b/solution.py
@@ -172,8 +172,8 @@
     return out.reshape(shape)
 
 
-def _update_kernel(x_ref, mom_ref, master_ref, mom_out, master_out, cols_out,
-                   rows_buf, work_buf, send1, recv1, send2, recv2, local_sem):
+def _update_kernel(x_ref, mom_ref, master_ref, mom_out, master_out,
+                   rows_buf, send1, recv1, local_sem):
     n, rows, cols = x_ref.shape
     me = lax.axis_index("tp")
     barrier = pltpu.get_barrier_semaphore()
@@ -211,28 +211,60 @@
     new_master = master_ref[...] - LEARNING_RATE * new_mom
     mom_out[...] = new_mom
     master_out[...] = new_master
-    work_buf[...] = new_master.astype(work_buf.dtype)
+
+
+def _columns_kernel(x_ref, cols_out, send, recv, local_sem):
+    n, rows, cols = cols_out.shape
+    me = lax.axis_index("tp")
+    barrier = pltpu.get_barrier_semaphore()
+    for off in range(1, n):
+        j = lax.rem(me + off, n)
+        pl.semaphore_signal(barrier, inc=1, device_id=_peer(("tp", n, 1), j),
+                            device_id_type=pl.DeviceIdType.MESH)
+    pl.semaphore_wait(barrier, n - 1)
+
+    def block(j):
+        return x_ref.at[:, pl.ds(pl.multiple_of(j * cols, cols), cols)]
 
     copies = []
     for off in range(1, n):
         j = lax.rem(me + off, n)
         cp = pltpu.make_async_remote_copy(
-            src_ref=work_buf.at[:, pl.ds(pl.multiple_of(j * cols, cols), cols)], dst_ref=cols_out.at[me],
-            send_sem=send2.at[j], recv_sem=recv2.at[me],
+            src_ref=block(j), dst_ref=cols_out.at[me],
+            send_sem=send.at[j], recv_sem=recv.at[me],
             device_id=_peer(("tp", n, 1), j), device_id_type=pl.DeviceIdType.MESH)
         cp.start()
         copies.append((j, cp))
-    own = pltpu.make_async_copy(
-        work_buf.at[:, pl.ds(pl.multiple_of(me * cols, cols), cols)], cols_out.at[me], local_sem.at[0])
+    own = pltpu.make_async_copy(block(me), cols_out.at[me], local_sem.at[0])
     own.start()
     own.wait()
     for j, cp in copies:
         pltpu.make_async_remote_copy(
-            src_ref=work_buf.at[:, pl.ds(pl.multiple_of(j * cols, cols), cols)], dst_ref=cols_out.at[j],
-            send_sem=send2.at[j], recv_sem=recv2.at[j],
+            src_ref=block(j), dst_ref=cols_out.at[j],
+            send_sem=send.at[j], recv_sem=recv.at[j],
             device_id=_peer(("tp", n, 1), j), device_id_type=pl.DeviceIdType.MESH).wait_recv()
     for j, cp in copies:
         cp.wait_send()
+
+
+def by_columns(x, n, collective_id):
+    rows, width = x.shape
+    cols = width // n
+    vmem = pl.BlockSpec(memory_space=pltpu.VMEM)
+    return pl.pallas_call(
+        _columns_kernel,
+        out_shape=jax.ShapeDtypeStruct((n, rows, cols), x.dtype),
+        in_specs=[vmem],
+        out_specs=vmem,
+        scratch_shapes=[
+            pltpu.SemaphoreType.DMA((n,)),
+            pltpu.SemaphoreType.DMA((n,)),
+            pltpu.SemaphoreType.DMA((1,)),
+        ],
+        compiler_params=pltpu.CompilerParams(collective_id=collective_id, has_side_effects=True),
+        cost_estimate=pl.CostEstimate(flops=0, bytes_accessed=2 * x.size * x.dtype.itemsize,
+                                      transcendentals=0),
+    )(x)
 
 
 def flat_update(own_block, momentum, master, n, collective_id):
@@ -246,15 +278,11 @@
         out_shape=(
             jax.ShapeDtypeStruct(momentum.shape, f32),
             jax.ShapeDtypeStruct(master.shape, f32),
-            jax.ShapeDtypeStruct((n, rows, cols), jnp.bfloat16),
         ),
         in_specs=[vmem, vmem, vmem],
-        out_specs=(vmem, vmem, vmem),
+        out_specs=(vmem, vmem),
         scratch_shapes=[
             pltpu.VMEM((rows, n * cols), f32),
-            pltpu.VMEM((rows, n * cols), jnp.bfloat16),
-            pltpu.SemaphoreType.DMA((n,)),
-            pltpu.SemaphoreType.DMA((n,)),
             pltpu.SemaphoreType.DMA((n,)),
             pltpu.SemaphoreType.DMA((n,)),
             pltpu.SemaphoreType.DMA((1,)),
@@ -296,6 +324,11 @@
     corrected = grads[0].astype(jnp.float32) + error[0]
     current = query
     replicas = lax.axis_size("rep")
+    tensor = lax.axis_size("tp")
+    kept = master - LEARNING_RATE * (MOMENTUM_DECAY * momentum)
+    kept_cols = by_columns(kept, tensor, 3)
+    kept_cols = kept_cols.reshape(-1, kept_cols.shape[-1])
+    kept_all = lax.all_gather(kept_cols, "rep", axis=0, tiled=True)
     rep_only = (("rep", replicas, 1),)
     both = split_levels("tp", lax.axis_size("tp"), 2) + split_levels("rep", replicas, 4)
     for power_pass in range(ROUNDS):
@@ -311,6 +344,7 @@
     approx = jnp.einsum("krd,krf->kdf", ortho_basis, current, precision=lax.Precision.HIGHEST)
     new_error = (corrected - approx)[None]
     matrices, model_width, shard_cols = approx.shape
+    weights = (kept_all.reshape(approx.shape) - LEARNING_RATE * approx).astype(jnp.bfloat16)
     block_rows = matrices * model_width // replicas
     span = min(matrices, -(-block_rows // model_width) + 1)
     first_row = lax.axis_index("rep") * block_rows
@@ -324,11 +358,7 @@
     own_block = lax.dynamic_slice_in_dim(
         pair, first_row - first_mat * model_width, block_rows, 0
     )
-    new_momentum, new_master, by_columns = flat_update(
-        own_block, momentum, master, lax.axis_size("tp"), 2)
-    by_columns = by_columns.reshape(block_rows, shard_cols)
-    weight_rows = lax.all_gather(by_columns, "rep", axis=0, tiled=True)
-    weights = weight_rows.reshape(matrices, model_width, shard_cols)
+    new_momentum, new_master = flat_update(own_block, momentum, master, tensor, 2)
     return (new_error, current, new_momentum, new_master, weights)
 
 

time: 298 us -> 270 us (0.906)
  waiting for transfers between devices: 38.2 us -> 0.04 us
  Pallas kernels: 146 us -> 154 us
  local copies, waits for them, and re-layouts: 16.8 us -> 11.5 us
  matrix products: 75.3 us -> 80.3 us
    all_gather x1, waiting for transfers between devices: 38.2 us -> 0.02 us  [local(): kept_all = lax.all_gather(kept_cols, 'rep', axis=0, tiled=True)]
    pallas_call x0 -> x1, Pallas kernels: none -> 14.4 us  [by_columns(): pl.pallas_call(_columns_kernel, out_shape=jax.ShapeDtypeStruct((n, rows,...]
    pallas_call x1, Pallas kernels: 20.8 us -> 15 us  [flat_update(): pl.pallas_call(_update_kernel, out_shape=(jax.ShapeDtypeStruct(momentum.s...]
    unnamed x33 -> x32, local copies, waits for them, and re-layouts: 7.5 us -> 2.18 us
    dot_general x1, matrix products: 13.3 us -> 18.3 us  [local(): jnp.einsum('krd,krf->kdf', ortho_basis, current, precision=lax.Precision....]
  transfers between devices with their start and end apart: 1 -> 1, of which waited for: 1 -> 0; matrix products, arithmetic and copies ran while one was open for 5% -> 28% of each run, Pallas kernels for 0% -> 53%
where the time goes in v6:
time: 270 us; the launch traced here: 265 us
  Pallas kernels  154 us (57%)
  matrix products  80.3 us (30%)
  between operations  14.7 us (5%)
  local copies, waits for them, and re-layouts  11.5 us (4%)
  other arithmetic  4.24 us (2%)
    pallas_call x4, Pallas kernels, allreduce(): pl.pallas_call(functools.partial(_allreduce_kernel, tuple(levels)), out_s...  125 us
    dot_general x2, matrix products, local(): jnp.einsum('kdf,krf->krd', corrected, current, precision=lax.Precision.HI...  23.8 us
    dot_general x1, matrix products, local(): jnp.einsum('krd,krf->kdf', ortho_basis, current, precision=lax.Precision....  18.3 us
    pallas_call x1, Pallas kernels, flat_update(): pl.pallas_call(_update_kernel, out_shape=(jax.ShapeDtypeStruct(momentum.s...  15 us
    pallas_call x1, Pallas kernels, by_columns(): pl.pallas_call(_columns_kernel, out_shape=jax.ShapeDtypeStruct((n, rows,...  14.4 us
    dot_general x10, matrix products, orthonormal(): jnp.einsum('krs,ksd->krd', gram_now, ortho_basis, precision=lax.Precision...  12.5 us
    dot_general x10, matrix products, local_gram(): jnp.einsum('krd,ksd->krs', factor, factor, precision=lax.Precision.HIGHEST)  12.2 us
    dot_general x2, matrix products, local(): jnp.einsum('kdf,krd->krf', corrected, ortho_basis, precision=lax.Precisio...  12 us
  transfers between devices with their start and end apart: 1, of which 0 were waited for; matrix products, arithmetic and copies ran while one was open for 28% of the time, Pallas kernels for 53%

profile of v6, /device:TPU:1, one launch (start us, length us, event | category | flops | bytes accessed | tf_op | source)
XLA Modules:
  0.0 265.3 jit_solution(7637549606460195647)
XLA Ops:
  7.2 0.0 all-gather.2.cloned.1.call-start
  7.2 2.2 multiply_subtract_fusion.x_ref
  9.4 14.4 %shard_map.97 = f32[8,72,256]{2,1,0:T(8,128)} custom-call(f32[72,2048]{1,0:T(8,128)} %multiply_subtract_fusion.x_ref), custom_call_target="tpu_custom_call" | custom-call | bytes 1179648 | tf_op jit(solution)/shard_map/pallas_call | solution.py:254
  23.8 12.2 %fusion.9 = f32[12,32,768]{2,1,0:T(8,128)S(1)} fusion(f32[12,32,256]{2,1,0:T(8,128)S(1)} %copy-done, f32[1,12,768,256]{3,2,1,0:T(8,128)} %param.6, bf16[1,12,768,256]{3,2,1,0:T(8,128)(2,1)} %param.5), kind=kOutput, calls=%fused_computation.12 | convolution fusion | flops 910688256 | bytes 15728640 | tf_op jit(solution)/shard_map/kdf,krf->krd/dot_general | solution.py:335
  36.0 1.4 reshape.68.x_ref
  37.4 45.1 %shard_map.92 = f32[2,4,4,4,18,128]{5,4,3,2,1,0:T(8,128)} custom-call(f32[2,4,4,4,18,128]{5,4,3,2,1,0:T(8,128)} %reshape.68.x_ref), custom_call_target="tpu_custom_call" | custom-call | flops 589824 | bytes 4718592 | tf_op jit(solution)/shard_map/pallas_call | solution.py:163
  82.6 1.8 reshape.69
  84.4 1.3 select_reduce_fusion.1
  85.7 1.3 fusion.21
  87.0 1.2 fusion.36
  88.2 1.2 fusion.20
  89.5 1.2 fusion.37
  90.7 1.2 fusion.19
  91.9 1.2 fusion.38
  93.1 1.2 fusion.18
  94.3 1.2 fusion.39
  95.5 1.4 fusion.17
  97.0 6.0 %fusion.4 = f32[12,32,256]{2,1,0:T(8,128)S(1)} fusion(f32[12,32,768]{2,1,0:T(8,128)S(1)} %fusion.17, f32[1,12,768,256]{3,2,1,0:T(8,128)S(1)} %bitcast.65, bf16[1,12,768,256]{3,2,1,0:T(8,128)(2,1)S(1)} %bitcast.69), kind=kOutput, calls=%fused_computation.5 | convolution fusion | flops 910688256 | bytes 15728640 | tf_op jit(solution)/shard_map/kdf,krd->krf/dot_general | solution.py:340
  103.0 0.8 reshape.70.x_ref
  103.7 18.8 %shard_map.93 = f32[16,48,128]{2,1,0:T(8,128)} custom-call(f32[16,48,128]{2,1,0:T(8,128)} %reshape.70.x_ref), custom_call_target="tpu_custom_call" | custom-call | flops 196608 | bytes 1572864 | tf_op jit(solution)/shard_map/pallas_call | solution.py:163
  122.6 1.0 broadcast_multiply_fusion.1
  123.6 0.1 div.15
  123.7 11.7 %fusion.2 = f32[12,32,768]{2,1,0:T(8,128)S(1)} fusion(f32[12,32,256]{2,1,0:T(8,128)S(1)} %div.15, f32[1,12,768,256]{3,2,1,0:T(8,128)} %param.6, bf16[1,12,768,256]{3,2,1,0:T(8,128)(2,1)} %param.5), kind=kOutput, calls=%fused_computation.3 | convolution fusion | flops 910688256 | bytes 15728640 | tf_op jit(solution)/shard_map/kdf,krf->krd/dot_general | solution.py:335
  135.4 1.4 reshape.71.x_ref
  136.8 42.7 %shard_map.94 = f32[2,4,4,4,18,128]{5,4,3,2,1,0:T(8,128)} custom-call(f32[2,4,4,4,18,128]{5,4,3,2,1,0:T(8,128)} %reshape.71.x_ref), custom_call_target="tpu_custom_call" | custom-call | flops 589824 | bytes 4718592 | tf_op jit(solution)/shard_map/pallas_call | solution.py:163
  179.5 2.0 reshape.72
  181.6 1.3 select_reduce_fusion
  182.9 1.3 fusion.16
  184.2 1.2 fusion.40
  185.4 1.2 fusion.15
  186.7 1.2 fusion.41
  187.9 1.2 fusion.14
  189.1 1.2 fusion.42
  190.3 1.2 fusion.13
  191.5 1.2 fusion.43
  192.7 1.4 fusion.12
  194.1 6.0 %fusion = f32[12,32,256]{2,1,0:T(8,128)S(1)} fusion(f32[12,32,768]{2,1,0:T(8,128)S(1)} %fusion.12, f32[1,12,768,256]{3,2,1,0:T(8,128)S(1)} %bitcast.67, bf16[1,12,768,256]{3,2,1,0:T(8,128)(2,1)S(1)} %bitcast.71), kind=kOutput, calls=%fused_computation.1 | convolution fusion | flops 910688256 | bytes 15728640 | tf_op jit(solution)/shard_map/kdf,krd->krf/dot_general | solution.py:340
  200.1 0.8 reshape.73.x_ref
  200.9 18.3 %shard_map.95 = f32[16,48,128]{2,1,0:T(8,128)} custom-call(f32[16,48,128]{2,1,0:T(8,128)} %reshape.73.x_ref), custom_call_target="tpu_custom_call" | custom-call | flops 196608 | bytes 1572864 | tf_op jit(solution)/shard_map/pallas_call | solution.py:163
  219.3 1.0 broadcast_multiply_fusion
  220.3 0.1 div.17
  220.4 1.4 fusion.26
  221.9 0.9 constant_dynamic-slice_fusion
  222.7 15.0 %shard_map.96 = (f32[72,2048]{1,0:T(8,128)}, f32[72,2048]{1,0:T(8,128)}) custom-call(f32[8,72,256]{2,1,0:T(8,128)} %bitcast.74, f32[72,2048]{1,0:T(8,128)} %mom_ref.1, f32[72,2048]{1,0:T(8,128)} %master_ref.1), custom_call_target="tpu_custom_call" | custom-call | flops 589824 | bytes 2949120 | tf_op jit(solution)/shard_map/pallas_call | solution.py:276
  237.8 18.3 %subtract_convert_fusion = (bf16[12,768,256]{2,1,0:T(8,128)(2,1)}, f32[1,12,768,256]{3,2,1,0:T(8,128)}) fusion(f32[12,768,256]{2,1,0:T(8,128)} %bitcast.72, f32[1,12,768,256]{3,2,1,0:T(8,128)} %param.6, bf16[1,12,768,256]{3,2,1,0:T(8,128)(2,1)} %param.5, f32[12,32,768]{2,1,0:T(8,128)S(1)} %fusion.12, f32[12,32,256]{2,1,0:T(8,128)S(1)} %div.17), kind=kOutput, calls=%fused_computation.10 | convolution fusion | flops 920125440 | bytes 39321600 | tf_op jit(solution)/shard_map/krd,krf->kdf/dot_general | solution.py:344
  256.2 0.8 copy.12
  257.0 0.4 copy-done.3
  257.4 0.8 copy.13
  (38 shorter events, 0.2 us)
Async XLA Ops:
  7.2 16.7 %copy-start = (f32[12,32,256]{2,1,0:T(8,128)S(1)}, f32[12,32,256]{2,1,0:T(8,128)}, u32[]{:S(2)}) copy-start(f32[12,32,256]{2,1,0:T(8,128)} %param.7) | copy-start | bytes 1179652
  7.2 230.6 %all-gather.2.cloned.1.call-start = ((), (), s32[]{:S(2)}) async-start(), calls=%async_computation | async-start | bytes 10027008 | tf_op jit(solution)/shard_map/all_gather | solution.py:331
  87.0 9.9 %slice-start = ((s8[9437184]{0:T(1024)(128)(4,1)}), s8[4194304]{0:T(1024)(128)(4,1)S(1)}, s32[]{:S(2)}) async-start(s8[9437184]{0:T(1024)(128)(4,1)} %bitcast.64), calls=%async_computation.1 | async-start | bytes 8388608
  88.2 8.7 %slice-start.6 = ((s8[4718592]{0:T(1024)(128)(4,1)}), s8[4194304]{0:T(1024)(128)(4,1)S(1)}, s32[]{:S(2)}) async-start(s8[4718592]{0:T(1024)(128)(4,1)} %bitcast.68), calls=%async_computation.7 | async-start | bytes 8388608
  89.5 7.5 %slice-start.1 = ((s8[9437184]{0:T(1024)(128)(4,1)}), s8[4194304]{0:T(1024)(128)(4,1)S(1)}, s32[]{:S(2)}) async-start(s8[9437184]{0:T(1024)(128)(4,1)} %bitcast.64), calls=%async_computation.2 | async-start | bytes 8388608
  91.9 5.1 %slice-start.7 = ((s8[4718592]{0:T(1024)(128)(4,1)}), s8[524288]{0:T(1024)(128)(4,1)S(1)}, s32[]{:S(2)}) async-start(s8[4718592]{0:T(1024)(128)(4,1)} %bitcast.68), calls=%async_computation.8 | async-start | bytes 1048576
  93.1 3.9 %slice-start.2 = ((s8[9437184]{0:T(1024)(128)(4,1)}), s8[1048576]{0:T(1024)(128)(4,1)S(1)}, s32[]{:S(2)}) async-start(s8[9437184]{0:T(1024)(128)(4,1)} %bitcast.64), calls=%async_computation.3 | async-start | bytes 2097152
  184.2 9.8 %slice-start.3 = ((s8[9437184]{0:T(1024)(128)(4,1)}), s8[4194304]{0:T(1024)(128)(4,1)S(1)}, s32[]{:S(2)}) async-start(s8[9437184]{0:T(1024)(128)(4,1)} %bitcast.66), calls=%async_computation.4 | async-start | bytes 8388608
  185.4 8.6 %slice-start.8 = ((s8[4718592]{0:T(1024)(128)(4,1)}), s8[4194304]{0:T(1024)(128)(4,1)S(1)}, s32[]{:S(2)}) async-start(s8[4718592]{0:T(1024)(128)(4,1)} %bitcast.70), calls=%async_computation.9 | async-start | bytes 8388608
  186.6 7.4 %slice-start.4 = ((s8[9437184]{0:T(1024)(128)(4,1)}), s8[4194304]{0:T(1024)(128)(4,1)S(1)}, s32[]{:S(2)}) async-start(s8[9437184]{0:T(1024)(128)(4,1)} %bitcast.66), calls=%async_computation.5 | async-start | bytes 8388608
  189.1 5.0 %slice-start.9 = ((s8[4718592]{0:T(1024)(128)(4,1)}), s8[524288]{0:T(1024)(128)(4,1)S(1)}, s32[]{:S(2)}) async-start(s8[4718592]{0:T(1024)(128)(4,1)} %bitcast.70), calls=%async_computation.10 | async-start | bytes 1048576
  190.3 3.8 %slice-start.5 = ((s8[9437184]{0:T(1024)(128)(4,1)}), s8[1048576]{0:T(1024)(128)(4,1)S(1)}, s32[]{:S(2)}) async-start(s8[9437184]{0:T(1024)(128)(4,1)} %bitcast.66), calls=%async_computation.6 | async-start | bytes 2097152
  220.4 17.4 %copy-start.2 = (f32[12,32,256]{2,1,0:T(8,128)}, f32[12,32,256]{2,1,0:T(8,128)S(1)}, u32[]{:S(2)}) copy-start(f32[12,32,256]{2,1,0:T(8,128)S(1)} %div.17) | copy-start | bytes 1179652
  237.8 18.3 %copy-start.4 = (f32[72,2048]{1,0:T(8,128)S(1)}, f32[72,2048]{1,0:T(8,128)}, u32[]{:S(2)}) copy-start(f32[72,2048]{1,0:T(8,128)} %get-tuple-element.26) | copy-start | bytes 1769476
  256.1 1.3 copy-start.3
  256.1 2.1 copy-start.1
Sparse Core Ops, SparseCore 0:
  23.9 78.3 all-gather.1

commit v7 on v6

--- a/solution.py
+++ b/solution.py
@@ -301,6 +301,24 @@
     return ((name, size // inner, inner), (name, inner, 1))
 
 
+def orthonormal_by_gram(factor):
+    hi = lax.Precision.HIGHEST
+    gram_now = local_gram(factor)
+    rank = factor.shape[1]
+    eye = jnp.eye(rank, dtype=factor.dtype)
+    sum_squares = jnp.trace(gram_now, axis1=1, axis2=2)[:, None, None]
+    factor_scale = lax.rsqrt(sum_squares + NORM_EPSILON)
+    gram_now = gram_now * (factor_scale * factor_scale)
+    mixing = None
+    for iteration in range(NS_STEPS):
+        step = 1.5 * eye - 0.5 * gram_now
+        mixing = step if mixing is None else jnp.einsum("krs,kst->krt", step, mixing, precision=hi)
+        if iteration < NS_STEPS - 1:
+            gram_now = jnp.einsum(
+                "krs,kst,kut->kru", step, gram_now, step, precision=hi)
+    return jnp.einsum("krs,ksd->krd", mixing * factor_scale, factor, precision=hi)
+
+
 def local_gram(factor):
     return jnp.einsum("krd,ksd->krs", factor, factor, precision=lax.Precision.HIGHEST)
 
@@ -336,7 +354,7 @@
             "kdf,krf->krd", corrected, current, precision=lax.Precision.HIGHEST
         )
         summed = allreduce(partial_factor, both, 0)
-        ortho_basis = orthonormal(summed, local_gram)
+        ortho_basis = orthonormal_by_gram(summed)
         partial_query = jnp.einsum(
             "kdf,krd->krf", corrected, ortho_basis, precision=lax.Precision.HIGHEST
         )

time: 270 us -> 260 us (0.963); the launches traced: 265 us -> 260 us
  matrix products: 80.3 us -> 75.5 us
    dot_general x10 -> x2, matrix products: 12.2 us -> 2.61 us  [local_gram(): jnp.einsum('krd,ksd->krs', factor, factor, precision=lax.Precision.HIGHEST)]
    dot_general x2, matrix products: 12 us -> 17.1 us  [local(): jnp.einsum('kdf,krd->krf', corrected, ortho_basis, precision=lax.Precisio...]
    dot_general x10 -> x26, matrix products: 12.5 us -> 11.8 us  [the longest x16 6.9 us: orthonormal_by_gram(): jnp.einsum('krs,kst,kut->kru', step, gram_now, step, precision=hi)]
  transfers between devices with their start and end apart: 1 -> 1, of which waited for: 0 -> 0; matrix products, arithmetic and copies ran while one was open for 28% -> 26% of each run, Pallas kernels for 53% -> 54%
where the time goes in v7:
time: 260 us
  Pallas kernels  155 us (60%)
  matrix products  75.5 us (29%)
  between operations  14.6 us (6%)
  local copies, waits for them, and re-layouts  10.8 us (4%)
  other arithmetic  4.25 us (2%)
    pallas_call x4, Pallas kernels, allreduce(): pl.pallas_call(functools.partial(_allreduce_kernel, tuple(levels)), out_s...  125 us
    dot_general x2, matrix products, local(): jnp.einsum('kdf,krf->krd', corrected, current, precision=lax.Precision.HI...  23.8 us
    dot_general x1, matrix products, local(): jnp.einsum('krd,krf->kdf', ortho_basis, current, precision=lax.Precision....  18.7 us
    dot_general x2, matrix products, local(): jnp.einsum('kdf,krd->krf', corrected, ortho_basis, precision=lax.Precisio...  17.1 us
    pallas_call x1, Pallas kernels, flat_update(): pl.pallas_call(_update_kernel, out_shape=(jax.ShapeDtypeStruct(momentum.s...  15 us
    pallas_call x1, Pallas kernels, by_columns(): pl.pallas_call(_columns_kernel, out_shape=jax.ShapeDtypeStruct((n, rows,...  14.4 us
    dot_general x16, matrix products, orthonormal_by_gram(): jnp.einsum('krs,kst,kut->kru', step, gram_now, step, precision=hi)  6.9 us
  transfers between devices with their start and end apart: 1, of which 0 were waited for; matrix products, arithmetic and copies ran while one was open for 26% of the time, Pallas kernels for 54%

profile of v7, /device:TPU:1, one launch (start us, length us, event | category | flops | bytes accessed | tf_op | source)
XLA Modules:
  0.0 259.6 jit_solution(11513388540100129123)
XLA Ops:
  7.2 2.2 multiply_subtract_fusion.x_ref
  9.4 14.4 %shard_map.97 = f32[8,72,256]{2,1,0:T(8,128)} custom-call(f32[72,2048]{1,0:T(8,128)} %multiply_subtract_fusion.x_ref), custom_call_target="tpu_custom_call" | custom-call | bytes 1179648 | tf_op jit(solution)/shard_map/pallas_call | solution.py:254
  23.8 12.2 %fusion.9 = f32[12,32,768]{2,1,0:T(8,128)S(1)} fusion(f32[12,32,256]{2,1,0:T(8,128)S(1)} %copy-done, f32[1,12,768,256]{3,2,1,0:T(8,128)} %param.6, bf16[1,12,768,256]{3,2,1,0:T(8,128)(2,1)} %param.5), kind=kOutput, calls=%fused_computation.12 | convolution fusion | flops 910688256 | bytes 15728640 | tf_op jit(solution)/shard_map/kdf,krf->krd/dot_general | solution.py:353
  36.0 1.4 reshape.76.x_ref
  37.4 45.1 %shard_map.92 = f32[2,4,4,4,18,128]{5,4,3,2,1,0:T(8,128)} custom-call(f32[2,4,4,4,18,128]{5,4,3,2,1,0:T(8,128)} %reshape.76.x_ref), custom_call_target="tpu_custom_call" | custom-call | flops 589824 | bytes 4718592 | tf_op jit(solution)/shard_map/pallas_call | solution.py:163
  82.6 1.7 reshape.77
  84.3 1.3 select_reduce_fusion.1
  85.6 0.4 fusion.35
  86.0 0.5 fusion.34
  86.9 0.4 fusion.32
  87.3 0.3 fusion.30
  87.7 0.4 fusion.29
  88.1 0.5 fusion.27
  88.6 0.5 fusion.13
  89.1 0.4 fusion.31
  89.5 0.3 fusion.28
  89.9 0.3 fusion.26
  90.5 1.1 fusion.118
  91.7 8.7 %fusion.4 = f32[12,32,256]{2,1,0:T(8,128)S(1)} fusion(f32[12,32,768]{2,1,0:T(8,128)S(1)} %fusion.118, f32[1,12,768,256]{3,2,1,0:T(8,128)} %param.6, bf16[1,12,768,256]{3,2,1,0:T(8,128)(2,1)S(1)} %bitcast.59), kind=kOutput, calls=%fused_computation.5 | convolution fusion | flops 910688256 | bytes 15728640 | tf_op jit(solution)/shard_map/kdf,krd->krf/dot_general | solution.py:358
  100.3 0.8 reshape.78.x_ref
  101.1 18.8 %shard_map.93 = f32[16,48,128]{2,1,0:T(8,128)} custom-call(f32[16,48,128]{2,1,0:T(8,128)} %reshape.78.x_ref), custom_call_target="tpu_custom_call" | custom-call | flops 196608 | bytes 1572864 | tf_op jit(solution)/shard_map/pallas_call | solution.py:163
  119.9 1.0 broadcast_multiply_fusion.1
  121.0 11.7 %fusion.2 = f32[12,32,768]{2,1,0:T(8,128)S(1)} fusion(f32[12,32,256]{2,1,0:T(8,128)S(1)} %div.15, f32[1,12,768,256]{3,2,1,0:T(8,128)} %param.6, bf16[1,12,768,256]{3,2,1,0:T(8,128)(2,1)} %param.5), kind=kOutput, calls=%fused_computation.3 | convolution fusion | flops 910688256 | bytes 15728640 | tf_op jit(solution)/shard_map/kdf,krf->krd/dot_general | solution.py:353
  132.7 1.4 reshape.79.x_ref
  134.1 42.8 %shard_map.94 = f32[2,4,4,4,18,128]{5,4,3,2,1,0:T(8,128)} custom-call(f32[2,4,4,4,18,128]{5,4,3,2,1,0:T(8,128)} %reshape.79.x_ref), custom_call_target="tpu_custom_call" | custom-call | flops 589824 | bytes 4718592 | tf_op jit(solution)/shard_map/pallas_call | solution.py:163
  177.0 1.9 reshape.80
  178.9 1.3 select_reduce_fusion
  180.2 0.4 fusion.25
  180.6 0.5 fusion.24
  181.5 0.4 fusion.22
  182.2 0.4 fusion.19
  182.7 0.5 fusion.17
  183.2 0.5 fusion.12
  183.7 0.4 fusion.21
  184.1 0.3 fusion.18
  184.4 0.3 fusion.16
  184.8 0.3 convolution_multiply_fusion
  185.1 1.1 fusion.119
  186.2 8.5 %fusion = f32[12,32,256]{2,1,0:T(8,128)S(1)} fusion(f32[12,32,768]{2,1,0:T(8,128)S(1)} %fusion.119, f32[1,12,768,256]{3,2,1,0:T(8,128)} %param.6, bf16[1,12,768,256]{3,2,1,0:T(8,128)(2,1)S(1)} %bitcast.61), kind=kOutput, calls=%fused_computation.1 | convolution fusion | flops 910688256 | bytes 15728640 | tf_op jit(solution)/shard_map/kdf,krd->krf/dot_general | solution.py:358
  194.7 0.8 reshape.81.x_ref
  195.5 18.4 %shard_map.95 = f32[16,48,128]{2,1,0:T(8,128)} custom-call(f32[16,48,128]{2,1,0:T(8,128)} %reshape.81.x_ref), custom_call_target="tpu_custom_call" | custom-call | flops 196608 | bytes 1572864 | tf_op jit(solution)/shard_map/pallas_call | solution.py:163
  213.9 1.0 broadcast_multiply_fusion
  215.1 1.4 fusion.14
  216.5 0.9 constant_dynamic-slice_fusion
  217.4 15.0 %shard_map.96 = (f32[72,2048]{1,0:T(8,128)}, f32[72,2048]{1,0:T(8,128)}) custom-call(f32[8,72,256]{2,1,0:T(8,128)} %bitcast.64, f32[72,2048]{1,0:T(8,128)} %mom_ref.1, f32[72,2048]{1,0:T(8,128)} %master_ref.1), custom_call_target="tpu_custom_call" | custom-call | flops 589824 | bytes 2949120 | tf_op jit(solution)/shard_map/pallas_call | solution.py:276
  232.4 18.7 %subtract_convert_fusion = (bf16[12,768,256]{2,1,0:T(8,128)(2,1)}, f32[1,12,768,256]{3,2,1,0:T(8,128)}) fusion(f32[12,768,256]{2,1,0:T(8,128)} %bitcast.62, f32[1,12,768,256]{3,2,1,0:T(8,128)} %param.6, bf16[1,12,768,256]{3,2,1,0:T(8,128)(2,1)} %param.5, f32[12,32,768]{2,1,0:T(8,128)S(1)} %fusion.119, f32[12,32,256]{2,1,0:T(8,128)S(1)} %div.17), kind=kOutput, calls=%fused_computation.10 | convolution fusion | flops 920125440 | bytes 39321600 | tf_op jit(solution)/shard_map/krd,krf->kdf/dot_general | solution.py:362
  251.1 0.8 copy.12
  251.9 0.8 copy.13
  (33 shorter events, 1.7 us)
Async XLA Ops:
  7.2 16.7 %copy-start = (f32[12,32,256]{2,1,0:T(8,128)S(1)}, f32[12,32,256]{2,1,0:T(8,128)}, u32[]{:S(2)}) copy-start(f32[12,32,256]{2,1,0:T(8,128)} %param.7) | copy-start | bytes 1179652
  7.2 225.2 %all-gather.2.cloned.1.call-start = ((), (), s32[]{:S(2)}) async-start(), calls=%async_computation | async-start | bytes 10027008 | tf_op jit(solution)/shard_map/all_gather | solution.py:349
  82.5 9.1 %slice-start = ((s8[4718592]{0:T(1024)(128)(4,1)}), s8[524288]{0:T(1024)(128)(4,1)S(1)}, s32[]{:S(2)}) async-start(s8[4718592]{0:T(1024)(128)(4,1)} %bitcast.58), calls=%async_computation.1 | async-start | bytes 1048576
  86.9 4.8 %slice-start.1 = ((s8[4718592]{0:T(1024)(128)(4,1)}), s8[4194304]{0:T(1024)(128)(4,1)S(1)}, s32[]{:S(2)}) async-start(s8[4718592]{0:T(1024)(128)(4,1)} %bitcast.58), calls=%async_computation.2 | async-start | bytes 8388608
  176.9 9.2 %slice-start.2 = ((s8[4718592]{0:T(1024)(128)(4,1)}), s8[524288]{0:T(1024)(128)(4,1)S(1)}, s32[]{:S(2)}) async-start(s8[4718592]{0:T(1024)(128)(4,1)} %bitcast.60), calls=%async_computation.3 | async-start | bytes 1048576
  181.4 4.8 %slice-start.3 = ((s8[4718592]{0:T(1024)(128)(4,1)}), s8[4194304]{0:T(1024)(128)(4,1)S(1)}, s32[]{:S(2)}) async-start(s8[4718592]{0:T(1024)(128)(4,1)} %bitcast.60), calls=%async_computation.4 | async-start | bytes 8388608
  215.0 36.1 %copy-start.2 = (f32[12,32,256]{2,1,0:T(8,128)}, f32[12,32,256]{2,1,0:T(8,128)S(1)}, u32[]{:S(2)}) copy-start(f32[12,32,256]{2,1,0:T(8,128)S(1)} %div.17) | copy-start | bytes 1179652
  232.4 18.7 %copy-start.4 = (f32[72,2048]{1,0:T(8,128)S(1)}, f32[72,2048]{1,0:T(8,128)}, u32[]{:S(2)}) copy-start(f32[72,2048]{1,0:T(8,128)} %get-tuple-element.26) | copy-start | bytes 1769476
  232.4 19.5 %copy-start.3 = (f32[72,2048]{1,0:T(8,128)S(1)}, f32[72,2048]{1,0:T(8,128)}, u32[]{:S(2)}) copy-start(f32[72,2048]{1,0:T(8,128)} %get-tuple-element.27) | copy-start | bytes 1769476
  232.4 20.3 %copy-start.1 = (f32[12,32,256]{2,1,0:T(8,128)S(1)}, f32[12,32,256]{2,1,0:T(8,128)}, u32[]{:S(2)}) copy-start(f32[12,32,256]{2,1,0:T(8,128)} %param.7) | copy-start | bytes 1179652
Sparse Core Ops, SparseCore 0:
  23.9 78.3 all-gather.1

commit v8 on v7

--- a/solution.py
+++ b/solution.py
@@ -224,7 +224,7 @@
     pl.semaphore_wait(barrier, n - 1)
 
     def block(j):
-        return x_ref.at[:, pl.ds(pl.multiple_of(j * cols, cols), cols)]
+        return x_ref.at[j]
 
     copies = []
     for off in range(1, n):
@@ -250,6 +250,7 @@
 def by_columns(x, n, collective_id):
     rows, width = x.shape
     cols = width // n
+    x = x.reshape(rows, n, cols).transpose(1, 0, 2)
     vmem = pl.BlockSpec(memory_space=pltpu.VMEM)
     return pl.pallas_call(
         _columns_kernel,

time: 260 us -> 260 us (level)
  no operation moved by 1% of the time
where the time goes in v8:
time: 260 us
  Pallas kernels  155 us (60%)
  matrix products  75.5 us (29%)
  between operations  14.6 us (6%)
  local copies, waits for them, and re-layouts  11.6 us (4%)
  other arithmetic  3.43 us (1%)
    pallas_call x4, Pallas kernels, allreduce(): pl.pallas_call(functools.partial(_allreduce_kernel, tuple(levels)), out_s...  125 us
    dot_general x2, matrix products, local(): jnp.einsum('kdf,krf->krd', corrected, current, precision=lax.Precision.HI...  23.8 us
    dot_general x1, matrix products, local(): jnp.einsum('krd,krf->kdf', ortho_basis, current, precision=lax.Precision....  18.7 us
    dot_general x2, matrix products, local(): jnp.einsum('kdf,krd->krf', corrected, ortho_basis, precision=lax.Precisio...  17.1 us
    pallas_call x1, Pallas kernels, flat_update(): pl.pallas_call(_update_kernel, out_shape=(jax.ShapeDtypeStruct(momentum.s...  15 us
    pallas_call x1, Pallas kernels, by_columns(): pl.pallas_call(_columns_kernel, out_shape=jax.ShapeDtypeStruct((n, rows,...  14.4 us
    dot_general x16, matrix products, orthonormal_by_gram(): jnp.einsum('krs,kst,kut->kru', step, gram_now, step, precision=hi)  6.9 us
  transfers between devices with their start and end apart: 1, of which 0 were waited for; matrix products, arithmetic and copies ran while one was open for 26% of the time, Pallas kernels for 54%

profile of v8, /device:TPU:1, one launch (start us, length us, event | category | flops | bytes accessed | tf_op | source)
XLA Modules:
  0.0 259.7 jit_solution(8679228037020112176)
XLA Ops:
  7.2 1.4 multiply_subtract_fusion
  8.6 0.9 copy.13
  9.4 14.4 %shard_map.97 = f32[8,72,256]{2,1,0:T(8,128)} custom-call(f32[8,72,256]{2,1,0:T(8,128)} %bitcast.74), custom_call_target="tpu_custom_call" | custom-call | bytes 1179648 | tf_op jit(solution)/shard_map/pallas_call | solution.py:255
  23.9 12.2 %fusion.9 = f32[12,32,768]{2,1,0:T(8,128)S(1)} fusion(f32[12,32,256]{2,1,0:T(8,128)S(1)} %copy-done, f32[1,12,768,256]{3,2,1,0:T(8,128)} %param.6, bf16[1,12,768,256]{3,2,1,0:T(8,128)(2,1)} %param.5), kind=kOutput, calls=%fused_computation.12 | convolution fusion | flops 910688256 | bytes 15728640 | tf_op jit(solution)/shard_map/kdf,krf->krd/dot_general | solution.py:354
  36.0 1.4 reshape.79.x_ref
  37.5 45.1 %shard_map.92 = f32[2,4,4,4,18,128]{5,4,3,2,1,0:T(8,128)} custom-call(f32[2,4,4,4,18,128]{5,4,3,2,1,0:T(8,128)} %reshape.79.x_ref), custom_call_target="tpu_custom_call" | custom-call | flops 589824 | bytes 4718592 | tf_op jit(solution)/shard_map/pallas_call | solution.py:163
  82.6 1.7 reshape.80
  84.3 1.3 select_reduce_fusion.1
  85.7 0.4 fusion.35
  86.1 0.5 fusion.34
  86.9 0.4 fusion.32
  87.7 0.4 fusion.29
  88.2 0.5 fusion.27
  88.7 0.5 fusion.13
  89.2 0.4 fusion.31
  89.6 0.3 fusion.28
  89.9 0.3 fusion.26
  90.6 1.1 fusion.118
  91.7 8.7 %fusion.4 = f32[12,32,256]{2,1,0:T(8,128)S(1)} fusion(f32[12,32,768]{2,1,0:T(8,128)S(1)} %fusion.118, f32[1,12,768,256]{3,2,1,0:T(8,128)} %param.6, bf16[1,12,768,256]{3,2,1,0:T(8,128)(2,1)S(1)} %bitcast.66), kind=kOutput, calls=%fused_computation.5 | convolution fusion | flops 910688256 | bytes 15728640 | tf_op jit(solution)/shard_map/kdf,krd->krf/dot_general | solution.py:359
  100.4 0.8 reshape.81.x_ref
  101.1 18.8 %shard_map.93 = f32[16,48,128]{2,1,0:T(8,128)} custom-call(f32[16,48,128]{2,1,0:T(8,128)} %reshape.81.x_ref), custom_call_target="tpu_custom_call" | custom-call | flops 196608 | bytes 1572864 | tf_op jit(solution)/shard_map/pallas_call | solution.py:163
  119.9 1.0 broadcast_multiply_fusion.1
  121.1 11.7 %fusion.2 = f32[12,32,768]{2,1,0:T(8,128)S(1)} fusion(f32[12,32,256]{2,1,0:T(8,128)S(1)} %div.15, f32[1,12,768,256]{3,2,1,0:T(8,128)} %param.6, bf16[1,12,768,256]{3,2,1,0:T(8,128)(2,1)} %param.5), kind=kOutput, calls=%fused_computation.3 | convolution fusion | flops 910688256 | bytes 15728640 | tf_op jit(solution)/shard_map/kdf,krf->krd/dot_general | solution.py:354
  132.7 1.4 reshape.82.x_ref
  134.1 42.8 %shard_map.94 = f32[2,4,4,4,18,128]{5,4,3,2,1,0:T(8,128)} custom-call(f32[2,4,4,4,18,128]{5,4,3,2,1,0:T(8,128)} %reshape.82.x_ref), custom_call_target="tpu_custom_call" | custom-call | flops 589824 | bytes 4718592 | tf_op jit(solution)/shard_map/pallas_call | solution.py:163
  177.0 1.9 reshape.83
  178.9 1.3 select_reduce_fusion
  180.2 0.4 fusion.25
  180.7 0.5 fusion.24
  181.5 0.4 fusion.22
  182.3 0.4 fusion.19
  182.7 0.5 fusion.17
  183.2 0.5 fusion.12
  183.7 0.4 fusion.21
  184.1 0.3 fusion.18
  184.5 0.3 fusion.16
  184.8 0.3 convolution_multiply_fusion
  185.1 1.1 fusion.119
  186.3 8.5 %fusion = f32[12,32,256]{2,1,0:T(8,128)S(1)} fusion(f32[12,32,768]{2,1,0:T(8,128)S(1)} %fusion.119, f32[1,12,768,256]{3,2,1,0:T(8,128)} %param.6, bf16[1,12,768,256]{3,2,1,0:T(8,128)(2,1)S(1)} %bitcast.68), kind=kOutput, calls=%fused_computation.1 | convolution fusion | flops 910688256 | bytes 15728640 | tf_op jit(solution)/shard_map/kdf,krd->krf/dot_general | solution.py:359
  194.7 0.8 reshape.84.x_ref
  195.5 18.4 %shard_map.95 = f32[16,48,128]{2,1,0:T(8,128)} custom-call(f32[16,48,128]{2,1,0:T(8,128)} %reshape.84.x_ref), custom_call_target="tpu_custom_call" | custom-call | flops 196608 | bytes 1572864 | tf_op jit(solution)/shard_map/pallas_call | solution.py:163
  213.9 1.0 broadcast_multiply_fusion
  215.1 1.4 fusion.14
  216.6 0.9 constant_dynamic-slice_fusion
  217.4 15.0 %shard_map.96 = (f32[72,2048]{1,0:T(8,128)}, f32[72,2048]{1,0:T(8,128)}) custom-call(f32[8,72,256]{2,1,0:T(8,128)} %bitcast.71, f32[72,2048]{1,0:T(8,128)} %mom_ref.1, f32[72,2048]{1,0:T(8,128)} %master_ref.1), custom_call_target="tpu_custom_call" | custom-call | flops 589824 | bytes 2949120 | tf_op jit(solution)/shard_map/pallas_call | solution.py:277
  232.5 18.7 %subtract_convert_fusion = (bf16[12,768,256]{2,1,0:T(8,128)(2,1)}, f32[1,12,768,256]{3,2,1,0:T(8,128)}) fusion(f32[12,768,256]{2,1,0:T(8,128)} %bitcast.69, f32[1,12,768,256]{3,2,1,0:T(8,128)} %param.6, bf16[1,12,768,256]{3,2,1,0:T(8,128)(2,1)} %param.5, f32[12,32,768]{2,1,0:T(8,128)S(1)} %fusion.119, f32[12,32,256]{2,1,0:T(8,128)S(1)} %div.17), kind=kOutput, calls=%fused_computation.10 | convolution fusion | flops 920125440 | bytes 39321600 | tf_op jit(solution)/shard_map/krd,krf->kdf/dot_general | solution.py:363
  251.2 0.8 copy.16
  252.0 0.8 copy.17
  (34 shorter events, 2.0 us)
Async XLA Ops:
  7.2 16.7 %copy-start = (f32[12,32,256]{2,1,0:T(8,128)S(1)}, f32[12,32,256]{2,1,0:T(8,128)}, u32[]{:S(2)}) copy-start(f32[12,32,256]{2,1,0:T(8,128)} %param.7) | copy-start | bytes 1179652
  7.2 225.3 %all-gather.2.cloned.1.call-start = ((), (), s32[]{:S(2)}) async-start(), calls=%async_computation | async-start | bytes 10027008 | tf_op jit(solution)/shard_map/all_gather | solution.py:350
  82.6 9.1 %slice-start = ((s8[4718592]{0:T(1024)(128)(4,1)}), s8[524288]{0:T(1024)(128)(4,1)S(1)}, s32[]{:S(2)}) async-start(s8[4718592]{0:T(1024)(128)(4,1)} %bitcast.65), calls=%async_computation.1 | async-start | bytes 1048576
  86.9 4.8 %slice-start.1 = ((s8[4718592]{0:T(1024)(128)(4,1)}), s8[4194304]{0:T(1024)(128)(4,1)S(1)}, s32[]{:S(2)}) async-start(s8[4718592]{0:T(1024)(128)(4,1)} %bitcast.65), calls=%async_computation.2 | async-start | bytes 8388608
  177.0 9.2 %slice-start.2 = ((s8[4718592]{0:T(1024)(128)(4,1)}), s8[524288]{0:T(1024)(128)(4,1)S(1)}, s32[]{:S(2)}) async-start(s8[4718592]{0:T(1024)(128)(4,1)} %bitcast.67), calls=%async_computation.3 | async-start | bytes 1048576
  181.5 4.8 %slice-start.3 = ((s8[4718592]{0:T(1024)(128)(4,1)}), s8[4194304]{0:T(1024)(128)(4,1)S(1)}, s32[]{:S(2)}) async-start(s8[4718592]{0:T(1024)(128)(4,1)} %bitcast.67), calls=%async_computation.4 | async-start | bytes 8388608
  215.1 36.1 %copy-start.2 = (f32[12,32,256]{2,1,0:T(8,128)}, f32[12,32,256]{2,1,0:T(8,128)S(1)}, u32[]{:S(2)}) copy-start(f32[12,32,256]{2,1,0:T(8,128)S(1)} %div.17) | copy-start | bytes 1179652
  232.5 18.7 %copy-start.4 = (f32[72,2048]{1,0:T(8,128)S(1)}, f32[72,2048]{1,0:T(8,128)}, u32[]{:S(2)}) copy-start(f32[72,2048]{1,0:T(8,128)} %get-tuple-element.26) | copy-start | bytes 1769476
  232.5 19.5 %copy-start.3 = (f32[72,2048]{1,0:T(8,128)S(1)}, f32[72,2048]{1,0:T(8,128)}, u32[]{:S(2)}) copy-start(f32[72,2048]{1,0:T(8,128)} %get-tuple-element.27) | copy-start | bytes 1769476
  232.5 20.3 %copy-start.1 = (f32[12,32,256]{2,1,0:T(8,128)S(1)}, f32[12,32,256]{2,1,0:T(8,128)}, u32[]{:S(2)}) copy-start(f32[12,32,256]{2,1,0:T(8,128)} %param.7) | copy-start | bytes 1179652
Sparse Core Ops, SparseCore 0:
  24.0 78.3 all-gather.1

commit v9 on v7

--- a/solution.py
+++ b/solution.py
@@ -30,7 +30,7 @@
     return tuple(base if axis == name else lax.axis_index(axis) for axis in MESH_AXES)
 
 
-def _allreduce_kernel(levels, x_ref, o_ref, *scratch):
+def _allreduce_kernel(levels, direct, x_ref, o_ref, *scratch):
     n_lev = len(levels)
     it = iter(scratch)
     recv = [next(it) for _ in range(n_lev)]
@@ -59,21 +59,26 @@
     src = x_ref
     for lev, (name, n, _) in enumerate(levels):
         m = me[lev]
+        last_direct = direct and lev == n_lev - 1
+
+        def piece(j, src=src, last_direct=last_direct):
+            return src if last_direct else src.at[j]
+
         copies = []
         for off in range(1, n):
             j = lax.rem(m + off, n)
             cp = pltpu.make_async_remote_copy(
-                src_ref=src.at[j], dst_ref=recv[lev].at[m],
+                src_ref=piece(j), dst_ref=recv[lev].at[m],
                 send_sem=rs_send[lev].at[off], recv_sem=rs_recv[lev].at[m],
                 device_id=_peer(levels[lev], j), device_id_type=pl.DeviceIdType.MESH)
             cp.start()
             copies.append((j, off, cp))
-        own = pltpu.make_async_copy(src.at[m], recv[lev].at[m], local_sem.at[0])
+        own = pltpu.make_async_copy(piece(m), recv[lev].at[m], local_sem.at[0])
         own.start()
         own.wait()
         for j, off, cp in copies:
             pltpu.make_async_remote_copy(
-                src_ref=src.at[j], dst_ref=recv[lev].at[j],
+                src_ref=piece(j), dst_ref=recv[lev].at[j],
                 send_sem=rs_send[lev].at[off], recv_sem=rs_recv[lev].at[j],
                 device_id=_peer(levels[lev], j), device_id_type=pl.DeviceIdType.MESH).wait_recv()
         for j, off, cp in copies:
@@ -81,6 +86,8 @@
         r = recv[lev]
         if lev < n_lev - 1:
             dst = sums[lev]
+        elif last_direct:
+            dst = gath_bufs[lev]
         else:
             dst = gath_bufs[lev].at[m]
         if len(r.shape) > 3:
@@ -110,7 +117,7 @@
         if lev < n_lev - 1:
             src = sums[lev]
 
-    for lev in reversed(range(n_lev)):
+    for lev in reversed(range(n_lev - 1 if direct else n_lev)):
         name, n, _ = levels[lev]
         m = me[lev]
         buf = gath_bufs[lev]
@@ -139,7 +146,7 @@
             cp.wait_send()
 
 
-def allreduce(x, levels, collective_id):
+def allreduce(x, levels, collective_id, direct=False):
     shape = x.shape
     total = x.size
     counts = [n for _, n, _ in levels]
@@ -151,7 +158,10 @@
     xr = x.reshape(full)
     scratch = []
     for lev in range(len(levels)):
-        scratch.append(pltpu.VMEM(full[lev:], jnp.float32))
+        if direct and lev == len(levels) - 1:
+            scratch.append(pltpu.VMEM((counts[lev],) + full[lev:], jnp.float32))
+        else:
+            scratch.append(pltpu.VMEM(full[lev:], jnp.float32))
     for lev in range(len(levels) - 1):
         scratch.append(pltpu.VMEM(full[lev + 1:], jnp.float32))
     for lev in range(len(levels) - 1):
@@ -161,7 +171,7 @@
             scratch.append(pltpu.SemaphoreType.DMA((n,)))
     scratch.append(pltpu.SemaphoreType.DMA((1,)))
     out = pl.pallas_call(
-        functools.partial(_allreduce_kernel, tuple(levels)),
+        functools.partial(_allreduce_kernel, tuple(levels), direct),
         out_shape=jax.ShapeDtypeStruct(full, jnp.float32),
         in_specs=[pl.BlockSpec(memory_space=pltpu.VMEM)],
         out_specs=pl.BlockSpec(memory_space=pltpu.VMEM),
@@ -353,7 +363,7 @@
         partial_factor = jnp.einsum(
             "kdf,krf->krd", corrected, current, precision=lax.Precision.HIGHEST
         )
-        summed = allreduce(partial_factor, both, 0)
+        summed = allreduce(partial_factor, both, 0, direct=True)
         ortho_basis = orthonormal_by_gram(summed)
         partial_query = jnp.einsum(
             "kdf,krd->krf", corrected, ortho_basis, precision=lax.Precision.HIGHEST

time: 260 us -> 255 us (0.981)
  Pallas kernels: 155 us -> 149 us
    pallas_call x4, Pallas kernels: 125 us -> 119 us  [allreduce(): pl.pallas_call(functools.partial(_allreduce_kernel, tuple(levels), direct...]
  transfers between devices with their start and end apart: 1 -> 1, of which waited for: 0 -> 0; matrix products, arithmetic and copies ran while one was open for 26% -> 27% of each run, Pallas kernels for 54% -> 53%
where the time goes in v9:
time: 255 us; the launch traced here: 254 us
  Pallas kernels  149 us (58%)
  matrix products  75.7 us (30%)
  between operations  14.6 us (6%)
  local copies, waits for them, and re-layouts  10.8 us (4%)
  other arithmetic  4.25 us (2%)
    pallas_call x4, Pallas kernels, allreduce(): pl.pallas_call(functools.partial(_allreduce_kernel, tuple(levels), direct...  119 us
    dot_general x2, matrix products, local(): jnp.einsum('kdf,krf->krd', corrected, current, precision=lax.Precision.HI...  23.8 us
    dot_general x1, matrix products, local(): jnp.einsum('krd,krf->kdf', ortho_basis, current, precision=lax.Precision....  18.7 us
    dot_general x2, matrix products, local(): jnp.einsum('kdf,krd->krf', corrected, ortho_basis, precision=lax.Precisio...  17.3 us
    pallas_call x1, Pallas kernels, flat_update(): pl.pallas_call(_update_kernel, out_shape=(jax.ShapeDtypeStruct(momentum.s...  15.3 us
    pallas_call x1, Pallas kernels, by_columns(): pl.pallas_call(_columns_kernel, out_shape=jax.ShapeDtypeStruct((n, rows,...  14.4 us
    dot_general x16, matrix products, orthonormal_by_gram(): jnp.einsum('krs,kst,kut->kru', step, gram_now, step, precision=hi)  6.9 us
  transfers between devices with their start and end apart: 1, of which 0 were waited for; matrix products, arithmetic and copies ran while one was open for 27% of the time, Pallas kernels for 53%

profile of v9, /device:TPU:1, one launch (start us, length us, event | category | flops | bytes accessed | tf_op | source)
XLA Modules:
  0.0 254.3 jit_solution(757646509541264532)
XLA Ops:
  7.2 2.2 multiply_subtract_fusion.x_ref
  9.4 14.4 %shard_map.97 = f32[8,72,256]{2,1,0:T(8,128)} custom-call(f32[72,2048]{1,0:T(8,128)} %multiply_subtract_fusion.x_ref), custom_call_target="tpu_custom_call" | custom-call | bytes 1179648 | tf_op jit(solution)/shard_map/pallas_call | solution.py:264
  23.8 12.2 %fusion.9 = f32[12,32,768]{2,1,0:T(8,128)S(1)} fusion(f32[12,32,256]{2,1,0:T(8,128)S(1)} %copy-done, f32[1,12,768,256]{3,2,1,0:T(8,128)} %param.6, bf16[1,12,768,256]{3,2,1,0:T(8,128)(2,1)} %param.5), kind=kOutput, calls=%fused_computation.12 | convolution fusion | flops 910688256 | bytes 15728640 | tf_op jit(solution)/shard_map/kdf,krf->krd/dot_general | solution.py:363
  36.0 1.4 reshape.76.x_ref
  37.4 42.4 %shard_map.92 = f32[2,4,4,4,18,128]{5,4,3,2,1,0:T(8,128)} custom-call(f32[2,4,4,4,18,128]{5,4,3,2,1,0:T(8,128)} %reshape.76.x_ref), custom_call_target="tpu_custom_call" | custom-call | flops 589824 | bytes 4718592 | tf_op jit(solution)/shard_map/pallas_call | solution.py:173
  79.9 1.7 reshape.77
  81.6 1.3 select_reduce_fusion.1
  82.9 0.4 fusion.35
  83.4 0.5 fusion.34
  84.2 0.4 fusion.32
  85.0 0.4 fusion.29
  85.4 0.5 fusion.27
  85.9 0.5 fusion.13
  86.5 0.4 fusion.31
  86.8 0.3 fusion.28
  87.2 0.3 fusion.26
  87.8 1.1 fusion.118
  89.0 8.8 %fusion.4 = f32[12,32,256]{2,1,0:T(8,128)S(1)} fusion(f32[12,32,768]{2,1,0:T(8,128)S(1)} %fusion.118, f32[1,12,768,256]{3,2,1,0:T(8,128)} %param.6, bf16[1,12,768,256]{3,2,1,0:T(8,128)(2,1)S(1)} %bitcast.59), kind=kOutput, calls=%fused_computation.5 | convolution fusion | flops 910688256 | bytes 15728640 | tf_op jit(solution)/shard_map/kdf,krd->krf/dot_general | solution.py:368
  97.8 0.8 reshape.78.x_ref
  98.6 19.1 %shard_map.93 = f32[16,48,128]{2,1,0:T(8,128)} custom-call(f32[16,48,128]{2,1,0:T(8,128)} %reshape.78.x_ref), custom_call_target="tpu_custom_call" | custom-call | flops 196608 | bytes 1572864 | tf_op jit(solution)/shard_map/pallas_call | solution.py:173
  117.7 1.0 broadcast_multiply_fusion.1
  118.8 11.7 %fusion.2 = f32[12,32,768]{2,1,0:T(8,128)S(1)} fusion(f32[12,32,256]{2,1,0:T(8,128)S(1)} %div.15, f32[1,12,768,256]{3,2,1,0:T(8,128)} %param.6, bf16[1,12,768,256]{3,2,1,0:T(8,128)(2,1)} %param.5), kind=kOutput, calls=%fused_computation.3 | convolution fusion | flops 910688256 | bytes 15728640 | tf_op jit(solution)/shard_map/kdf,krf->krd/dot_general | solution.py:363
  130.5 1.4 reshape.79.x_ref
  131.9 40.5 %shard_map.94 = f32[2,4,4,4,18,128]{5,4,3,2,1,0:T(8,128)} custom-call(f32[2,4,4,4,18,128]{5,4,3,2,1,0:T(8,128)} %reshape.79.x_ref), custom_call_target="tpu_custom_call" | custom-call | flops 589824 | bytes 4718592 | tf_op jit(solution)/shard_map/pallas_call | solution.py:173
  172.4 1.9 reshape.80
  174.3 1.3 select_reduce_fusion
  175.6 0.4 fusion.25
  176.0 0.5 fusion.24
  176.9 0.4 fusion.22
  177.3 0.3 fusion.20
  177.7 0.4 fusion.19
  178.1 0.5 fusion.17
  178.6 0.5 fusion.12
  179.1 0.4 fusion.21
  179.5 0.3 fusion.18
  179.8 0.3 fusion.16
  180.2 0.3 convolution_multiply_fusion
  180.5 1.1 fusion.119
  181.6 8.5 %fusion = f32[12,32,256]{2,1,0:T(8,128)S(1)} fusion(f32[12,32,768]{2,1,0:T(8,128)S(1)} %fusion.119, f32[1,12,768,256]{3,2,1,0:T(8,128)} %param.6, bf16[1,12,768,256]{3,2,1,0:T(8,128)(2,1)S(1)} %bitcast.61), kind=kOutput, calls=%fused_computation.1 | convolution fusion | flops 910688256 | bytes 15728640 | tf_op jit(solution)/shard_map/kdf,krd->krf/dot_general | solution.py:368
  190.1 0.8 reshape.81.x_ref
  190.9 17.3 %shard_map.95 = f32[16,48,128]{2,1,0:T(8,128)} custom-call(f32[16,48,128]{2,1,0:T(8,128)} %reshape.81.x_ref), custom_call_target="tpu_custom_call" | custom-call | flops 196608 | bytes 1572864 | tf_op jit(solution)/shard_map/pallas_call | solution.py:173
  208.3 1.0 broadcast_multiply_fusion
  209.4 1.4 fusion.14
  210.9 0.9 constant_dynamic-slice_fusion
  211.7 15.3 %shard_map.96 = (f32[72,2048]{1,0:T(8,128)}, f32[72,2048]{1,0:T(8,128)}) custom-call(f32[8,72,256]{2,1,0:T(8,128)} %bitcast.64, f32[72,2048]{1,0:T(8,128)} %mom_ref.1, f32[72,2048]{1,0:T(8,128)} %master_ref.1), custom_call_target="tpu_custom_call" | custom-call | flops 589824 | bytes 2949120 | tf_op jit(solution)/shard_map/pallas_call | solution.py:286
  227.1 18.7 %subtract_convert_fusion = (bf16[12,768,256]{2,1,0:T(8,128)(2,1)}, f32[1,12,768,256]{3,2,1,0:T(8,128)}) fusion(f32[12,768,256]{2,1,0:T(8,128)} %bitcast.62, f32[1,12,768,256]{3,2,1,0:T(8,128)} %param.6, bf16[1,12,768,256]{3,2,1,0:T(8,128)(2,1)} %param.5, f32[12,32,768]{2,1,0:T(8,128)S(1)} %fusion.119, f32[12,32,256]{2,1,0:T(8,128)S(1)} %div.17), kind=kOutput, calls=%fused_computation.10 | convolution fusion | flops 920125440 | bytes 39321600 | tf_op jit(solution)/shard_map/krd,krf->kdf/dot_general | solution.py:372
  245.8 0.8 copy.12
  246.6 0.8 copy.13
  (33 shorter events, 1.7 us)
Async XLA Ops:
  7.2 16.7 %copy-start = (f32[12,32,256]{2,1,0:T(8,128)S(1)}, f32[12,32,256]{2,1,0:T(8,128)}, u32[]{:S(2)}) copy-start(f32[12,32,256]{2,1,0:T(8,128)} %param.7) | copy-start | bytes 1179652
  7.2 219.9 %all-gather.2.cloned.1.call-start = ((), (), s32[]{:S(2)}) async-start(), calls=%async_computation | async-start | bytes 10027008 | tf_op jit(solution)/shard_map/all_gather | solution.py:359
  79.8 9.1 %slice-start = ((s8[4718592]{0:T(1024)(128)(4,1)}), s8[524288]{0:T(1024)(128)(4,1)S(1)}, s32[]{:S(2)}) async-start(s8[4718592]{0:T(1024)(128)(4,1)} %bitcast.58), calls=%async_computation.1 | async-start | bytes 1048576
  84.2 4.8 %slice-start.1 = ((s8[4718592]{0:T(1024)(128)(4,1)}), s8[4194304]{0:T(1024)(128)(4,1)S(1)}, s32[]{:S(2)}) async-start(s8[4718592]{0:T(1024)(128)(4,1)} %bitcast.58), calls=%async_computation.2 | async-start | bytes 8388608
  172.4 9.3 %slice-start.2 = ((s8[4718592]{0:T(1024)(128)(4,1)}), s8[524288]{0:T(1024)(128)(4,1)S(1)}, s32[]{:S(2)}) async-start(s8[4718592]{0:T(1024)(128)(4,1)} %bitcast.60), calls=%async_computation.3 | async-start | bytes 1048576
  176.9 4.8 %slice-start.3 = ((s8[4718592]{0:T(1024)(128)(4,1)}), s8[4194304]{0:T(1024)(128)(4,1)S(1)}, s32[]{:S(2)}) async-start(s8[4718592]{0:T(1024)(128)(4,1)} %bitcast.60), calls=%async_computation.4 | async-start | bytes 8388608
  209.4 36.4 %copy-start.2 = (f32[12,32,256]{2,1,0:T(8,128)}, f32[12,32,256]{2,1,0:T(8,128)S(1)}, u32[]{:S(2)}) copy-start(f32[12,32,256]{2,1,0:T(8,128)S(1)} %div.17) | copy-start | bytes 1179652
  227.1 18.7 %copy-start.4 = (f32[72,2048]{1,0:T(8,128)S(1)}, f32[72,2048]{1,0:T(8,128)}, u32[]{:S(2)}) copy-start(f32[72,2048]{1,0:T(8,128)} %get-tuple-element.26) | copy-start | bytes 1769476
  227.1 19.5 %copy-start.3 = (f32[72,2048]{1,0:T(8,128)S(1)}, f32[72,2048]{1,0:T(8,128)}, u32[]{:S(2)}) copy-start(f32[72,2048]{1,0:T(8,128)} %get-tuple-element.27) | copy-start | bytes 1769476
  227.1 20.3 %copy-start.1 = (f32[12,32,256]{2,1,0:T(8,128)S(1)}, f32[12,32,256]{2,1,0:T(8,128)}, u32[]{:S(2)}) copy-start(f32[12,32,256]{2,1,0:T(8,128)} %param.7) | copy-start | bytes 1179652
Sparse Core Ops, SparseCore 0:
  23.9 78.3 all-gather.1

commit v10 on v9

--- a/solution.py
+++ b/solution.py
@@ -357,7 +357,7 @@
     kept_cols = by_columns(kept, tensor, 3)
     kept_cols = kept_cols.reshape(-1, kept_cols.shape[-1])
     kept_all = lax.all_gather(kept_cols, "rep", axis=0, tiled=True)
-    rep_only = (("rep", replicas, 1),)
+    rep_only = split_levels("rep", replicas, 4)
     both = split_levels("tp", lax.axis_size("tp"), 2) + split_levels("rep", replicas, 4)
     for power_pass in range(ROUNDS):
         partial_factor = jnp.einsum(
@@ -368,7 +368,7 @@
         partial_query = jnp.einsum(
             "kdf,krd->krf", corrected, ortho_basis, precision=lax.Precision.HIGHEST
         )
-        current = allreduce(partial_query, rep_only, 1) / replicas
+        current = allreduce(partial_query, rep_only, 1, direct=len(rep_only) > 1) / replicas
     approx = jnp.einsum("krd,krf->kdf", ortho_basis, current, precision=lax.Precision.HIGHEST)
     new_error = (corrected - approx)[None]
     matrices, model_width, shard_cols = approx.shape

time: 255 us -> 262 us (1.027)
  Pallas kernels: 149 us -> 156 us
    pallas_call x4, Pallas kernels: 119 us -> 128 us  [allreduce(): pl.pallas_call(functools.partial(_allreduce_kernel, tuple(levels), direct...]
  transfers between devices with their start and end apart: 1 -> 1, of which waited for: 0 -> 0; matrix products, arithmetic and copies ran while one was open for 27% -> 26% of each run, Pallas kernels for 53% -> 54%
where the time goes in v10:
time: 262 us; the launch traced here: 261 us
  Pallas kernels  156 us (60%)
  matrix products  75.7 us (29%)
  between operations  14.6 us (6%)
  local copies, waits for them, and re-layouts  10.8 us (4%)
  other arithmetic  4.25 us (2%)
    pallas_call x4, Pallas kernels, allreduce(): pl.pallas_call(functools.partial(_allreduce_kernel, tuple(levels), direct...  128 us
    dot_general x2, matrix products, local(): jnp.einsum('kdf,krf->krd', corrected, current, precision=lax.Precision.HI...  23.8 us
    dot_general x1, matrix products, local(): jnp.einsum('krd,krf->kdf', ortho_basis, current, precision=lax.Precision....  18.7 us
    dot_general x2, matrix products, local(): jnp.einsum('kdf,krd->krf', corrected, ortho_basis, precision=lax.Precisio...  17.3 us
    pallas_call x1, Pallas kernels, by_columns(): pl.pallas_call(_columns_kernel, out_shape=jax.ShapeDtypeStruct((n, rows,...  14.4 us
    pallas_call x1, Pallas kernels, flat_update(): pl.pallas_call(_update_kernel, out_shape=(jax.ShapeDtypeStruct(momentum.s...  13.5 us
    dot_general x16, matrix products, orthonormal_by_gram(): jnp.einsum('krs,kst,kut->kru', step, gram_now, step, precision=hi)  6.9 us
  transfers between devices with their start and end apart: 1, of which 0 were waited for; matrix products, arithmetic and copies ran while one was open for 26% of the time, Pallas kernels for 54%

profile of v10, /device:TPU:1, one launch (start us, length us, event | category | flops | bytes accessed | tf_op | source)
XLA Modules:
  0.0 261.3 jit_solution(7292908300973790570)
XLA Ops:
  7.2 2.2 multiply_subtract_fusion.x_ref
  9.4 14.4 %shard_map.97 = f32[8,72,256]{2,1,0:T(8,128)} custom-call(f32[72,2048]{1,0:T(8,128)} %multiply_subtract_fusion.x_ref), custom_call_target="tpu_custom_call" | custom-call | bytes 1179648 | tf_op jit(solution)/shard_map/pallas_call | solution.py:264
  23.8 12.2 %fusion.9 = f32[12,32,768]{2,1,0:T(8,128)S(1)} fusion(f32[12,32,256]{2,1,0:T(8,128)S(1)} %copy-done, f32[1,12,768,256]{3,2,1,0:T(8,128)} %param.6, bf16[1,12,768,256]{3,2,1,0:T(8,128)(2,1)} %param.5), kind=kOutput, calls=%fused_computation.12 | convolution fusion | flops 910688256 | bytes 15728640 | tf_op jit(solution)/shard_map/kdf,krf->krd/dot_general | solution.py:363
  36.0 1.4 reshape.76.x_ref
  37.4 42.4 %shard_map.92 = f32[2,4,4,4,18,128]{5,4,3,2,1,0:T(8,128)} custom-call(f32[2,4,4,4,18,128]{5,4,3,2,1,0:T(8,128)} %reshape.76.x_ref), custom_call_target="tpu_custom_call" | custom-call | flops 589824 | bytes 4718592 | tf_op jit(solution)/shard_map/pallas_call | solution.py:173
  79.9 1.7 reshape.77
  81.6 1.3 select_reduce_fusion.1
  82.9 0.4 fusion.35
  83.4 0.5 fusion.34
  84.2 0.4 fusion.32
  85.0 0.4 fusion.29
  85.4 0.5 fusion.27
  85.9 0.5 fusion.13
  86.5 0.4 fusion.31
  86.8 0.3 fusion.28
  87.2 0.3 fusion.26
  87.8 1.1 fusion.118
  89.0 8.8 %fusion.4 = f32[12,32,256]{2,1,0:T(8,128)S(1)} fusion(f32[12,32,768]{2,1,0:T(8,128)S(1)} %fusion.118, f32[1,12,768,256]{3,2,1,0:T(8,128)} %param.6, bf16[1,12,768,256]{3,2,1,0:T(8,128)(2,1)S(1)} %bitcast.63), kind=kOutput, calls=%fused_computation.5 | convolution fusion | flops 910688256 | bytes 15728640 | tf_op jit(solution)/shard_map/kdf,krd->krf/dot_general | solution.py:368
  97.8 0.8 reshape.78.x_ref
  98.6 22.6 %shard_map.93 = f32[4,4,48,128]{3,2,1,0:T(8,128)} custom-call(f32[4,4,48,128]{3,2,1,0:T(8,128)} %reshape.78.x_ref), custom_call_target="tpu_custom_call" | custom-call | flops 196608 | bytes 1572864 | tf_op jit(solution)/shard_map/pallas_call | solution.py:173
  121.2 1.0 broadcast_multiply_fusion.1
  122.4 11.7 %fusion.2 = f32[12,32,768]{2,1,0:T(8,128)S(1)} fusion(f32[12,32,256]{2,1,0:T(8,128)S(1)} %div.15, f32[1,12,768,256]{3,2,1,0:T(8,128)} %param.6, bf16[1,12,768,256]{3,2,1,0:T(8,128)(2,1)} %param.5), kind=kOutput, calls=%fused_computation.3 | convolution fusion | flops 910688256 | bytes 15728640 | tf_op jit(solution)/shard_map/kdf,krf->krd/dot_general | solution.py:363
  134.0 1.4 reshape.79.x_ref
  135.5 39.8 %shard_map.94 = f32[2,4,4,4,18,128]{5,4,3,2,1,0:T(8,128)} custom-call(f32[2,4,4,4,18,128]{5,4,3,2,1,0:T(8,128)} %reshape.79.x_ref), custom_call_target="tpu_custom_call" | custom-call | flops 589824 | bytes 4718592 | tf_op jit(solution)/shard_map/pallas_call | solution.py:173
  175.3 1.9 reshape.80
  177.2 1.3 select_reduce_fusion
  178.5 0.4 fusion.25
  179.0 0.5 fusion.24
  179.5 0.3 fusion.23
  179.8 0.4 fusion.22
  180.6 0.4 fusion.19
  181.0 0.5 fusion.17
  181.6 0.5 fusion.12
  182.1 0.4 fusion.21
  182.4 0.3 fusion.18
  182.8 0.3 fusion.16
  183.1 0.3 convolution_multiply_fusion
  183.4 1.1 fusion.119
  184.6 8.5 %fusion = f32[12,32,256]{2,1,0:T(8,128)S(1)} fusion(f32[12,32,768]{2,1,0:T(8,128)S(1)} %fusion.119, f32[1,12,768,256]{3,2,1,0:T(8,128)} %param.6, bf16[1,12,768,256]{3,2,1,0:T(8,128)(2,1)S(1)} %bitcast.65), kind=kOutput, calls=%fused_computation.1 | convolution fusion | flops 910688256 | bytes 15728640 | tf_op jit(solution)/shard_map/kdf,krd->krf/dot_general | solution.py:368
  193.1 0.8 reshape.81.x_ref
  193.8 23.3 %shard_map.95 = f32[4,4,48,128]{3,2,1,0:T(8,128)} custom-call(f32[4,4,48,128]{3,2,1,0:T(8,128)} %reshape.81.x_ref), custom_call_target="tpu_custom_call" | custom-call | flops 196608 | bytes 1572864 | tf_op jit(solution)/shard_map/pallas_call | solution.py:173
  217.1 1.0 broadcast_multiply_fusion
  218.3 1.4 fusion.14
  219.8 0.9 constant_dynamic-slice_fusion
  220.6 13.5 %shard_map.96 = (f32[72,2048]{1,0:T(8,128)}, f32[72,2048]{1,0:T(8,128)}) custom-call(f32[8,72,256]{2,1,0:T(8,128)} %bitcast.68, f32[72,2048]{1,0:T(8,128)} %mom_ref.1, f32[72,2048]{1,0:T(8,128)} %master_ref.1), custom_call_target="tpu_custom_call" | custom-call | flops 589824 | bytes 2949120 | tf_op jit(solution)/shard_map/pallas_call | solution.py:286
  234.2 18.7 %subtract_convert_fusion = (bf16[12,768,256]{2,1,0:T(8,128)(2,1)}, f32[1,12,768,256]{3,2,1,0:T(8,128)}) fusion(f32[12,768,256]{2,1,0:T(8,128)} %bitcast.66, f32[1,12,768,256]{3,2,1,0:T(8,128)} %param.6, bf16[1,12,768,256]{3,2,1,0:T(8,128)(2,1)} %param.5, f32[12,32,768]{2,1,0:T(8,128)S(1)} %fusion.119, f32[12,32,256]{2,1,0:T(8,128)S(1)} %div.17), kind=kOutput, calls=%fused_computation.10 | convolution fusion | flops 920125440 | bytes 39321600 | tf_op jit(solution)/shard_map/krd,krf->kdf/dot_general | solution.py:372
  252.9 0.8 copy.12
  253.7 0.8 copy.13
  (33 shorter events, 1.7 us)
Async XLA Ops:
  7.2 16.7 %copy-start = (f32[12,32,256]{2,1,0:T(8,128)S(1)}, f32[12,32,256]{2,1,0:T(8,128)}, u32[]{:S(2)}) copy-start(f32[12,32,256]{2,1,0:T(8,128)} %param.7) | copy-start | bytes 1179652
  7.2 227.0 %all-gather.2.cloned.1.call-start = ((), (), s32[]{:S(2)}) async-start(), calls=%async_computation | async-start | bytes 10027008 | tf_op jit(solution)/shard_map/all_gather | solution.py:359
  79.8 9.1 %slice-start = ((s8[4718592]{0:T(1024)(128)(4,1)}), s8[524288]{0:T(1024)(128)(4,1)S(1)}, s32[]{:S(2)}) async-start(s8[4718592]{0:T(1024)(128)(4,1)} %bitcast.62), calls=%async_computation.1 | async-start | bytes 1048576
  84.2 4.8 %slice-start.1 = ((s8[4718592]{0:T(1024)(128)(4,1)}), s8[4194304]{0:T(1024)(128)(4,1)S(1)}, s32[]{:S(2)}) async-start(s8[4718592]{0:T(1024)(128)(4,1)} %bitcast.62), calls=%async_computation.2 | async-start | bytes 8388608
  175.3 9.3 %slice-start.2 = ((s8[4718592]{0:T(1024)(128)(4,1)}), s8[524288]{0:T(1024)(128)(4,1)S(1)}, s32[]{:S(2)}) async-start(s8[4718592]{0:T(1024)(128)(4,1)} %bitcast.64), calls=%async_computation.3 | async-start | bytes 1048576
  179.8 4.8 %slice-start.3 = ((s8[4718592]{0:T(1024)(128)(4,1)}), s8[4194304]{0:T(1024)(128)(4,1)S(1)}, s32[]{:S(2)}) async-start(s8[4718592]{0:T(1024)(128)(4,1)} %bitcast.64), calls=%async_computation.4 | async-start | bytes 8388608
  218.3 34.6 %copy-start.2 = (f32[12,32,256]{2,1,0:T(8,128)}, f32[12,32,256]{2,1,0:T(8,128)S(1)}, u32[]{:S(2)}) copy-start(f32[12,32,256]{2,1,0:T(8,128)S(1)} %div.17) | copy-start | bytes 1179652
  234.1 18.7 %copy-start.4 = (f32[72,2048]{1,0:T(8,128)S(1)}, f32[72,2048]{1,0:T(8,128)}, u32[]{:S(2)}) copy-start(f32[72,2048]{1,0:T(8,128)} %get-tuple-element.26) | copy-start | bytes 1769476
  234.2 19.5 %copy-start.3 = (f32[72,2048]{1,0:T(8,128)S(1)}, f32[72,2048]{1,0:T(8,128)}, u32[]{:S(2)}) copy-start(f32[72,2048]{1,0:T(8,128)} %get-tuple-element.27) | copy-start | bytes 1769476
  234.2 20.3 %copy-start.1 = (f32[12,32,256]{2,1,0:T(8,128)S(1)}, f32[12,32,256]{2,1,0:T(8,128)}, u32[]{:S(2)}) copy-start(f32[12,32,256]{2,1,0:T(8,128)} %param.7) | copy-start | bytes 1179652
Sparse Core Ops, SparseCore 0:
  23.9 78.3 all-gather.1

commit v11 on v9

--- a/solution.py
+++ b/solution.py
@@ -358,7 +358,7 @@
     kept_cols = kept_cols.reshape(-1, kept_cols.shape[-1])
     kept_all = lax.all_gather(kept_cols, "rep", axis=0, tiled=True)
     rep_only = (("rep", replicas, 1),)
-    both = split_levels("tp", lax.axis_size("tp"), 2) + split_levels("rep", replicas, 4)
+    both = split_levels("tp", lax.axis_size("tp"), 2)[::-1] + split_levels("rep", replicas, 4)
     for power_pass in range(ROUNDS):
         partial_factor = jnp.einsum(
             "kdf,krf->krd", corrected, current, precision=lax.Precision.HIGHEST

time: 255 us -> 282 us (1.11)
  Pallas kernels: 149 us -> 176 us
    pallas_call x4, Pallas kernels: 119 us -> 146 us  [allreduce(): pl.pallas_call(functools.partial(_allreduce_kernel, tuple(levels), direct...]
  transfers between devices with their start and end apart: 1 -> 1, of which waited for: 0 -> 0; matrix products, arithmetic and copies ran while one was open for 27% -> 24% of each run, Pallas kernels for 53% -> 58%
where the time goes in v11:
time: 282 us; the launch traced here: 281 us
  Pallas kernels  176 us (62%)
  matrix products  75.5 us (27%)
  between operations  14.5 us (5%)
  local copies, waits for them, and re-layouts  10.7 us (4%)
  other arithmetic  4.25 us (2%)
    pallas_call x4, Pallas kernels, allreduce(): pl.pallas_call(functools.partial(_allreduce_kernel, tuple(levels), direct...  146 us
    dot_general x2, matrix products, local(): jnp.einsum('kdf,krf->krd', corrected, current, precision=lax.Precision.HI...  23.8 us
    dot_general x1, matrix products, local(): jnp.einsum('krd,krf->kdf', ortho_basis, current, precision=lax.Precision....  18.7 us
    dot_general x2, matrix products, local(): jnp.einsum('kdf,krd->krf', corrected, ortho_basis, precision=lax.Precisio...  17.1 us
    pallas_call x1, Pallas kernels, flat_update(): pl.pallas_call(_update_kernel, out_shape=(jax.ShapeDtypeStruct(momentum.s...  16 us
    pallas_call x1, Pallas kernels, by_columns(): pl.pallas_call(_columns_kernel, out_shape=jax.ShapeDtypeStruct((n, rows,...  14.4 us
    dot_general x16, matrix products, orthonormal_by_gram(): jnp.einsum('krs,kst,kut->kru', step, gram_now, step, precision=hi)  6.91 us
  transfers between devices with their start and end apart: 1, of which 0 were waited for; matrix products, arithmetic and copies ran while one was open for 24% of the time, Pallas kernels for 58%

profile of v11, /device:TPU:1, one launch (start us, length us, event | category | flops | bytes accessed | tf_op | source)
XLA Modules:
  0.0 281.3 jit_solution(10453918248173869532)
XLA Ops:
  7.2 2.2 multiply_subtract_fusion.x_ref
  9.4 14.4 %shard_map.97 = f32[8,72,256]{2,1,0:T(8,128)} custom-call(f32[72,2048]{1,0:T(8,128)} %multiply_subtract_fusion.x_ref), custom_call_target="tpu_custom_call" | custom-call | bytes 1179648 | tf_op jit(solution)/shard_map/pallas_call | solution.py:264
  23.8 12.2 %fusion.9 = f32[12,32,768]{2,1,0:T(8,128)S(1)} fusion(f32[12,32,256]{2,1,0:T(8,128)S(1)} %copy-done, f32[1,12,768,256]{3,2,1,0:T(8,128)} %param.6, bf16[1,12,768,256]{3,2,1,0:T(8,128)(2,1)} %param.5), kind=kOutput, calls=%fused_computation.12 | convolution fusion | flops 910688256 | bytes 15728640 | tf_op jit(solution)/shard_map/kdf,krf->krd/dot_general | solution.py:363
  36.0 1.4 reshape.76.x_ref
  37.4 59.5 %shard_map.92 = f32[4,2,4,4,18,128]{5,4,3,2,1,0:T(8,128)} custom-call(f32[4,2,4,4,18,128]{5,4,3,2,1,0:T(8,128)} %reshape.76.x_ref), custom_call_target="tpu_custom_call" | custom-call | flops 589824 | bytes 4718592 | tf_op jit(solution)/shard_map/pallas_call | solution.py:173
  97.0 1.7 reshape.77
  98.7 1.3 select_reduce_fusion.1
  100.0 0.4 fusion.35
  100.4 0.5 fusion.34
  101.3 0.4 fusion.32
  102.1 0.4 fusion.29
  102.5 0.5 fusion.27
  103.0 0.5 fusion.13
  103.5 0.4 fusion.31
  103.9 0.3 fusion.28
  104.2 0.3 fusion.26
  104.9 1.1 fusion.118
  106.0 8.7 %fusion.4 = f32[12,32,256]{2,1,0:T(8,128)S(1)} fusion(f32[12,32,768]{2,1,0:T(8,128)S(1)} %fusion.118, f32[1,12,768,256]{3,2,1,0:T(8,128)} %param.6, bf16[1,12,768,256]{3,2,1,0:T(8,128)(2,1)S(1)} %bitcast.59), kind=kOutput, calls=%fused_computation.5 | convolution fusion | flops 910688256 | bytes 15728640 | tf_op jit(solution)/shard_map/kdf,krd->krf/dot_general | solution.py:368
  114.7 0.8 reshape.78.x_ref
  115.5 17.4 %shard_map.93 = f32[16,48,128]{2,1,0:T(8,128)} custom-call(f32[16,48,128]{2,1,0:T(8,128)} %reshape.78.x_ref), custom_call_target="tpu_custom_call" | custom-call | flops 196608 | bytes 1572864 | tf_op jit(solution)/shard_map/pallas_call | solution.py:173
  132.9 1.0 broadcast_multiply_fusion.1
  134.1 11.7 %fusion.2 = f32[12,32,768]{2,1,0:T(8,128)S(1)} fusion(f32[12,32,256]{2,1,0:T(8,128)S(1)} %div.15, f32[1,12,768,256]{3,2,1,0:T(8,128)} %param.6, bf16[1,12,768,256]{3,2,1,0:T(8,128)(2,1)} %param.5), kind=kOutput, calls=%fused_computation.3 | convolution fusion | flops 910688256 | bytes 15728640 | tf_op jit(solution)/shard_map/kdf,krf->krd/dot_general | solution.py:363
  145.8 1.4 reshape.79.x_ref
  147.2 52.4 %shard_map.94 = f32[4,2,4,4,18,128]{5,4,3,2,1,0:T(8,128)} custom-call(f32[4,2,4,4,18,128]{5,4,3,2,1,0:T(8,128)} %reshape.79.x_ref), custom_call_target="tpu_custom_call" | custom-call | flops 589824 | bytes 4718592 | tf_op jit(solution)/shard_map/pallas_call | solution.py:173
  199.6 1.9 reshape.80
  201.5 1.3 select_reduce_fusion
  202.8 0.4 fusion.25
  203.3 0.5 fusion.24
  204.1 0.4 fusion.22
  204.6 0.3 fusion.20
  204.9 0.4 fusion.19
  205.3 0.5 fusion.17
  205.9 0.5 fusion.12
  206.4 0.4 fusion.21
  206.8 0.3 fusion.18
  207.1 0.3 fusion.16
  207.4 0.3 convolution_multiply_fusion
  207.7 1.1 fusion.119
  208.9 8.5 %fusion = f32[12,32,256]{2,1,0:T(8,128)S(1)} fusion(f32[12,32,768]{2,1,0:T(8,128)S(1)} %fusion.119, f32[1,12,768,256]{3,2,1,0:T(8,128)} %param.6, bf16[1,12,768,256]{3,2,1,0:T(8,128)(2,1)S(1)} %bitcast.61), kind=kOutput, calls=%fused_computation.1 | convolution fusion | flops 910688256 | bytes 15728640 | tf_op jit(solution)/shard_map/kdf,krd->krf/dot_general | solution.py:368
  217.3 0.8 reshape.81.x_ref
  218.1 16.5 %shard_map.95 = f32[16,48,128]{2,1,0:T(8,128)} custom-call(f32[16,48,128]{2,1,0:T(8,128)} %reshape.81.x_ref), custom_call_target="tpu_custom_call" | custom-call | flops 196608 | bytes 1572864 | tf_op jit(solution)/shard_map/pallas_call | solution.py:173
  234.6 1.0 broadcast_multiply_fusion
  235.8 1.4 fusion.14
  237.2 0.9 constant_dynamic-slice_fusion
  238.1 16.0 %shard_map.96 = (f32[72,2048]{1,0:T(8,128)}, f32[72,2048]{1,0:T(8,128)}) custom-call(f32[8,72,256]{2,1,0:T(8,128)} %bitcast.64, f32[72,2048]{1,0:T(8,128)} %mom_ref.1, f32[72,2048]{1,0:T(8,128)} %master_ref.1), custom_call_target="tpu_custom_call" | custom-call | flops 589824 | bytes 2949120 | tf_op jit(solution)/shard_map/pallas_call | solution.py:286
  254.1 18.7 %subtract_convert_fusion = (bf16[12,768,256]{2,1,0:T(8,128)(2,1)}, f32[1,12,768,256]{3,2,1,0:T(8,128)}) fusion(f32[12,768,256]{2,1,0:T(8,128)} %bitcast.62, f32[1,12,768,256]{3,2,1,0:T(8,128)} %param.6, bf16[1,12,768,256]{3,2,1,0:T(8,128)(2,1)} %param.5, f32[12,32,768]{2,1,0:T(8,128)S(1)} %fusion.119, f32[12,32,256]{2,1,0:T(8,128)S(1)} %div.17), kind=kOutput, calls=%fused_computation.10 | convolution fusion | flops 920125440 | bytes 39321600 | tf_op jit(solution)/shard_map/krd,krf->kdf/dot_general | solution.py:372
  272.8 0.8 copy.12
  273.7 0.8 copy.13
  (33 shorter events, 1.7 us)
Async XLA Ops:
  7.2 16.7 %copy-start = (f32[12,32,256]{2,1,0:T(8,128)S(1)}, f32[12,32,256]{2,1,0:T(8,128)}, u32[]{:S(2)}) copy-start(f32[12,32,256]{2,1,0:T(8,128)} %param.7) | copy-start | bytes 1179652
  7.2 246.9 %all-gather.2.cloned.1.call-start = ((), (), s32[]{:S(2)}) async-start(), calls=%async_computation | async-start | bytes 10027008 | tf_op jit(solution)/shard_map/all_gather | solution.py:359
  97.0 9.1 %slice-start = ((s8[4718592]{0:T(1024)(128)(4,1)}), s8[524288]{0:T(1024)(128)(4,1)S(1)}, s32[]{:S(2)}) async-start(s8[4718592]{0:T(1024)(128)(4,1)} %bitcast.58), calls=%async_computation.1 | async-start | bytes 1048576
  101.3 4.8 %slice-start.1 = ((s8[4718592]{0:T(1024)(128)(4,1)}), s8[4194304]{0:T(1024)(128)(4,1)S(1)}, s32[]{:S(2)}) async-start(s8[4718592]{0:T(1024)(128)(4,1)} %bitcast.58), calls=%async_computation.2 | async-start | bytes 8388608
  199.6 9.2 %slice-start.2 = ((s8[4718592]{0:T(1024)(128)(4,1)}), s8[524288]{0:T(1024)(128)(4,1)S(1)}, s32[]{:S(2)}) async-start(s8[4718592]{0:T(1024)(128)(4,1)} %bitcast.60), calls=%async_computation.3 | async-start | bytes 1048576
  204.1 4.8 %slice-start.3 = ((s8[4718592]{0:T(1024)(128)(4,1)}), s8[4194304]{0:T(1024)(128)(4,1)S(1)}, s32[]{:S(2)}) async-start(s8[4718592]{0:T(1024)(128)(4,1)} %bitcast.60), calls=%async_computation.4 | async-start | bytes 8388608
  235.8 37.1 %copy-start.2 = (f32[12,32,256]{2,1,0:T(8,128)}, f32[12,32,256]{2,1,0:T(8,128)S(1)}, u32[]{:S(2)}) copy-start(f32[12,32,256]{2,1,0:T(8,128)S(1)} %div.17) | copy-start | bytes 1179652
  254.1 18.7 %copy-start.4 = (f32[72,2048]{1,0:T(8,128)S(1)}, f32[72,2048]{1,0:T(8,128)}, u32[]{:S(2)}) copy-start(f32[72,2048]{1,0:T(8,128)} %get-tuple-element.26) | copy-start | bytes 1769476
  254.1 19.5 %copy-start.3 = (f32[72,2048]{1,0:T(8,128)S(1)}, f32[72,2048]{1,0:T(8,128)}, u32[]{:S(2)}) copy-start(f32[72,2048]{1,0:T(8,128)} %get-tuple-element.27) | copy-start | bytes 1769476
  254.1 20.3 %copy-start.1 = (f32[12,32,256]{2,1,0:T(8,128)S(1)}, f32[12,32,256]{2,1,0:T(8,128)}, u32[]{:S(2)}) copy-start(f32[12,32,256]{2,1,0:T(8,128)} %param.7) | copy-start | bytes 1179652
Sparse Core Ops, SparseCore 0:
  23.9 79.8 all-gather.1

commit v12 on v9

--- a/solution.py
+++ b/solution.py
@@ -73,9 +73,10 @@
                 device_id=_peer(levels[lev], j), device_id_type=pl.DeviceIdType.MESH)
             cp.start()
             copies.append((j, off, cp))
-        own = pltpu.make_async_copy(piece(m), recv[lev].at[m], local_sem.at[0])
-        own.start()
-        own.wait()
+        if last_direct:
+            own = pltpu.make_async_copy(piece(m), recv[lev].at[m], local_sem.at[0])
+            own.start()
+            own.wait()
         for j, off, cp in copies:
             pltpu.make_async_remote_copy(
                 src_ref=piece(j), dst_ref=recv[lev].at[j],
@@ -96,23 +97,33 @@
             for d in lead:
                 count *= d
 
-            def body(i, carry, r=r, dst=dst, n=n, lead=lead):
+            def body(i, carry, r=r, dst=dst, n=n, lead=lead, src=src, m=m, last_direct=last_direct):
                 idx = []
                 rest = i
                 for d in reversed(lead):
                     idx.append(lax.rem(rest, d))
                     rest = lax.div(rest, d)
                 idx = tuple(reversed(idx))
-                acc = r[(0,) + idx]
-                for j in range(1, n):
-                    acc = acc + r[(j,) + idx]
+                if last_direct:
+                    acc = r[(0,) + idx]
+                    for j in range(1, n):
+                        acc = acc + r[(j,) + idx]
+                else:
+                    acc = src[(m,) + idx]
+                    for off in range(1, n):
+                        acc = acc + r[(lax.rem(m + off, n),) + idx]
                 dst[idx] = acc
                 return carry
             lax.fori_loop(0, count, body, 0)
-        else:
+        elif last_direct:
             acc = r[0]
             for j in range(1, n):
                 acc = acc + r[j]
+            dst[...] = acc
+        else:
+            acc = src[m]
+            for off in range(1, n):
+                acc = acc + r[lax.rem(m + off, n)]
             dst[...] = acc
         if lev < n_lev - 1:
             src = sums[lev]

time: 255 us -> 255 us (level)
  no operation moved by 1% of the time
where the time goes in v12:
time: 255 us; the launch traced here: 254 us
  Pallas kernels  149 us (58%)
  matrix products  75.7 us (30%)
  between operations  14.6 us (6%)
  local copies, waits for them, and re-layouts  10.8 us (4%)
  other arithmetic  4.25 us (2%)
    pallas_call x4, Pallas kernels, allreduce(): pl.pallas_call(functools.partial(_allreduce_kernel, tuple(levels), direct...  119 us
    dot_general x2, matrix products, local(): jnp.einsum('kdf,krf->krd', corrected, current, precision=lax.Precision.HI...  23.8 us
    dot_general x1, matrix products, local(): jnp.einsum('krd,krf->kdf', ortho_basis, current, precision=lax.Precision....  18.7 us
    dot_general x2, matrix products, local(): jnp.einsum('kdf,krd->krf', corrected, ortho_basis, precision=lax.Precisio...  17.3 us
    pallas_call x1, Pallas kernels, flat_update(): pl.pallas_call(_update_kernel, out_shape=(jax.ShapeDtypeStruct(momentum.s...  15.3 us
    pallas_call x1, Pallas kernels, by_columns(): pl.pallas_call(_columns_kernel, out_shape=jax.ShapeDtypeStruct((n, rows,...  14.4 us
    dot_general x16, matrix products, orthonormal_by_gram(): jnp.einsum('krs,kst,kut->kru', step, gram_now, step, precision=hi)  6.9 us
  transfers between devices with their start and end apart: 1, of which 0 were waited for; matrix products, arithmetic and copies ran while one was open for 27% of the time, Pallas kernels for 53%

profile of v12, /device:TPU:1, one launch (start us, length us, event | category | flops | bytes accessed | tf_op | source)
XLA Modules:
  0.0 254.4 jit_solution(14652717320892523632)
XLA Ops:
  7.2 2.2 multiply_subtract_fusion.x_ref
  9.4 14.4 %shard_map.97 = f32[8,72,256]{2,1,0:T(8,128)} custom-call(f32[72,2048]{1,0:T(8,128)} %multiply_subtract_fusion.x_ref), custom_call_target="tpu_custom_call" | custom-call | bytes 1179648 | tf_op jit(solution)/shard_map/pallas_call | solution.py:275
  23.8 12.2 %fusion.9 = f32[12,32,768]{2,1,0:T(8,128)S(1)} fusion(f32[12,32,256]{2,1,0:T(8,128)S(1)} %copy-done, f32[1,12,768,256]{3,2,1,0:T(8,128)} %param.6, bf16[1,12,768,256]{3,2,1,0:T(8,128)(2,1)} %param.5), kind=kOutput, calls=%fused_computation.12 | convolution fusion | flops 910688256 | bytes 15728640 | tf_op jit(solution)/shard_map/kdf,krf->krd/dot_general | solution.py:374
  36.0 1.4 reshape.76.x_ref
  37.4 42.5 %shard_map.92 = f32[2,4,4,4,18,128]{5,4,3,2,1,0:T(8,128)} custom-call(f32[2,4,4,4,18,128]{5,4,3,2,1,0:T(8,128)} %reshape.76.x_ref), custom_call_target="tpu_custom_call" | custom-call | flops 589824 | bytes 4718592 | tf_op jit(solution)/shard_map/pallas_call | solution.py:184
  79.9 1.7 reshape.77
  81.7 1.3 select_reduce_fusion.1
  83.0 0.4 fusion.35
  83.4 0.5 fusion.34
  84.3 0.4 fusion.32
  85.1 0.4 fusion.29
  85.5 0.5 fusion.27
  86.0 0.5 fusion.13
  86.5 0.4 fusion.31
  86.9 0.3 fusion.28
  87.3 0.3 fusion.26
  87.9 1.1 fusion.118
  89.1 8.8 %fusion.4 = f32[12,32,256]{2,1,0:T(8,128)S(1)} fusion(f32[12,32,768]{2,1,0:T(8,128)S(1)} %fusion.118, f32[1,12,768,256]{3,2,1,0:T(8,128)} %param.6, bf16[1,12,768,256]{3,2,1,0:T(8,128)(2,1)S(1)} %bitcast.59), kind=kOutput, calls=%fused_computation.5 | convolution fusion | flops 910688256 | bytes 15728640 | tf_op jit(solution)/shard_map/kdf,krd->krf/dot_general | solution.py:379
  97.9 0.8 reshape.78.x_ref
  98.7 19.2 %shard_map.93 = f32[16,48,128]{2,1,0:T(8,128)} custom-call(f32[16,48,128]{2,1,0:T(8,128)} %reshape.78.x_ref), custom_call_target="tpu_custom_call" | custom-call | flops 196608 | bytes 1572864 | tf_op jit(solution)/shard_map/pallas_call | solution.py:184
  117.8 1.0 broadcast_multiply_fusion.1
  119.0 11.7 %fusion.2 = f32[12,32,768]{2,1,0:T(8,128)S(1)} fusion(f32[12,32,256]{2,1,0:T(8,128)S(1)} %div.15, f32[1,12,768,256]{3,2,1,0:T(8,128)} %param.6, bf16[1,12,768,256]{3,2,1,0:T(8,128)(2,1)} %param.5), kind=kOutput, calls=%fused_computation.3 | convolution fusion | flops 910688256 | bytes 15728640 | tf_op jit(solution)/shard_map/kdf,krf->krd/dot_general | solution.py:374
  130.7 1.4 reshape.79.x_ref
  132.1 40.4 %shard_map.94 = f32[2,4,4,4,18,128]{5,4,3,2,1,0:T(8,128)} custom-call(f32[2,4,4,4,18,128]{5,4,3,2,1,0:T(8,128)} %reshape.79.x_ref), custom_call_target="tpu_custom_call" | custom-call | flops 589824 | bytes 4718592 | tf_op jit(solution)/shard_map/pallas_call | solution.py:184
  172.6 1.9 reshape.80
  174.5 1.3 select_reduce_fusion
  175.8 0.4 fusion.25
  176.2 0.5 fusion.24
  177.1 0.4 fusion.22
  177.5 0.3 fusion.20
  177.8 0.4 fusion.19
  178.3 0.5 fusion.17
  178.8 0.5 fusion.12
  179.3 0.4 fusion.21
  179.7 0.3 fusion.18
  180.0 0.3 fusion.16
  180.4 0.3 convolution_multiply_fusion
  180.7 1.1 fusion.119
  181.8 8.5 %fusion = f32[12,32,256]{2,1,0:T(8,128)S(1)} fusion(f32[12,32,768]{2,1,0:T(8,128)S(1)} %fusion.119, f32[1,12,768,256]{3,2,1,0:T(8,128)} %param.6, bf16[1,12,768,256]{3,2,1,0:T(8,128)(2,1)S(1)} %bitcast.61), kind=kOutput, calls=%fused_computation.1 | convolution fusion | flops 910688256 | bytes 15728640 | tf_op jit(solution)/shard_map/kdf,krd->krf/dot_general | solution.py:379
  190.3 0.8 reshape.81.x_ref
  191.1 17.3 %shard_map.95 = f32[16,48,128]{2,1,0:T(8,128)} custom-call(f32[16,48,128]{2,1,0:T(8,128)} %reshape.81.x_ref), custom_call_target="tpu_custom_call" | custom-call | flops 196608 | bytes 1572864 | tf_op jit(solution)/shard_map/pallas_call | solution.py:184
  208.4 1.0 broadcast_multiply_fusion
  209.6 1.4 fusion.14
  211.0 0.9 constant_dynamic-slice_fusion
  211.9 15.3 %shard_map.96 = (f32[72,2048]{1,0:T(8,128)}, f32[72,2048]{1,0:T(8,128)}) custom-call(f32[8,72,256]{2,1,0:T(8,128)} %bitcast.64, f32[72,2048]{1,0:T(8,128)} %mom_ref.1, f32[72,2048]{1,0:T(8,128)} %master_ref.1), custom_call_target="tpu_custom_call" | custom-call | flops 589824 | bytes 2949120 | tf_op jit(solution)/shard_map/pallas_call | solution.py:297
  227.3 18.7 %subtract_convert_fusion = (bf16[12,768,256]{2,1,0:T(8,128)(2,1)}, f32[1,12,768,256]{3,2,1,0:T(8,128)}) fusion(f32[12,768,256]{2,1,0:T(8,128)} %bitcast.62, f32[1,12,768,256]{3,2,1,0:T(8,128)} %param.6, bf16[1,12,768,256]{3,2,1,0:T(8,128)(2,1)} %param.5, f32[12,32,768]{2,1,0:T(8,128)S(1)} %fusion.119, f32[12,32,256]{2,1,0:T(8,128)S(1)} %div.17), kind=kOutput, calls=%fused_computation.10 | convolution fusion | flops 920125440 | bytes 39321600 | tf_op jit(solution)/shard_map/krd,krf->kdf/dot_general | solution.py:383
  246.0 0.8 copy.12
  246.8 0.8 copy.13
  (33 shorter events, 1.7 us)
Async XLA Ops:
  7.2 16.7 %copy-start = (f32[12,32,256]{2,1,0:T(8,128)S(1)}, f32[12,32,256]{2,1,0:T(8,128)}, u32[]{:S(2)}) copy-start(f32[12,32,256]{2,1,0:T(8,128)} %param.7) | copy-start | bytes 1179652
  7.2 220.0 %all-gather.2.cloned.1.call-start = ((), (), s32[]{:S(2)}) async-start(), calls=%async_computation | async-start | bytes 10027008 | tf_op jit(solution)/shard_map/all_gather | solution.py:370
  79.9 9.1 %slice-start = ((s8[4718592]{0:T(1024)(128)(4,1)}), s8[524288]{0:T(1024)(128)(4,1)S(1)}, s32[]{:S(2)}) async-start(s8[4718592]{0:T(1024)(128)(4,1)} %bitcast.58), calls=%async_computation.1 | async-start | bytes 1048576
  84.3 4.8 %slice-start.1 = ((s8[4718592]{0:T(1024)(128)(4,1)}), s8[4194304]{0:T(1024)(128)(4,1)S(1)}, s32[]{:S(2)}) async-start(s8[4718592]{0:T(1024)(128)(4,1)} %bitcast.58), calls=%async_computation.2 | async-start | bytes 8388608
  172.5 9.2 %slice-start.2 = ((s8[4718592]{0:T(1024)(128)(4,1)}), s8[524288]{0:T(1024)(128)(4,1)S(1)}, s32[]{:S(2)}) async-start(s8[4718592]{0:T(1024)(128)(4,1)} %bitcast.60), calls=%async_computation.3 | async-start | bytes 1048576
  177.0 4.8 %slice-start.3 = ((s8[4718592]{0:T(1024)(128)(4,1)}), s8[4194304]{0:T(1024)(128)(4,1)S(1)}, s32[]{:S(2)}) async-start(s8[4718592]{0:T(1024)(128)(4,1)} %bitcast.60), calls=%async_computation.4 | async-start | bytes 8388608
  209.5 36.4 %copy-start.2 = (f32[12,32,256]{2,1,0:T(8,128)}, f32[12,32,256]{2,1,0:T(8,128)S(1)}, u32[]{:S(2)}) copy-start(f32[12,32,256]{2,1,0:T(8,128)S(1)} %div.17) | copy-start | bytes 1179652
  227.2 18.7 %copy-start.4 = (f32[72,2048]{1,0:T(8,128)S(1)}, f32[72,2048]{1,0:T(8,128)}, u32[]{:S(2)}) copy-start(f32[72,2048]{1,0:T(8,128)} %get-tuple-element.26) | copy-start | bytes 1769476
  227.2 19.5 %copy-start.3 = (f32[72,2048]{1,0:T(8,128)S(1)}, f32[72,2048]{1,0:T(8,128)}, u32[]{:S(2)}) copy-start(f32[72,2048]{1,0:T(8,128)} %get-tuple-element.27) | copy-start | bytes 1769476
  227.3 20.3 %copy-start.1 = (f32[12,32,256]{2,1,0:T(8,128)S(1)}, f32[12,32,256]{2,1,0:T(8,128)}, u32[]{:S(2)}) copy-start(f32[12,32,256]{2,1,0:T(8,128)} %param.7) | copy-start | bytes 1179652
Sparse Core Ops, SparseCore 0:
  23.9 78.3 all-gather.1

commit v13 on v12

--- a/solution.py
+++ b/solution.py
@@ -369,7 +369,7 @@
     kept_cols = kept_cols.reshape(-1, kept_cols.shape[-1])
     kept_all = lax.all_gather(kept_cols, "rep", axis=0, tiled=True)
     rep_only = (("rep", replicas, 1),)
-    both = split_levels("tp", lax.axis_size("tp"), 2) + split_levels("rep", replicas, 4)
+    both = split_levels("tp", lax.axis_size("tp"), 2) + split_levels("rep", replicas, 4)[::-1]
     for power_pass in range(ROUNDS):
         partial_factor = jnp.einsum(
             "kdf,krf->krd", corrected, current, precision=lax.Precision.HIGHEST

time: 255 us -> 255 us (level)
  no operation moved by 1% of the time
where the time goes in v13:
time: 255 us
  Pallas kernels  150 us (59%)
  matrix products  75.6 us (30%)
  between operations  14.6 us (6%)
  local copies, waits for them, and re-layouts  10.8 us (4%)
  other arithmetic  4.25 us (2%)
    pallas_call x4, Pallas kernels, allreduce(): pl.pallas_call(functools.partial(_allreduce_kernel, tuple(levels), direct...  120 us
    dot_general x2, matrix products, local(): jnp.einsum('kdf,krf->krd', corrected, current, precision=lax.Precision.HI...  23.8 us
    dot_general x1, matrix products, local(): jnp.einsum('krd,krf->kdf', ortho_basis, current, precision=lax.Precision....  18.7 us
    dot_general x2, matrix products, local(): jnp.einsum('kdf,krd->krf', corrected, ortho_basis, precision=lax.Precisio...  17.3 us
    pallas_call x1, Pallas kernels, flat_update(): pl.pallas_call(_update_kernel, out_shape=(jax.ShapeDtypeStruct(momentum.s...  14.9 us
    pallas_call x1, Pallas kernels, by_columns(): pl.pallas_call(_columns_kernel, out_shape=jax.ShapeDtypeStruct((n, rows,...  14.4 us
    dot_general x16, matrix products, orthonormal_by_gram(): jnp.einsum('krs,kst,kut->kru', step, gram_now, step, precision=hi)  6.9 us
  transfers between devices with their start and end apart: 1, of which 0 were waited for; matrix products, arithmetic and copies ran while one was open for 27% of the time, Pallas kernels for 53%

profile of v13, /device:TPU:1, one launch (start us, length us, event | category | flops | bytes accessed | tf_op | source)
XLA Modules:
  0.0 255.0 jit_solution(9786016261307106202)
XLA Ops:
  7.2 2.2 multiply_subtract_fusion.x_ref
  9.4 14.4 %shard_map.97 = f32[8,72,256]{2,1,0:T(8,128)} custom-call(f32[72,2048]{1,0:T(8,128)} %multiply_subtract_fusion.x_ref), custom_call_target="tpu_custom_call" | custom-call | bytes 1179648 | tf_op jit(solution)/shard_map/pallas_call | solution.py:275
  23.8 12.2 %fusion.9 = f32[12,32,768]{2,1,0:T(8,128)S(1)} fusion(f32[12,32,256]{2,1,0:T(8,128)S(1)} %copy-done, f32[1,12,768,256]{3,2,1,0:T(8,128)} %param.6, bf16[1,12,768,256]{3,2,1,0:T(8,128)(2,1)} %param.5), kind=kOutput, calls=%fused_computation.12 | convolution fusion | flops 910688256 | bytes 15728640 | tf_op jit(solution)/shard_map/kdf,krf->krd/dot_general | solution.py:374
  36.0 1.4 reshape.76.x_ref
  37.4 42.7 %shard_map.92 = f32[2,4,4,4,18,128]{5,4,3,2,1,0:T(8,128)} custom-call(f32[2,4,4,4,18,128]{5,4,3,2,1,0:T(8,128)} %reshape.76.x_ref), custom_call_target="tpu_custom_call" | custom-call | flops 589824 | bytes 4718592 | tf_op jit(solution)/shard_map/pallas_call | solution.py:184
  80.1 1.7 reshape.77
  81.8 1.3 select_reduce_fusion.1
  83.2 0.4 fusion.35
  83.6 0.5 fusion.34
  84.4 0.4 fusion.32
  84.9 0.3 fusion.30
  85.2 0.4 fusion.29
  85.7 0.5 fusion.27
  86.2 0.5 fusion.13
  86.7 0.4 fusion.31
  87.1 0.3 fusion.28
  87.4 0.3 fusion.26
  88.1 1.1 fusion.118
  89.2 8.8 %fusion.4 = f32[12,32,256]{2,1,0:T(8,128)S(1)} fusion(f32[12,32,768]{2,1,0:T(8,128)S(1)} %fusion.118, f32[1,12,768,256]{3,2,1,0:T(8,128)} %param.6, bf16[1,12,768,256]{3,2,1,0:T(8,128)(2,1)S(1)} %bitcast.59), kind=kOutput, calls=%fused_computation.5 | convolution fusion | flops 910688256 | bytes 15728640 | tf_op jit(solution)/shard_map/kdf,krd->krf/dot_general | solution.py:379
  98.0 0.8 reshape.78.x_ref
  98.8 19.7 %shard_map.93 = f32[16,48,128]{2,1,0:T(8,128)} custom-call(f32[16,48,128]{2,1,0:T(8,128)} %reshape.78.x_ref), custom_call_target="tpu_custom_call" | custom-call | flops 196608 | bytes 1572864 | tf_op jit(solution)/shard_map/pallas_call | solution.py:184
  118.5 1.0 broadcast_multiply_fusion.1
  119.6 11.7 %fusion.2 = f32[12,32,768]{2,1,0:T(8,128)S(1)} fusion(f32[12,32,256]{2,1,0:T(8,128)S(1)} %div.15, f32[1,12,768,256]{3,2,1,0:T(8,128)} %param.6, bf16[1,12,768,256]{3,2,1,0:T(8,128)(2,1)} %param.5), kind=kOutput, calls=%fused_computation.3 | convolution fusion | flops 910688256 | bytes 15728640 | tf_op jit(solution)/shard_map/kdf,krf->krd/dot_general | solution.py:374
  131.3 1.4 reshape.79.x_ref
  132.7 39.6 %shard_map.94 = f32[2,4,4,4,18,128]{5,4,3,2,1,0:T(8,128)} custom-call(f32[2,4,4,4,18,128]{5,4,3,2,1,0:T(8,128)} %reshape.79.x_ref), custom_call_target="tpu_custom_call" | custom-call | flops 589824 | bytes 4718592 | tf_op jit(solution)/shard_map/pallas_call | solution.py:184
  172.3 1.9 reshape.80
  174.2 1.3 select_reduce_fusion
  175.6 0.4 fusion.25
  176.0 0.5 fusion.24
  176.8 0.4 fusion.22
  177.6 0.4 fusion.19
  178.1 0.5 fusion.17
  178.6 0.5 fusion.12
  179.1 0.4 fusion.21
  179.5 0.3 fusion.18
  179.8 0.3 fusion.16
  180.1 0.3 convolution_multiply_fusion
  180.5 1.1 fusion.119
  181.6 8.5 %fusion = f32[12,32,256]{2,1,0:T(8,128)S(1)} fusion(f32[12,32,768]{2,1,0:T(8,128)S(1)} %fusion.119, f32[1,12,768,256]{3,2,1,0:T(8,128)} %param.6, bf16[1,12,768,256]{3,2,1,0:T(8,128)(2,1)S(1)} %bitcast.61), kind=kOutput, calls=%fused_computation.1 | convolution fusion | flops 910688256 | bytes 15728640 | tf_op jit(solution)/shard_map/kdf,krd->krf/dot_general | solution.py:379
  190.1 0.8 reshape.81.x_ref
  190.8 18.5 %shard_map.95 = f32[16,48,128]{2,1,0:T(8,128)} custom-call(f32[16,48,128]{2,1,0:T(8,128)} %reshape.81.x_ref), custom_call_target="tpu_custom_call" | custom-call | flops 196608 | bytes 1572864 | tf_op jit(solution)/shard_map/pallas_call | solution.py:184
  209.4 1.0 broadcast_multiply_fusion
  210.6 1.4 fusion.14
  212.0 0.9 constant_dynamic-slice_fusion
  212.9 14.9 %shard_map.96 = (f32[72,2048]{1,0:T(8,128)}, f32[72,2048]{1,0:T(8,128)}) custom-call(f32[8,72,256]{2,1,0:T(8,128)} %bitcast.64, f32[72,2048]{1,0:T(8,128)} %mom_ref.1, f32[72,2048]{1,0:T(8,128)} %master_ref.1), custom_call_target="tpu_custom_call" | custom-call | flops 589824 | bytes 2949120 | tf_op jit(solution)/shard_map/pallas_call | solution.py:297
  227.8 18.7 %subtract_convert_fusion = (bf16[12,768,256]{2,1,0:T(8,128)(2,1)}, f32[1,12,768,256]{3,2,1,0:T(8,128)}) fusion(f32[12,768,256]{2,1,0:T(8,128)} %bitcast.62, f32[1,12,768,256]{3,2,1,0:T(8,128)} %param.6, bf16[1,12,768,256]{3,2,1,0:T(8,128)(2,1)} %param.5, f32[12,32,768]{2,1,0:T(8,128)S(1)} %fusion.119, f32[12,32,256]{2,1,0:T(8,128)S(1)} %div.17), kind=kOutput, calls=%fused_computation.10 | convolution fusion | flops 920125440 | bytes 39321600 | tf_op jit(solution)/shard_map/krd,krf->kdf/dot_general | solution.py:383
  246.5 0.8 copy.12
  247.3 0.8 copy.13
  (33 shorter events, 1.7 us)
Async XLA Ops:
  7.2 16.7 %copy-start = (f32[12,32,256]{2,1,0:T(8,128)S(1)}, f32[12,32,256]{2,1,0:T(8,128)}, u32[]{:S(2)}) copy-start(f32[12,32,256]{2,1,0:T(8,128)} %param.7) | copy-start | bytes 1179652
  7.2 220.6 %all-gather.2.cloned.1.call-start = ((), (), s32[]{:S(2)}) async-start(), calls=%async_computation | async-start | bytes 10027008 | tf_op jit(solution)/shard_map/all_gather | solution.py:370
  80.1 9.1 %slice-start = ((s8[4718592]{0:T(1024)(128)(4,1)}), s8[524288]{0:T(1024)(128)(4,1)S(1)}, s32[]{:S(2)}) async-start(s8[4718592]{0:T(1024)(128)(4,1)} %bitcast.58), calls=%async_computation.1 | async-start | bytes 1048576
  84.4 4.8 %slice-start.1 = ((s8[4718592]{0:T(1024)(128)(4,1)}), s8[4194304]{0:T(1024)(128)(4,1)S(1)}, s32[]{:S(2)}) async-start(s8[4718592]{0:T(1024)(128)(4,1)} %bitcast.58), calls=%async_computation.2 | async-start | bytes 8388608
  172.3 9.3 %slice-start.2 = ((s8[4718592]{0:T(1024)(128)(4,1)}), s8[524288]{0:T(1024)(128)(4,1)S(1)}, s32[]{:S(2)}) async-start(s8[4718592]{0:T(1024)(128)(4,1)} %bitcast.60), calls=%async_computation.3 | async-start | bytes 1048576
  176.8 4.8 %slice-start.3 = ((s8[4718592]{0:T(1024)(128)(4,1)}), s8[4194304]{0:T(1024)(128)(4,1)S(1)}, s32[]{:S(2)}) async-start(s8[4718592]{0:T(1024)(128)(4,1)} %bitcast.60), calls=%async_computation.4 | async-start | bytes 8388608
  210.5 36.0 %copy-start.2 = (f32[12,32,256]{2,1,0:T(8,128)}, f32[12,32,256]{2,1,0:T(8,128)S(1)}, u32[]{:S(2)}) copy-start(f32[12,32,256]{2,1,0:T(8,128)S(1)} %div.17) | copy-start | bytes 1179652
  227.8 18.7 %copy-start.4 = (f32[72,2048]{1,0:T(8,128)S(1)}, f32[72,2048]{1,0:T(8,128)}, u32[]{:S(2)}) copy-start(f32[72,2048]{1,0:T(8,128)} %get-tuple-element.26) | copy-start | bytes 1769476
  227.8 19.5 %copy-start.3 = (f32[72,2048]{1,0:T(8,128)S(1)}, f32[72,2048]{1,0:T(8,128)}, u32[]{:S(2)}) copy-start(f32[72,2048]{1,0:T(8,128)} %get-tuple-element.27) | copy-start | bytes 1769476
  227.8 20.3 %copy-start.1 = (f32[12,32,256]{2,1,0:T(8,128)S(1)}, f32[12,32,256]{2,1,0:T(8,128)}, u32[]{:S(2)}) copy-start(f32[12,32,256]{2,1,0:T(8,128)} %param.7) | copy-start | bytes 1179652
Sparse Core Ops, SparseCore 0:
  23.9 78.5 all-gather.1

commit v14 on v12

--- a/solution.py
+++ b/solution.py
@@ -132,13 +132,7 @@
         name, n, _ = levels[lev]
         m = me[lev]
         buf = gath_bufs[lev]
-        if lev == n_lev - 1:
-            piece = buf.at[m]
-        else:
-            piece = gath_bufs[lev + 1]
-            own = pltpu.make_async_copy(piece, buf.at[m], local_sem.at[0])
-            own.start()
-            own.wait()
+        piece = buf.at[m] if lev == n_lev - 1 else gath_bufs[lev + 1]
         copies = []
         for off in range(1, n):
             j = lax.rem(m + off, n)
@@ -148,6 +142,10 @@
                 device_id=_peer(levels[lev], j), device_id_type=pl.DeviceIdType.MESH)
             cp.start()
             copies.append((j, off, cp))
+        if lev < n_lev - 1:
+            own = pltpu.make_async_copy(piece, buf.at[m], local_sem.at[0])
+            own.start()
+            own.wait()
         for j, off, cp in copies:
             pltpu.make_async_remote_copy(
                 src_ref=piece, dst_ref=buf.at[j],

time: 255 us -> 255 us (level)
  no operation moved by 1% of the time
where the time goes in v14:
time: 255 us; the launch traced here: 254 us
  Pallas kernels  149 us (58%)
  matrix products  75.6 us (30%)
  between operations  14.6 us (6%)
  local copies, waits for them, and re-layouts  10.8 us (4%)
  other arithmetic  4.25 us (2%)
    pallas_call x4, Pallas kernels, allreduce(): pl.pallas_call(functools.partial(_allreduce_kernel, tuple(levels), direct...  119 us
    dot_general x2, matrix products, local(): jnp.einsum('kdf,krf->krd', corrected, current, precision=lax.Precision.HI...  23.8 us
    dot_general x1, matrix products, local(): jnp.einsum('krd,krf->kdf', ortho_basis, current, precision=lax.Precision....  18.7 us
    dot_general x2, matrix products, local(): jnp.einsum('kdf,krd->krf', corrected, ortho_basis, precision=lax.Precisio...  17.3 us
    pallas_call x1, Pallas kernels, flat_update(): pl.pallas_call(_update_kernel, out_shape=(jax.ShapeDtypeStruct(momentum.s...  15.3 us
    pallas_call x1, Pallas kernels, by_columns(): pl.pallas_call(_columns_kernel, out_shape=jax.ShapeDtypeStruct((n, rows,...  14.4 us
    dot_general x16, matrix products, orthonormal_by_gram(): jnp.einsum('krs,kst,kut->kru', step, gram_now, step, precision=hi)  6.9 us
  transfers between devices with their start and end apart: 1, of which 0 were waited for; matrix products, arithmetic and copies ran while one was open for 27% of the time, Pallas kernels for 53%

profile of v14, /device:TPU:1, one launch (start us, length us, event | category | flops | bytes accessed | tf_op | source)
XLA Modules:
  0.0 254.2 jit_solution(13161431965350067759)
XLA Ops:
  7.2 2.2 multiply_subtract_fusion.x_ref
  9.4 14.4 %shard_map.97 = f32[8,72,256]{2,1,0:T(8,128)} custom-call(f32[72,2048]{1,0:T(8,128)} %multiply_subtract_fusion.x_ref), custom_call_target="tpu_custom_call" | custom-call | bytes 1179648 | tf_op jit(solution)/shard_map/pallas_call | solution.py:273
  23.8 12.2 %fusion.9 = f32[12,32,768]{2,1,0:T(8,128)S(1)} fusion(f32[12,32,256]{2,1,0:T(8,128)S(1)} %copy-done, f32[1,12,768,256]{3,2,1,0:T(8,128)} %param.6, bf16[1,12,768,256]{3,2,1,0:T(8,128)(2,1)} %param.5), kind=kOutput, calls=%fused_computation.12 | convolution fusion | flops 910688256 | bytes 15728640 | tf_op jit(solution)/shard_map/kdf,krf->krd/dot_general | solution.py:372
  36.0 1.4 reshape.76.x_ref
  37.4 42.4 %shard_map.92 = f32[2,4,4,4,18,128]{5,4,3,2,1,0:T(8,128)} custom-call(f32[2,4,4,4,18,128]{5,4,3,2,1,0:T(8,128)} %reshape.76.x_ref), custom_call_target="tpu_custom_call" | custom-call | flops 589824 | bytes 4718592 | tf_op jit(solution)/shard_map/pallas_call | solution.py:182
  79.8 1.7 reshape.77
  81.6 1.3 select_reduce_fusion.1
  82.9 0.4 fusion.35
  83.3 0.5 fusion.34
  84.2 0.4 fusion.32
  85.0 0.4 fusion.29
  85.4 0.5 fusion.27
  85.9 0.5 fusion.13
  86.4 0.4 fusion.31
  86.8 0.3 fusion.28
  87.1 0.3 fusion.26
  87.8 1.1 fusion.118
  89.0 8.8 %fusion.4 = f32[12,32,256]{2,1,0:T(8,128)S(1)} fusion(f32[12,32,768]{2,1,0:T(8,128)S(1)} %fusion.118, f32[1,12,768,256]{3,2,1,0:T(8,128)} %param.6, bf16[1,12,768,256]{3,2,1,0:T(8,128)(2,1)S(1)} %bitcast.59), kind=kOutput, calls=%fused_computation.5 | convolution fusion | flops 910688256 | bytes 15728640 | tf_op jit(solution)/shard_map/kdf,krd->krf/dot_general | solution.py:377
  97.8 0.8 reshape.78.x_ref
  98.6 19.2 %shard_map.93 = f32[16,48,128]{2,1,0:T(8,128)} custom-call(f32[16,48,128]{2,1,0:T(8,128)} %reshape.78.x_ref), custom_call_target="tpu_custom_call" | custom-call | flops 196608 | bytes 1572864 | tf_op jit(solution)/shard_map/pallas_call | solution.py:182
  117.8 1.0 broadcast_multiply_fusion.1
  118.9 11.7 %fusion.2 = f32[12,32,768]{2,1,0:T(8,128)S(1)} fusion(f32[12,32,256]{2,1,0:T(8,128)S(1)} %div.15, f32[1,12,768,256]{3,2,1,0:T(8,128)} %param.6, bf16[1,12,768,256]{3,2,1,0:T(8,128)(2,1)} %param.5), kind=kOutput, calls=%fused_computation.3 | convolution fusion | flops 910688256 | bytes 15728640 | tf_op jit(solution)/shard_map/kdf,krf->krd/dot_general | solution.py:372
  130.6 1.4 reshape.79.x_ref
  132.0 40.3 %shard_map.94 = f32[2,4,4,4,18,128]{5,4,3,2,1,0:T(8,128)} custom-call(f32[2,4,4,4,18,128]{5,4,3,2,1,0:T(8,128)} %reshape.79.x_ref), custom_call_target="tpu_custom_call" | custom-call | flops 589824 | bytes 4718592 | tf_op jit(solution)/shard_map/pallas_call | solution.py:182
  172.3 1.9 reshape.80
  174.3 1.3 select_reduce_fusion
  175.6 0.4 fusion.25
  176.0 0.5 fusion.24
  176.9 0.4 fusion.22
  177.3 0.3 fusion.20
  177.6 0.4 fusion.19
  178.1 0.5 fusion.17
  178.6 0.5 fusion.12
  179.1 0.4 fusion.21
  179.5 0.3 fusion.18
  179.8 0.3 fusion.16
  180.1 0.3 convolution_multiply_fusion
  180.5 1.1 fusion.119
  181.6 8.5 %fusion = f32[12,32,256]{2,1,0:T(8,128)S(1)} fusion(f32[12,32,768]{2,1,0:T(8,128)S(1)} %fusion.119, f32[1,12,768,256]{3,2,1,0:T(8,128)} %param.6, bf16[1,12,768,256]{3,2,1,0:T(8,128)(2,1)S(1)} %bitcast.61), kind=kOutput, calls=%fused_computation.1 | convolution fusion | flops 910688256 | bytes 15728640 | tf_op jit(solution)/shard_map/kdf,krd->krf/dot_general | solution.py:377
  190.1 0.8 reshape.81.x_ref
  190.8 17.3 %shard_map.95 = f32[16,48,128]{2,1,0:T(8,128)} custom-call(f32[16,48,128]{2,1,0:T(8,128)} %reshape.81.x_ref), custom_call_target="tpu_custom_call" | custom-call | flops 196608 | bytes 1572864 | tf_op jit(solution)/shard_map/pallas_call | solution.py:182
  208.2 1.0 broadcast_multiply_fusion
  209.4 1.4 fusion.14
  210.8 0.9 constant_dynamic-slice_fusion
  211.7 15.3 %shard_map.96 = (f32[72,2048]{1,0:T(8,128)}, f32[72,2048]{1,0:T(8,128)}) custom-call(f32[8,72,256]{2,1,0:T(8,128)} %bitcast.64, f32[72,2048]{1,0:T(8,128)} %mom_ref.1, f32[72,2048]{1,0:T(8,128)} %master_ref.1), custom_call_target="tpu_custom_call" | custom-call | flops 589824 | bytes 2949120 | tf_op jit(solution)/shard_map/pallas_call | solution.py:295
  227.0 18.7 %subtract_convert_fusion = (bf16[12,768,256]{2,1,0:T(8,128)(2,1)}, f32[1,12,768,256]{3,2,1,0:T(8,128)}) fusion(f32[12,768,256]{2,1,0:T(8,128)} %bitcast.62, f32[1,12,768,256]{3,2,1,0:T(8,128)} %param.6, bf16[1,12,768,256]{3,2,1,0:T(8,128)(2,1)} %param.5, f32[12,32,768]{2,1,0:T(8,128)S(1)} %fusion.119, f32[12,32,256]{2,1,0:T(8,128)S(1)} %div.17), kind=kOutput, calls=%fused_computation.10 | convolution fusion | flops 920125440 | bytes 39321600 | tf_op jit(solution)/shard_map/krd,krf->kdf/dot_general | solution.py:381
  245.7 0.8 copy.12
  246.5 0.8 copy.13
  (33 shorter events, 1.7 us)
Async XLA Ops:
  7.2 16.7 %copy-start = (f32[12,32,256]{2,1,0:T(8,128)S(1)}, f32[12,32,256]{2,1,0:T(8,128)}, u32[]{:S(2)}) copy-start(f32[12,32,256]{2,1,0:T(8,128)} %param.7) | copy-start | bytes 1179652
  7.2 219.8 %all-gather.2.cloned.1.call-start = ((), (), s32[]{:S(2)}) async-start(), calls=%async_computation | async-start | bytes 10027008 | tf_op jit(solution)/shard_map/all_gather | solution.py:368
  79.8 9.1 %slice-start = ((s8[4718592]{0:T(1024)(128)(4,1)}), s8[524288]{0:T(1024)(128)(4,1)S(1)}, s32[]{:S(2)}) async-start(s8[4718592]{0:T(1024)(128)(4,1)} %bitcast.58), calls=%async_computation.1 | async-start | bytes 1048576
  84.2 4.8 %slice-start.1 = ((s8[4718592]{0:T(1024)(128)(4,1)}), s8[4194304]{0:T(1024)(128)(4,1)S(1)}, s32[]{:S(2)}) async-start(s8[4718592]{0:T(1024)(128)(4,1)} %bitcast.58), calls=%async_computation.2 | async-start | bytes 8388608
  172.3 9.2 %slice-start.2 = ((s8[4718592]{0:T(1024)(128)(4,1)}), s8[524288]{0:T(1024)(128)(4,1)S(1)}, s32[]{:S(2)}) async-start(s8[4718592]{0:T(1024)(128)(4,1)} %bitcast.60), calls=%async_computation.3 | async-start | bytes 1048576
  176.8 4.8 %slice-start.3 = ((s8[4718592]{0:T(1024)(128)(4,1)}), s8[4194304]{0:T(1024)(128)(4,1)S(1)}, s32[]{:S(2)}) async-start(s8[4718592]{0:T(1024)(128)(4,1)} %bitcast.60), calls=%async_computation.4 | async-start | bytes 8388608
  209.3 36.4 %copy-start.2 = (f32[12,32,256]{2,1,0:T(8,128)}, f32[12,32,256]{2,1,0:T(8,128)S(1)}, u32[]{:S(2)}) copy-start(f32[12,32,256]{2,1,0:T(8,128)S(1)} %div.17) | copy-start | bytes 1179652
  227.0 18.7 %copy-start.4 = (f32[72,2048]{1,0:T(8,128)S(1)}, f32[72,2048]{1,0:T(8,128)}, u32[]{:S(2)}) copy-start(f32[72,2048]{1,0:T(8,128)} %get-tuple-element.26) | copy-start | bytes 1769476
  227.0 19.5 %copy-start.3 = (f32[72,2048]{1,0:T(8,128)S(1)}, f32[72,2048]{1,0:T(8,128)}, u32[]{:S(2)}) copy-start(f32[72,2048]{1,0:T(8,128)} %get-tuple-element.27) | copy-start | bytes 1769476
  227.0 20.3 %copy-start.1 = (f32[12,32,256]{2,1,0:T(8,128)S(1)}, f32[12,32,256]{2,1,0:T(8,128)}, u32[]{:S(2)}) copy-start(f32[12,32,256]{2,1,0:T(8,128)} %param.7) | copy-start | bytes 1179652
Sparse Core Ops, SparseCore 0:
  23.9 78.3 all-gather.1
